TPU v7x, 32 devices: a whole 2x2x4 slice. The times are simulated.
32 devices in a mesh: grp: 2 (over y), tm: 4 (over z), row: 4 (over x, core).
Axes of the slice: x: 2, y: 2, z: 4, core: 2. Of those that a mesh axis runs over, the one named last changes fastest.
Arguments:
- frames: bfloat16 [16, 8, 24, 512], P(('grp', 'tm'), 'row'), parts along dimension 0, may hold values from -6 to 6
- w_in: bfloat16 [3, 3, 512, 512], P(None, None, None, ('tm', 'row')), may hold values from -0.046875 to 0.046875
- w_out: bfloat16 [3, 3, 512, 512], P(None, None, None, ('tm', 'row')), may hold values from -0.09375 to 0.09375
- decay_codes: int32 [512], replicated, may hold values from 0 to 15
- resets: int32 [16], P(('grp', 'tm')), parts along dimension 0, may hold values from 0 to 1, as said below
Outputs:
- mixed: bfloat16 [16, 8, 24, 512], P(('grp', 'tm'), 'row'), parts along dimension 0
There are 2 independent parts, one for each index of `grp`. A program takes and returns all parts, laid end to end along the dimension named above; an argument that names none is the same for every part. Nothing has to cross between parts.
Inputs may be any that keep to these rules, and one draw needn't show every extreme that they name: `decay_codes`: an entry of the table of 16 decays. `resets`: some frames start an episode and some do not.
All inputs are finite; a program needn't handle non-finite values.
Results may differ from a plain program's by a relative error of at most 0.005.
Values may be sent and summed in bfloat16 or wider, within the bound.
No kernel may reach another device: no remote copies, remote signals or barrier semaphores. Data moves between devices by JAX's collectives and lax.ppermute only.
A program may use at most 64 MiB of HBM per device.

v0:
```python
import functools
import math

import jax
import jax.numpy as jnp
from jax import lax
from jax.experimental import pallas as pl
from jax.experimental.pallas import tpu as pltpu
from jax.sharding import PartitionSpec as P


LEVELS = 16
WINDOW = 4096


LOW_LOG = math.log(0.995)
HIGH_LOG = math.log(0.9999)


def entering(part, axis, combine, identity):
    place = lax.axis_index(axis)
    gathered = jax.tree.map(lambda a: lax.all_gather(a, axis), part)
    state = jax.tree.map(lambda a, e: jnp.zeros_like(a) + jnp.asarray(e, a.dtype), part, identity)

    def one(turn, state):
        return combine(
            state, jax.tree.map(lambda a: lax.dynamic_index_in_dim(a, turn, 0, False), gathered)
        )

    return lax.fori_loop(0, place, one, state)


def extended_2(array, sides, width):
    for axis, dim in sides:
        size, length = (lax.axis_size(axis), array.shape[dim])
        up = [(i, (i + 1) % size) for i in range(size - 1)]
        down = [(j, i) for i, j in up]
        last = lax.slice_in_dim(array, length - width, length, axis=dim)
        initial = lax.slice_in_dim(array, 0, width, axis=dim)
        before = lax.ppermute(last, axis, up)
        after = lax.ppermute(initial, axis, down)
        array = jnp.concatenate([before, array, after], axis=dim)
    return array


def frame_rates(decay_codes, frame_count):
    levels = jnp.arange(LEVELS, dtype=jnp.int32)
    log_table = LOW_LOG + levels.astype(jnp.float32) / (LEVELS - 1) * (HIGH_LOG - LOW_LOG)
    picked = (decay_codes[:, None] == levels[None, :]).astype(jnp.float32)
    log_rate = jnp.sum(picked * log_table[None, :], axis=1)
    return jnp.exp(WINDOW / frame_count * log_rate)


def conv_rows(rows, weight):
    count, height, width = (rows.shape[0], rows.shape[1] - 2, rows.shape[2])
    padded = jnp.pad(rows, ((0, 0), (0, 0), (1, 1), (0, 0)))
    total = jnp.zeros((count, height, width, weight.shape[3]), jnp.float32)
    for i in range(3):
        for j in range(3):
            total = total + jnp.einsum(
                "frwc,ck->frwk",
                padded[:, i : i + height, j : j + width],
                weight[i, j],
                preferred_element_type=jnp.float32,
            )
    return total


def carry_combine(earlier, later):
    return (earlier[0] * later[0], later[0][None, None, :] * earlier[1] + later[1])


def recurrence(drive, gates):

    def advance(carry, inputs):
        state, product = carry
        frame_drive, gate = inputs
        state = gate[None, None, :] * state + frame_drive
        product = product * gate
        return ((state, product), (state, product))

    start = (jnp.zeros(drive.shape[1:], jnp.float32), jnp.ones((drive.shape[3],), jnp.float32))
    (last_state, last_product), (states, products) = lax.scan(advance, start, (drive, gates))
    identity = (jnp.ones_like(last_product), jnp.zeros_like(last_state))
    _, before_state = entering((last_product, last_state), "tm", carry_combine, identity)
    return states + products[:, None, None, :] * before_state[None]


def on_device(frames, w_in, w_out, decay_codes, resets):
    frame_count = frames.shape[0] * lax.axis_size("tm")
    rates = frame_rates(decay_codes, frame_count)
    gates = (1.0 - resets.astype(jnp.float32))[:, None] * rates[None, :]
    extended = extended_2(frames, (("row", 1),), 1)
    state = recurrence(
        conv_rows(extended, lax.all_gather(w_in, ("tm", "row"), axis=3, tiled=True)), gates
    )
    hidden = jax.nn.gelu(state).astype(jnp.bfloat16)
    hidden_rows = extended_2(hidden, (("row", 1),), 1)
    return conv_rows(hidden_rows, lax.all_gather(w_out, ("tm", "row"), axis=3, tiled=True)).astype(
        jnp.bfloat16
    )


BF16 = jnp.bfloat16
F32 = jnp.float32
VMEM = pl.BlockSpec(memory_space=pltpu.VMEM)
ANY = pl.BlockSpec(memory_space=pl.ANY)
MARKS = 8


def swapped(array, axis, distance):
    size = lax.axis_size(axis)
    return lax.ppermute(array, axis, [(i, i ^ distance) for i in range(size)])


def across(array):
    pairs = [(i, i + 1) for i in range(1, lax.axis_size("row") - 1, 2)]
    return lax.ppermute(array, "row", pairs + [(j, i) for i, j in pairs])


def dot_nt(a, b):
    return lax.dot_general(a, b, (((1,), (1,)), ((), ())), preferred_element_type=F32)


def shifted_columns(flat, offset, width):
    if offset == 0:
        return flat
    length = flat.shape[0]
    column = lax.rem(lax.broadcasted_iota(jnp.int32, flat.shape, 0), width)
    edge = 0 if offset < 0 else width - 1
    return jnp.where(column == edge, 0.0, pltpu.roll(flat, (-offset) % length, 0))


def payload_kernel(frames_hbm, resets_hbm, out, frames, resets, sem):
    copies = [
        pltpu.make_async_copy(frames_hbm, frames, sem.at[0]),
        pltpu.make_async_copy(resets_hbm, resets, sem.at[1]),
    ]
    for copy in copies:
        copy.start()
    for copy in copies:
        copy.wait()
    count, height, width, channels = frames.shape
    blocks = count * width
    for row in range(height):
        values = jnp.concatenate([frames[k, row].astype(F32) for k in range(count)])
        out[row * blocks : (row + 1) * blocks, :] = values.astype(BF16)
    place = lax.broadcasted_iota(jnp.int32, (MARKS, channels), 0)
    marks = jnp.zeros((MARKS, channels), F32)
    for k in range(count):
        marks = jnp.where(place == k, resets[k].astype(F32), marks)
    out[height * blocks :, :] = marks.astype(BF16)


def pieces_kernel(w, q0, q1, q2, q3):
    z = lax.axis_index("tm")
    lanes = q0.shape[3]
    for d, q in enumerate((q0, q1, q2, q3)):
        here = pl.ds(pl.multiple_of((z ^ d) * lanes, lanes), lanes)
        for i in range(3):
            for j in range(3):
                q[i, j] = w[i, j, :, here]


def drive_kernel(
    dims, f0, f1, f2, f3, e012, e3, near, w0, w1, w2, w3, codes, hid, x, w, gates, states
):
    count, height, width, frame_total = dims
    blocks = count * width
    z, r = lax.axis_index("tm"), lax.axis_index("row")
    odd = lax.rem(r, 2)
    rate = WINDOW / frame_total
    code = codes[pl.ds(z, 1), :].astype(F32)
    rates = jnp.exp(rate * (LOW_LOG + code / (LEVELS - 1) * (HIGH_LOG - LOW_LOG)))
    lanes = rates.shape[1]
    far = (e012.at[0], e012.at[1], e012.at[2], e3)
    for d, f in enumerate((f0, f1, f2, f3)):
        at = z ^ d
        here = pl.ds(pl.multiple_of(at * blocks, blocks), blocks)
        for row in range(height):
            part = slice(row * blocks, (row + 1) * blocks)
            x[height + row, here, :] = f[part, :]
            x[2 * height * odd + row, here, :] = far[d][part, :]
            x[2 * height * (1 - odd) + row, here, :] = near[d, part, :]
        marks = f[height * blocks :, :lanes].astype(F32)
        for k in range(count):
            gates[pl.ds(at * count + k, 1), :] = (1.0 - marks[k : k + 1, :]) * rates
    for d, block in enumerate((w0, w1, w2, w3)):
        for i in range(3):
            for j in range(3):
                w[i, j, pl.ds(r ^ d, 1)] = block[i, j][None]
    slab = x.shape[1]
    shown = height + 2
    total = None
    for i in range(3):
        rows = x[height - 2 + i : height - 2 + i + shown].reshape(shown * slab, x.shape[2])
        term = dot_nt(rows, w[i].reshape(3 * lanes, x.shape[2]))
        total = term if total is None else total + term
    drive = total[:, lanes : 2 * lanes]
    drive = drive + shifted_columns(total[:, :lanes], -1, width)
    drive = drive + shifted_columns(total[:, 2 * lanes :], 1, width)
    for row in range(shown):
        state = jnp.zeros((width, lanes), F32)
        for t in range(frame_total):
            first = row * slab + t * width
            state = gates[t : t + 1, :] * state + drive[first : first + width]
            states[first : first + width, :] = state
    last = lax.axis_size("row") - 1
    for row in range(shown):
        values = jax.nn.gelu(states[row * slab : (row + 1) * slab, :])
        if row == 0:
            values = jnp.where(r == 0, 0.0, values)
        if row == shown - 1:
            values = jnp.where(r == last, 0.0, values)
        hid[row] = values.astype(BF16)


def mix_kernel(dims, hid, q0, g1, g2, g3, x0, x123, c0, cx0, cx123, p0, p1, p2, p3, a, w, part):
    count, height, width = dims
    z, r = lax.axis_index("tm"), lax.axis_index("row")
    outs, lanes = q0.shape[2], q0.shape[3]
    held = (
        (q0, g1, g2, g3),
        tuple(c0.at[e] for e in range(4)),
        (x0,) + tuple(x123.at[e] for e in range(3)),
        (cx0,) + tuple(cx123.at[e] for e in range(3)),
    )
    for d in range(4):
        for e in range(4):
            slot = (z ^ e) * 4 + (r ^ d)
            here = pl.ds(pl.multiple_of(slot * outs, outs), outs)
            for i in range(3):
                for j in range(3):
                    tap = 3 * i + j
                    w[here, tap * lanes : (tap + 1) * lanes] = held[d][e][i, j]
    for row in range(height + 2):
        values = hid[row].astype(F32)
        for j in range(3):
            moved = shifted_columns(values, j - 1, width).astype(BF16)
            for i in range(3):
                out_row = row - i
                if 0 <= out_row < height:
                    tap = 3 * i + j
                    a[out_row, :, tap * lanes : (tap + 1) * lanes] = moved
    for row in range(height):
        part[row] = dot_nt(a[row], w[...])
    blocks = count * width
    for d, out in enumerate((p0, p1, p2, p3)):
        here = pl.ds(pl.multiple_of((z ^ d) * blocks, blocks), blocks)
        for row in range(height):
            out[row] = part[row, here, :].astype(out.dtype)


def sum_kernel(width, p0, p1, p2, p3, out):
    total = p0[...] + p1[...].astype(F32) + p2[...].astype(F32) + p3[...].astype(F32)
    for row in range(total.shape[0]):
        for k in range(total.shape[1] // width):
            out[k, row] = total[row, k * width : (k + 1) * width].astype(BF16)


def call(kernel, outs, scratch, *args, flops=0, specs=None):
    moved = sum(a.size * a.dtype.itemsize for a in args)
    return pl.pallas_call(
        kernel,
        out_shape=outs,
        in_specs=specs or [VMEM] * len(args),
        out_specs=jax.tree.map(lambda _: VMEM, outs),
        scratch_shapes=scratch,
        cost_estimate=pl.CostEstimate(flops=flops, bytes_accessed=moved, transcendentals=0),
        compiler_params=pltpu.CompilerParams(vmem_limit_bytes=24 * 2**20),
    )(*args)


def on_device_4x4(frames, w_in, w_out, decay_codes, resets):
    return staged(frames, w_in, w_out, decay_codes, resets)


def staged(frames, w_in, w_out, decay_codes, resets):
    count, height, width, channels = frames.shape
    blocks = count * width
    total = 4 * count
    lanes = channels // 4
    outs = w_out.shape[3]
    shape = jax.ShapeDtypeStruct
    w0 = w_in.transpose(0, 1, 3, 2)
    w2 = swapped(w0, "row", 2)
    w1 = swapped(w0, "row", 1)
    f0 = call(
        payload_kernel,
        shape((height * blocks + MARKS, channels), BF16),
        [
            pltpu.VMEM(frames.shape, BF16),
            pltpu.SMEM(resets.shape, resets.dtype),
            pltpu.SemaphoreType.DMA((2,)),
        ],
        frames,
        resets,
        specs=[ANY, ANY],
    )
    f2 = swapped(f0, "tm", 2)
    f1 = swapped(f0, "tm", 1)
    piece = shape((3, 3, outs, lanes), BF16)
    q0, q1, q2, q3 = call(pieces_kernel, (piece,) * 4, [], w_out.transpose(0, 1, 3, 2))
    x0 = swapped(q0, "row", 2)
    g2 = swapped(q2, "tm", 2)
    g3 = swapped(q3, "tm", 3)
    f3 = swapped(f2, "tm", 1)
    e012 = across(jnp.stack([f0, f1, f2]))
    g1 = swapped(q1, "tm", 1)
    w3 = swapped(w2, "row", 1)
    e3 = across(f3)
    near = swapped(jnp.stack([f0, f1, f2, f3]), "row", 1)
    x123 = swapped(jnp.stack([g1, g2, g3]), "row", 2)
    c0 = swapped(jnp.stack([q0, g1, g2, g3]), "row", 1)
    cx0 = swapped(x0, "row", 1)
    slab = total * width
    hidden = call(
        functools.partial(drive_kernel, (count, height, width, total)),
        shape((height + 2, slab, lanes), BF16),
        [
            pltpu.VMEM((3 * height, slab, channels), BF16),
            pltpu.VMEM((3, 3, 4, w_in.shape[3], channels), BF16),
            pltpu.VMEM((max(8, total), lanes), F32),
            pltpu.VMEM(((height + 2) * slab, lanes), F32),
        ],
        f0,
        f1,
        f2,
        f3,
        e012,
        e3,
        near,
        w0,
        w1,
        w2,
        w3,
        decay_codes.reshape(4, lanes),
        flops=2 * (height + 2) * slab * 9 * channels * lanes,
    )
    cx123 = swapped(x123, "row", 1)
    part = functools.partial(shape, (height, blocks, channels))
    parts = call(
        functools.partial(mix_kernel, (count, height, width)),
        (part(F32), part(BF16), part(BF16), part(BF16)),
        [
            pltpu.VMEM((height, slab, 9 * lanes), BF16),
            pltpu.VMEM((channels, 9 * lanes), BF16),
            pltpu.VMEM((height, slab, channels), F32),
        ],
        hidden,
        q0,
        g1,
        g2,
        g3,
        x0,
        x123,
        c0,
        cx0,
        cx123,
        flops=2 * height * slab * 9 * channels * lanes,
    )
    received = {d: swapped(parts[d], "tm", d) for d in (3, 2, 1)}
    return call(
        functools.partial(sum_kernel, width),
        shape(frames.shape, BF16),
        [],
        parts[0],
        received[1],
        received[2],
        received[3],
    )


def solution(mesh):
    small = mesh.shape["tm"] == 4 and mesh.shape["row"] == 4
    return jax.shard_map(
        on_device_4x4 if small else on_device,
        mesh=mesh,
        in_specs=(
            P(("grp", "tm"), "row", None, None),
            P(None, None, None, ("tm", "row")),
            P(None, None, None, ("tm", "row")),
            P(),
            P(("grp", "tm")),
        ),
        out_specs=P(("grp", "tm"), "row", None, None),
        check_vma=False,
    )
```

profile of v0, /device:TPU:0, one launch (start us, length us, event | category | flops | bytes accessed | tf_op | source)
XLA Modules:
  0.0 49.6 jit_solution(6803888742862414411)
XLA Ops:
  0.0 0.9 %copy-done.1 = bf16[2,2,24,512]{3,2,1,0:T(8,128)(2,1)S(1)} copy-done((bf16[2,2,24,512]{3,2,1,0:T(8,128)(2,1)S(1)}, bf16[2,2,24,512]{3,2,1,0:T(8,128)(2,1)}, u32[]{:S(2)}) %copy-start.1) | copy-done | bytes 98328
  0.9 0.7 %copy-done.2 = s32[2]{0:T(128)S(1)} copy-done((s32[2]{0:T(128)S(1)}, s32[2]{0:T(128)}, u32[]{:S(2)}) %copy-start.2) | copy-done | bytes 32
  1.5 0.7 %shard_map.55.f0 = bf16[104,512]{1,0:T(8,128)(2,1)S(1)} custom-call(bf16[2,2,24,512]{3,2,1,0:T(8,128)(2,1)S(1)} %copy-done.1, s32[2]{0:T(128)S(1)} %copy-done.2), custom_call_target="tpu_custom_call" | custom-call | bytes 98312 | tf_op jit(solution)/shard_map/pallas_call | solution.py:263
  2.2 4.1 %collective-permute-start.1 = (bf16[104,512]{1,0:T(8,128)(2,1)S(1)}, bf16[104,512]{1,0:T(8,128)(2,1)S(1)}, u32[]{:S(2)}, u32[]{:S(2)}) collective-permute-start(bf16[104,512]{1,0:T(8,128)(2,1)S(1)} %shard_map.55.f0), channel_id=1, source_target_pairs={{0,8},{4,12},{8,0},{12,4},{1,9},{5,13},{9,1},{13,5},{2,10},{6,14},... | collective-permute-start | bytes 319496 | tf_op jit(solution)/shard_map/ppermute | solution.py:113
  6.3 1.0 %copy-done = bf16[3,3,512,32]{2,3,1,0:T(8,128)(2,1)S(1)} copy-done((bf16[3,3,512,32]{2,3,1,0:T(8,128)(2,1)S(1)}, bf16[3,3,512,32]{2,3,1,0:T(8,128)(2,1)}, u32[]{:S(2)}) %copy-start) | copy-done | bytes 294936
  7.4 1.6 %collective-permute-start.9 = (bf16[3,3,32,128]{3,2,1,0:T(8,128)(2,1)S(1)}, bf16[3,3,32,128]{3,2,1,0:T(8,128)(2,1)S(1)}, u32[]{:S(2)}, u32[]{:S(2)}) collective-permute-start(bf16[3,3,32,128]{3,2,1,0:T(8,128)(2,1)S(1)} %get-tuple-element.14), channel_id=1, source_target_pairs={{0,4},{4,0},{8,12},{12,8},{1,5},{5,1},{9,13},{13,9},{2,6},{6,2},{1... | collective-permute-start | bytes 221192 | tf_op jit(solution)/shard_map/ppermute | solution.py:113
  9.0 0.3 collective-permute-start.10
  9.3 2.5 %collective-permute-start.11 = (bf16[3,3,32,128]{3,2,1,0:T(8,128)(2,1)S(1)}, bf16[3,3,32,128]{3,2,1,0:T(8,128)(2,1)S(1)}, u32[]{:S(2)}, u32[]{:S(2)}) collective-permute-start(bf16[3,3,32,128]{3,2,1,0:T(8,128)(2,1)S(1)} %get-tuple-element.16), channel_id=1, source_target_pairs={{0,12},{4,8},{8,4},{12,0},{1,13},{5,9},{9,5},{13,1},{2,14},{6,10},... | collective-permute-start | bytes 221192 | tf_op jit(solution)/shard_map/ppermute | solution.py:113
  11.8 0.7 %collective-permute-start = (bf16[104,512]{1,0:T(8,128)(2,1)S(1)}, bf16[104,512]{1,0:T(8,128)(2,1)S(1)}, u32[]{:S(2)}, u32[]{:S(2)}) collective-permute-start(bf16[104,512]{1,0:T(8,128)(2,1)S(1)} %shard_map.55.f0), channel_id=1, source_target_pairs={{0,4},{4,0},{8,12},{12,8},{1,5},{5,1},{9,13},{13,9},{2,6},{6,2},{1... | collective-permute-start | bytes 319496 | tf_op jit(solution)/shard_map/ppermute | solution.py:113
  12.5 0.1 collective-permute-done.9.g1
  12.6 1.5 %collective-permute-start.7 = (bf16[3,3,32,512]{3,2,1,0:T(8,128)(2,1)S(1)}, bf16[3,3,32,512]{3,2,1,0:T(8,128)(2,1)S(1)}, u32[]{:S(2)}, u32[]{:S(2)}) collective-permute-start(bf16[3,3,32,512]{3,2,1,0:T(8,128)(2,1)S(1)} %bitcast.26), channel_id=1, source_target_pairs={{0,2},{1,3},{2,0},{3,1},{4,6},{5,7},{6,4},{7,5},{8,10},{9,11},{10,... | collective-permute-start | bytes 884744 | tf_op jit(solution)/shard_map/ppermute | solution.py:113
  14.1 2.7 %collective-permute-done.10.g2 = bf16[3,3,32,128]{3,2,1,0:T(8,128)(2,1)S(1)} collective-permute-done((bf16[3,3,32,128]{3,2,1,0:T(8,128)(2,1)S(1)}, bf16[3,3,32,128]{3,2,1,0:T(8,128)(2,1)S(1)}, u32[]{:S(2)}, u32[]{:S(2)}) %collective-permute-start.10) | collective-permute-done | bytes 73760 | tf_op jit(solution)/shard_map/ppermute | solution.py:113
  16.8 1.5 %collective-permute-start.12 = (bf16[3,3,32,128]{3,2,1,0:T(8,128)(2,1)S(1)}, bf16[3,3,32,128]{3,2,1,0:T(8,128)(2,1)S(1)}, u32[]{:S(2)}, u32[]{:S(2)}) collective-permute-start(bf16[3,3,32,128]{3,2,1,0:T(8,128)(2,1)S(1)} %get-tuple-element.13.q0), channel_id=1, source_target_pairs={{0,2},{1,3},{2,0},{3,1},{4,6},{5,7},{6,4},{7,5},{8,10},{9,11},{10,... | collective-permute-start | bytes 221192 | tf_op jit(solution)/shard_map/ppermute | solution.py:113
  18.3 1.8 %collective-permute-start.2 = (bf16[104,512]{1,0:T(8,128)(2,1)S(1)}, bf16[104,512]{1,0:T(8,128)(2,1)S(1)}, u32[]{:S(2)}, u32[]{:S(2)}) collective-permute-start(bf16[104,512]{1,0:T(8,128)(2,1)S(1)} %collective-permute-done.1.f2), channel_id=1, source_target_pairs={{0,4},{4,0},{8,12},{12,8},{1,5},{5,1},{9,13},{13,9},{2,6},{6,2},{1... | collective-permute-start | bytes 319496 | tf_op jit(solution)/shard_map/ppermute | solution.py:113
  20.2 0.6 %collective-permute-start.13 = (bf16[3,3,3,32,128]{4,3,2,1,0:T(8,128)(2,1)S(1)}, bf16[3,3,3,32,128]{4,3,2,1,0:T(8,128)(2,1)S(1)}, u32[]{:S(2)}, u32[]{:S(2)}) collective-permute-start(bf16[3,3,3,32,128]{4,3,2,1,0:T(8,128)(2,1)S(1)} %pad_maximum_fusion.3), channel_id=1, source_target_pairs={{0,2},{1,3},{2,0},{3,1},{4,6},{5,7},{6,4},{7,5},{8,10},{9,11},{10,... | collective-permute-start | bytes 663560 | tf_op jit(solution)/shard_map/ppermute | solution.py:113
  20.8 2.7 %collective-permute-done.2.f3 = bf16[104,512]{1,0:T(8,128)(2,1)S(1)} collective-permute-done((bf16[104,512]{1,0:T(8,128)(2,1)S(1)}, bf16[104,512]{1,0:T(8,128)(2,1)S(1)}, u32[]{:S(2)}, u32[]{:S(2)}) %collective-permute-start.2) | collective-permute-done | bytes 106528 | tf_op jit(solution)/shard_map/ppermute | solution.py:113
  23.4 0.1 pad_maximum_fusion
  23.5 0.1 collective-permute-start.5
  23.6 0.7 %collective-permute-start.3 = (bf16[3,104,512]{2,1,0:T(8,128)(2,1)S(1)}, bf16[3,104,512]{2,1,0:T(8,128)(2,1)S(1)}, u32[]{:S(2)}, u32[]{:S(2)}) collective-permute-start(bf16[3,104,512]{2,1,0:T(8,128)(2,1)S(1)} %pad_maximum_fusion.1), channel_id=1, source_target_pairs={{1,2},{2,1},{5,6},{6,5},{9,10},{10,9},{13,14},{14,13},{17,18},{18,... | collective-permute-start | bytes 958472 | tf_op jit(solution)/shard_map/ppermute | solution.py:118
  24.3 0.7 %collective-permute-start.4 = (bf16[104,512]{1,0:T(8,128)(2,1)S(1)}, bf16[104,512]{1,0:T(8,128)(2,1)S(1)}, u32[]{:S(2)}, u32[]{:S(2)}) collective-permute-start(bf16[104,512]{1,0:T(8,128)(2,1)S(1)} %collective-permute-done.2.f3), channel_id=1, source_target_pairs={{1,2},{2,1},{5,6},{6,5},{9,10},{10,9},{13,14},{14,13},{17,18},{18,... | collective-permute-start | bytes 319496 | tf_op jit(solution)/shard_map/ppermute | solution.py:118
  25.0 4.8 %collective-permute-start.8 = (bf16[3,3,32,512]{3,2,1,0:T(8,128)(2,1)S(1)}, bf16[3,3,32,512]{3,2,1,0:T(8,128)(2,1)S(1)}, u32[]{:S(2)}, u32[]{:S(2)}) collective-permute-start(bf16[3,3,32,512]{3,2,1,0:T(8,128)(2,1)S(1)} %collective-permute-done.7.w2), channel_id=1, source_target_pairs={{0,1},{1,0},{2,3},{3,2},{4,5},{5,4},{6,7},{7,6},{8,9},{9,8},{10,11... | collective-permute-start | bytes 884744 | tf_op jit(solution)/shard_map/ppermute | solution.py:113
  29.8 0.1 collective-permute-start.14
  29.9 3.6 %collective-permute-start.16 = (bf16[3,3,3,32,128]{4,3,2,1,0:T(8,128)(2,1)S(1)}, bf16[3,3,3,32,128]{4,3,2,1,0:T(8,128)(2,1)S(1)}, u32[]{:S(2)}, u32[]{:S(2)}) collective-permute-start(bf16[3,3,3,32,128]{4,3,2,1,0:T(8,128)(2,1)S(1)} %collective-permute-done.13.x123), channel_id=1, source_target_pairs={{0,1},{1,0},{2,3},{3,2},{4,5},{5,4},{6,7},{7,6},{8,9},{9,8},{10,11... | collective-permute-start | bytes 663560 | tf_op jit(solution)/shard_map/ppermute | solution.py:113
  33.6 1.7 %shard_map.56.hid = bf16[4,192,128]{2,1,0:T(8,128)(2,1)S(1)} custom-call(bf16[104,512]{1,0:T(8,128)(2,1)S(1)} %shard_map.55.f0, bf16[104,512]{1,0:T(8,128)(2,1)S(1)} %collective-permute-done.f1, bf16[104,512]{1,0:T(8,128)(2,1)S(1)} %collective-permute-done.1.f2, bf16[104,512]{1,0:T(8,128)(2,1)S(1)} %collective-permute-done.2.f3, ...), custom_call_target="tpu_custom_call" | custom-call | flops 905969664 | bytes 2459648 | tf_op jit(solution)/shard_map/pallas_call | solution.py:263
  35.3 1.2 %shard_map.58 = (f32[2,48,512]{2,1,0:T(8,128)S(1)}, bf16[2,48,512]{2,1,0:T(8,128)(2,1)S(1)}, bf16[2,48,512]{2,1,0:T(8,128)(2,1)S(1)}, bf16[2,48,512]{2,1,0:T(8,128)(2,1)S(1)}) custom-call(bf16[4,192,128]{2,1,0:T(8,128)(2,1)S(1)} %shard_map.56.hid, bf16[3,3,32,128]{3,2,1,0:T(8,128)(2,1)S(1)} %get-tuple-element.13.q0, ...), custom_call_target="tpu_custom_call" | custom-call | flops 452984832 | bytes 1376256 | tf_op jit(solution)/shard_map/pallas_call | solution.py:263
  36.5 1.5 %collective-permute-start.17 = (bf16[2,48,512]{2,1,0:T(8,128)(2,1)S(1)}, bf16[2,48,512]{2,1,0:T(8,128)(2,1)S(1)}, u32[]{:S(2)}, u32[]{:S(2)}) collective-permute-start(bf16[2,48,512]{2,1,0:T(8,128)(2,1)S(1)} %get-tuple-element.18), channel_id=1, source_target_pairs={{0,4},{4,0},{8,12},{12,8},{1,5},{5,1},{9,13},{13,9},{2,6},{6,2},{1... | collective-permute-start | bytes 294920 | tf_op jit(solution)/shard_map/ppermute | solution.py:113
  38.0 2.3 %collective-permute-start.18 = (bf16[2,48,512]{2,1,0:T(8,128)(2,1)S(1)}, bf16[2,48,512]{2,1,0:T(8,128)(2,1)S(1)}, u32[]{:S(2)}, u32[]{:S(2)}) collective-permute-start(bf16[2,48,512]{2,1,0:T(8,128)(2,1)S(1)} %get-tuple-element.19), channel_id=1, source_target_pairs={{0,8},{4,12},{8,0},{12,4},{1,9},{5,13},{9,1},{13,5},{2,10},{6,14},... | collective-permute-start | bytes 294920 | tf_op jit(solution)/shard_map/ppermute | solution.py:113
  40.3 1.1 %collective-permute-start.19 = (bf16[2,48,512]{2,1,0:T(8,128)(2,1)S(1)}, bf16[2,48,512]{2,1,0:T(8,128)(2,1)S(1)}, u32[]{:S(2)}, u32[]{:S(2)}) collective-permute-start(bf16[2,48,512]{2,1,0:T(8,128)(2,1)S(1)} %get-tuple-element.20), channel_id=1, source_target_pairs={{0,12},{4,8},{8,4},{12,0},{1,13},{5,9},{9,5},{13,1},{2,14},{6,10},... | collective-permute-start | bytes 294920 | tf_op jit(solution)/shard_map/ppermute | solution.py:113
  41.4 0.4 collective-permute-done.17.p1
  41.8 2.1 %collective-permute-done.18.p2 = bf16[2,48,512]{2,1,0:T(8,128)(2,1)S(1)} collective-permute-done((bf16[2,48,512]{2,1,0:T(8,128)(2,1)S(1)}, bf16[2,48,512]{2,1,0:T(8,128)(2,1)S(1)}, u32[]{:S(2)}, u32[]{:S(2)}) %collective-permute-start.18) | collective-permute-done | bytes 98336 | tf_op jit(solution)/shard_map/ppermute | solution.py:113
  43.9 5.0 %collective-permute-done.19.p3 = bf16[2,48,512]{2,1,0:T(8,128)(2,1)S(1)} collective-permute-done((bf16[2,48,512]{2,1,0:T(8,128)(2,1)S(1)}, bf16[2,48,512]{2,1,0:T(8,128)(2,1)S(1)}, u32[]{:S(2)}, u32[]{:S(2)}) %collective-permute-start.19) | collective-permute-done | bytes 98336 | tf_op jit(solution)/shard_map/ppermute | solution.py:113
  48.9 0.7 %shard_map.59 = bf16[2,2,24,512]{3,2,1,0:T(8,128)(2,1)} custom-call(f32[2,48,512]{2,1,0:T(8,128)S(1)} %get-tuple-element.17.p0, bf16[2,48,512]{2,1,0:T(8,128)(2,1)S(1)} %collective-permute-done.17.p1, bf16[2,48,512]{2,1,0:T(8,128)(2,1)S(1)} %collective-permute-done.18.p2, bf16[2,48,512]{2,1,0:T(8,128)(2,1)S(1)} %collective-permute-done.19.p3), custom_call_target="tpu_custom_call" | custom-call | bytes 491520 | tf_op jit(solution)/shard_map/pallas_call | solution.py:263
  (27 shorter events, 0.2 us)
Async XLA Ops:
  0.0 0.9 %copy-start.1 = (bf16[2,2,24,512]{3,2,1,0:T(8,128)(2,1)S(1)}, bf16[2,2,24,512]{3,2,1,0:T(8,128)(2,1)}, u32[]{:S(2)}) copy-start(bf16[2,2,24,512]{3,2,1,0:T(8,128)(2,1)} %frames_hbm.1) | copy-start | bytes 294916
  0.9 0.7 %copy-start.2 = (s32[2]{0:T(128)S(1)}, s32[2]{0:T(128)}, u32[]{:S(2)}) copy-start(s32[2]{0:T(128)} %resets_hbm.1) | copy-start | bytes 28
  2.2 16.1 %collective-permute-start.1 = (bf16[104,512]{1,0:T(8,128)(2,1)S(1)}, bf16[104,512]{1,0:T(8,128)(2,1)S(1)}, u32[]{:S(2)}, u32[]{:S(2)}) collective-permute-start(bf16[104,512]{1,0:T(8,128)(2,1)S(1)} %shard_map.55.f0), channel_id=1, source_target_pairs={{0,8},{4,12},{8,0},{12,4},{1,9},{5,13},{9,1},{13,5},{2,10},{6,14},... | collective-permute-start | bytes 319496 | tf_op jit(solution)/shard_map/ppermute | solution.py:113
  6.3 1.0 %copy-start = (bf16[3,3,512,32]{2,3,1,0:T(8,128)(2,1)S(1)}, bf16[3,3,512,32]{2,3,1,0:T(8,128)(2,1)}, u32[]{:S(2)}) copy-start(bf16[3,3,512,32]{2,3,1,0:T(8,128)(2,1)} %param.7) | copy-start | bytes 884740
  7.3 5.3 %copy-start.3 = (bf16[3,3,512,32]{2,3,1,0:T(8,128)(2,1)S(1)}, bf16[3,3,512,32]{2,3,1,0:T(8,128)(2,1)}, u32[]{:S(2)}) copy-start(bf16[3,3,512,32]{2,3,1,0:T(8,128)(2,1)} %param.6) | copy-start | bytes 884740
  7.4 5.2 %collective-permute-start.9 = (bf16[3,3,32,128]{3,2,1,0:T(8,128)(2,1)S(1)}, bf16[3,3,32,128]{3,2,1,0:T(8,128)(2,1)S(1)}, u32[]{:S(2)}, u32[]{:S(2)}) collective-permute-start(bf16[3,3,32,128]{3,2,1,0:T(8,128)(2,1)S(1)} %get-tuple-element.14), channel_id=1, source_target_pairs={{0,4},{4,0},{8,12},{12,8},{1,5},{5,1},{9,13},{13,9},{2,6},{6,2},{1... | collective-permute-start | bytes 221192 | tf_op jit(solution)/shard_map/ppermute | solution.py:113
  9.0 7.8 %collective-permute-start.10 = (bf16[3,3,32,128]{3,2,1,0:T(8,128)(2,1)S(1)}, bf16[3,3,32,128]{3,2,1,0:T(8,128)(2,1)S(1)}, u32[]{:S(2)}, u32[]{:S(2)}) collective-permute-start(bf16[3,3,32,128]{3,2,1,0:T(8,128)(2,1)S(1)} %get-tuple-element.15), channel_id=1, source_target_pairs={{0,8},{4,12},{8,0},{12,4},{1,9},{5,13},{9,1},{13,5},{2,10},{6,14},... | collective-permute-start | bytes 221192 | tf_op jit(solution)/shard_map/ppermute | solution.py:113
  9.3 7.5 %collective-permute-start.11 = (bf16[3,3,32,128]{3,2,1,0:T(8,128)(2,1)S(1)}, bf16[3,3,32,128]{3,2,1,0:T(8,128)(2,1)S(1)}, u32[]{:S(2)}, u32[]{:S(2)}) collective-permute-start(bf16[3,3,32,128]{3,2,1,0:T(8,128)(2,1)S(1)} %get-tuple-element.16), channel_id=1, source_target_pairs={{0,12},{4,8},{8,4},{12,0},{1,13},{5,9},{9,5},{13,1},{2,14},{6,10},... | collective-permute-start | bytes 221192 | tf_op jit(solution)/shard_map/ppermute | solution.py:113
  11.8 8.3 %collective-permute-start = (bf16[104,512]{1,0:T(8,128)(2,1)S(1)}, bf16[104,512]{1,0:T(8,128)(2,1)S(1)}, u32[]{:S(2)}, u32[]{:S(2)}) collective-permute-start(bf16[104,512]{1,0:T(8,128)(2,1)S(1)} %shard_map.55.f0), channel_id=1, source_target_pairs={{0,4},{4,0},{8,12},{12,8},{1,5},{5,1},{9,13},{13,9},{2,6},{6,2},{1... | collective-permute-start | bytes 319496 | tf_op jit(solution)/shard_map/ppermute | solution.py:113
  12.6 11.7 %collective-permute-start.7 = (bf16[3,3,32,512]{3,2,1,0:T(8,128)(2,1)S(1)}, bf16[3,3,32,512]{3,2,1,0:T(8,128)(2,1)S(1)}, u32[]{:S(2)}, u32[]{:S(2)}) collective-permute-start(bf16[3,3,32,512]{3,2,1,0:T(8,128)(2,1)S(1)} %bitcast.26), channel_id=1, source_target_pairs={{0,2},{1,3},{2,0},{3,1},{4,6},{5,7},{6,4},{7,5},{8,10},{9,11},{10,... | collective-permute-start | bytes 884744 | tf_op jit(solution)/shard_map/ppermute | solution.py:113
  16.8 8.2 %collective-permute-start.6 = (bf16[3,3,32,512]{3,2,1,0:T(8,128)(2,1)S(1)}, bf16[3,3,32,512]{3,2,1,0:T(8,128)(2,1)S(1)}, u32[]{:S(2)}, u32[]{:S(2)}) collective-permute-start(bf16[3,3,32,512]{3,2,1,0:T(8,128)(2,1)S(1)} %bitcast.27), channel_id=1, source_target_pairs={{0,1},{1,0},{2,3},{3,2},{4,5},{5,4},{6,7},{7,6},{8,9},{9,8},{10,11... | collective-permute-start | bytes 884744 | tf_op jit(solution)/shard_map/ppermute | solution.py:113
  16.8 6.8 %collective-permute-start.12 = (bf16[3,3,32,128]{3,2,1,0:T(8,128)(2,1)S(1)}, bf16[3,3,32,128]{3,2,1,0:T(8,128)(2,1)S(1)}, u32[]{:S(2)}, u32[]{:S(2)}) collective-permute-start(bf16[3,3,32,128]{3,2,1,0:T(8,128)(2,1)S(1)} %get-tuple-element.13.q0), channel_id=1, source_target_pairs={{0,2},{1,3},{2,0},{3,1},{4,6},{5,7},{6,4},{7,5},{8,10},{9,11},{10,... | collective-permute-start | bytes 221192 | tf_op jit(solution)/shard_map/ppermute | solution.py:113
  18.3 5.1 %collective-permute-start.2 = (bf16[104,512]{1,0:T(8,128)(2,1)S(1)}, bf16[104,512]{1,0:T(8,128)(2,1)S(1)}, u32[]{:S(2)}, u32[]{:S(2)}) collective-permute-start(bf16[104,512]{1,0:T(8,128)(2,1)S(1)} %collective-permute-done.1.f2), channel_id=1, source_target_pairs={{0,4},{4,0},{8,12},{12,8},{1,5},{5,1},{9,13},{13,9},{2,6},{6,2},{1... | collective-permute-start | bytes 319496 | tf_op jit(solution)/shard_map/ppermute | solution.py:113
  20.2 9.7 %collective-permute-start.13 = (bf16[3,3,3,32,128]{4,3,2,1,0:T(8,128)(2,1)S(1)}, bf16[3,3,3,32,128]{4,3,2,1,0:T(8,128)(2,1)S(1)}, u32[]{:S(2)}, u32[]{:S(2)}) collective-permute-start(bf16[3,3,3,32,128]{4,3,2,1,0:T(8,128)(2,1)S(1)} %pad_maximum_fusion.3), channel_id=1, source_target_pairs={{0,2},{1,3},{2,0},{3,1},{4,6},{5,7},{6,4},{7,5},{8,10},{9,11},{10,... | collective-permute-start | bytes 663560 | tf_op jit(solution)/shard_map/ppermute | solution.py:113
  23.5 10.1 %collective-permute-start.5 = (bf16[4,104,512]{2,1,0:T(8,128)(2,1)S(1)}, bf16[4,104,512]{2,1,0:T(8,128)(2,1)S(1)}, u32[]{:S(2)}, u32[]{:S(2)}) collective-permute-start(bf16[4,104,512]{2,1,0:T(8,128)(2,1)S(1)} %pad_maximum_fusion), channel_id=1, source_target_pairs={{0,1},{1,0},{2,3},{3,2},{4,5},{5,4},{6,7},{7,6},{8,9},{9,8},{10,11... | collective-permute-start | bytes 1277960 | tf_op jit(solution)/shard_map/ppermute | solution.py:113
  23.6 9.9 %collective-permute-start.3 = (bf16[3,104,512]{2,1,0:T(8,128)(2,1)S(1)}, bf16[3,104,512]{2,1,0:T(8,128)(2,1)S(1)}, u32[]{:S(2)}, u32[]{:S(2)}) collective-permute-start(bf16[3,104,512]{2,1,0:T(8,128)(2,1)S(1)} %pad_maximum_fusion.1), channel_id=1, source_target_pairs={{1,2},{2,1},{5,6},{6,5},{9,10},{10,9},{13,14},{14,13},{17,18},{18,... | collective-permute-start | bytes 958472 | tf_op jit(solution)/shard_map/ppermute | solution.py:118
  24.3 5.6 %collective-permute-start.4 = (bf16[104,512]{1,0:T(8,128)(2,1)S(1)}, bf16[104,512]{1,0:T(8,128)(2,1)S(1)}, u32[]{:S(2)}, u32[]{:S(2)}) collective-permute-start(bf16[104,512]{1,0:T(8,128)(2,1)S(1)} %collective-permute-done.2.f3), channel_id=1, source_target_pairs={{1,2},{2,1},{5,6},{6,5},{9,10},{10,9},{13,14},{14,13},{17,18},{18,... | collective-permute-start | bytes 319496 | tf_op jit(solution)/shard_map/ppermute | solution.py:118
  25.0 8.6 %collective-permute-start.8 = (bf16[3,3,32,512]{3,2,1,0:T(8,128)(2,1)S(1)}, bf16[3,3,32,512]{3,2,1,0:T(8,128)(2,1)S(1)}, u32[]{:S(2)}, u32[]{:S(2)}) collective-permute-start(bf16[3,3,32,512]{3,2,1,0:T(8,128)(2,1)S(1)} %collective-permute-done.7.w2), channel_id=1, source_target_pairs={{0,1},{1,0},{2,3},{3,2},{4,5},{5,4},{6,7},{7,6},{8,9},{9,8},{10,11... | collective-permute-start | bytes 884744 | tf_op jit(solution)/shard_map/ppermute | solution.py:113
  29.8 3.8 %copy-start.4 = (s32[512]{0:T(512)S(1)}, s32[512]{0:T(512)}, u32[]{:S(2)}) copy-start(s32[512]{0:T(512)} %param.8) | copy-start | bytes 6148
  29.8 5.5 %collective-permute-start.14 = (bf16[4,3,3,32,128]{4,3,2,1,0:T(8,128)(2,1)S(1)}, bf16[4,3,3,32,128]{4,3,2,1,0:T(8,128)(2,1)S(1)}, u32[]{:S(2)}, u32[]{:S(2)}) collective-permute-start(bf16[4,3,3,32,128]{4,3,2,1,0:T(8,128)(2,1)S(1)} %pad_maximum_fusion.2), channel_id=1, source_target_pairs={{0,1},{1,0},{2,3},{3,2},{4,5},{5,4},{6,7},{7,6},{8,9},{9,8},{10,11... | collective-permute-start | bytes 884744 | tf_op jit(solution)/shard_map/ppermute | solution.py:113
  29.9 5.4 %collective-permute-start.16 = (bf16[3,3,3,32,128]{4,3,2,1,0:T(8,128)(2,1)S(1)}, bf16[3,3,3,32,128]{4,3,2,1,0:T(8,128)(2,1)S(1)}, u32[]{:S(2)}, u32[]{:S(2)}) collective-permute-start(bf16[3,3,3,32,128]{4,3,2,1,0:T(8,128)(2,1)S(1)} %collective-permute-done.13.x123), channel_id=1, source_target_pairs={{0,1},{1,0},{2,3},{3,2},{4,5},{5,4},{6,7},{7,6},{8,9},{9,8},{10,11... | collective-permute-start | bytes 663560 | tf_op jit(solution)/shard_map/ppermute | solution.py:113
  33.6 1.7 %collective-permute-start.15 = (bf16[3,3,32,128]{3,2,1,0:T(8,128)(2,1)S(1)}, bf16[3,3,32,128]{3,2,1,0:T(8,128)(2,1)S(1)}, u32[]{:S(2)}, u32[]{:S(2)}) collective-permute-start(bf16[3,3,32,128]{3,2,1,0:T(8,128)(2,1)S(1)} %collective-permute-done.12.x0), channel_id=1, source_target_pairs={{0,1},{1,0},{2,3},{3,2},{4,5},{5,4},{6,7},{7,6},{8,9},{9,8},{10,11... | collective-permute-start | bytes 221192 | tf_op jit(solution)/shard_map/ppermute | solution.py:113
  36.5 5.3 %collective-permute-start.17 = (bf16[2,48,512]{2,1,0:T(8,128)(2,1)S(1)}, bf16[2,48,512]{2,1,0:T(8,128)(2,1)S(1)}, u32[]{:S(2)}, u32[]{:S(2)}) collective-permute-start(bf16[2,48,512]{2,1,0:T(8,128)(2,1)S(1)} %get-tuple-element.18), channel_id=1, source_target_pairs={{0,4},{4,0},{8,12},{12,8},{1,5},{5,1},{9,13},{13,9},{2,6},{6,2},{1... | collective-permute-start | bytes 294920 | tf_op jit(solution)/shard_map/ppermute | solution.py:113
  38.0 5.9 %collective-permute-start.18 = (bf16[2,48,512]{2,1,0:T(8,128)(2,1)S(1)}, bf16[2,48,512]{2,1,0:T(8,128)(2,1)S(1)}, u32[]{:S(2)}, u32[]{:S(2)}) collective-permute-start(bf16[2,48,512]{2,1,0:T(8,128)(2,1)S(1)} %get-tuple-element.19), channel_id=1, source_target_pairs={{0,8},{4,12},{8,0},{12,4},{1,9},{5,13},{9,1},{13,5},{2,10},{6,14},... | collective-permute-start | bytes 294920 | tf_op jit(solution)/shard_map/ppermute | solution.py:113
  40.3 8.6 %collective-permute-start.19 = (bf16[2,48,512]{2,1,0:T(8,128)(2,1)S(1)}, bf16[2,48,512]{2,1,0:T(8,128)(2,1)S(1)}, u32[]{:S(2)}, u32[]{:S(2)}) collective-permute-start(bf16[2,48,512]{2,1,0:T(8,128)(2,1)S(1)} %get-tuple-element.20), channel_id=1, source_target_pairs={{0,12},{4,8},{8,4},{12,0},{1,13},{5,9},{9,5},{13,1},{2,14},{6,10},... | collective-permute-start | bytes 294920 | tf_op jit(solution)/shard_map/ppermute | solution.py:113
where the time goes:
time: 49.8 us; the launch traced here: 49.6 us
  starting transfers between devices  29.5 us (59%)
  waiting for transfers between devices  13 us (26%)
  Pallas kernels  4.28 us (9%)
  local copies, waits for them, and re-layouts  2.52 us (5%)
    ppermute x18, starting transfers between devices, swapped(): return lax.ppermute(array, axis, [(i, i ^ distance) for i in range(size)])  28.1 us
    ppermute x18, waiting for transfers between devices, swapped(): return lax.ppermute(array, axis, [(i, i ^ distance) for i in range(size)])  13 us
    pallas_call x5, Pallas kernels, call(): pl.pallas_call(kernel, out_shape=outs, in_specs=specs or [VMEM] * len(arg...  4.28 us
    unnamed x10, local copies, waits for them, and re-layouts  2.52 us
    ppermute x2, starting transfers between devices, across(): return lax.ppermute(array, 'row', pairs + [(j, i) for i, j in pairs])  1.35 us
  transfers between devices with their start and end apart: 20, of which 6 were waited for; matrix products, arithmetic and copies ran while one was open for 0% of the time, Pallas kernels for 3%

commit v1 on v0

--- a/solution.py
+++ b/solution.py
@@ -104,8 +104,7 @@
 BF16 = jnp.bfloat16
 F32 = jnp.float32
 VMEM = pl.BlockSpec(memory_space=pltpu.VMEM)
-ANY = pl.BlockSpec(memory_space=pl.ANY)
-MARKS = 8
+MARKS = 16
 
 
 def swapped(array, axis, distance):
@@ -131,39 +130,18 @@
     return jnp.where(column == edge, 0.0, pltpu.roll(flat, (-offset) % length, 0))
 
 
-def payload_kernel(frames_hbm, resets_hbm, out, frames, resets, sem):
-    copies = [
-        pltpu.make_async_copy(frames_hbm, frames, sem.at[0]),
-        pltpu.make_async_copy(resets_hbm, resets, sem.at[1]),
-    ]
-    for copy in copies:
-        copy.start()
-    for copy in copies:
-        copy.wait()
-    count, height, width, channels = frames.shape
-    blocks = count * width
-    for row in range(height):
-        values = jnp.concatenate([frames[k, row].astype(F32) for k in range(count)])
-        out[row * blocks : (row + 1) * blocks, :] = values.astype(BF16)
-    place = lax.broadcasted_iota(jnp.int32, (MARKS, channels), 0)
-    marks = jnp.zeros((MARKS, channels), F32)
-    for k in range(count):
-        marks = jnp.where(place == k, resets[k].astype(F32), marks)
-    out[height * blocks :, :] = marks.astype(BF16)
-
-
-def pieces_kernel(w, q0, q1, q2, q3):
+def pieces_kernel(w, marks, q0, q1, q2, q3):
     z = lax.axis_index("tm")
-    lanes = q0.shape[3]
+    outs, lanes = w.shape[2], q0.shape[1]
     for d, q in enumerate((q0, q1, q2, q3)):
-        here = pl.ds(pl.multiple_of((z ^ d) * lanes, lanes), lanes)
-        for i in range(3):
-            for j in range(3):
-                q[i, j] = w[i, j, :, here]
+        there = pl.ds(pl.multiple_of((z ^ d) * lanes, lanes), lanes)
+        for tap in range(9):
+            q[tap * outs : (tap + 1) * outs, :] = w[tap // 3, tap % 3, :, there]
+        q[9 * outs :, :] = marks[...]
 
 
 def drive_kernel(
-    dims, f0, f1, f2, f3, e012, e3, near, w0, w1, w2, w3, codes, hid, x, w, gates, states
+    dims, f0, f1, f2, f3, m0, m1, m2, m3, e012, e3, near, w0, w1, w2, w3, codes, hid, x, w, gates, states
 ):
     count, height, width, frame_total = dims
     blocks = count * width
@@ -174,17 +152,23 @@
     rates = jnp.exp(rate * (LOW_LOG + code / (LEVELS - 1) * (HIGH_LOG - LOW_LOG)))
     lanes = rates.shape[1]
     far = (e012.at[0], e012.at[1], e012.at[2], e3)
+    marks = (m0, m1, m2, m3)
     for d, f in enumerate((f0, f1, f2, f3)):
         at = z ^ d
         here = pl.ds(pl.multiple_of(at * blocks, blocks), blocks)
+
+        def placed(slot, source, row):
+            firsts = [(k * height + row) * width for k in range(count)]
+            parts = [source[first : first + width, :].astype(F32) for first in firsts]
+            x[slot, here, :] = jnp.concatenate(parts).astype(BF16)
+
         for row in range(height):
-            part = slice(row * blocks, (row + 1) * blocks)
-            x[height + row, here, :] = f[part, :]
-            x[2 * height * odd + row, here, :] = far[d][part, :]
-            x[2 * height * (1 - odd) + row, here, :] = near[d, part, :]
-        marks = f[height * blocks :, :lanes].astype(F32)
+            placed(height + row, f, row)
+            placed(2 * height * odd + row, far[d], row)
+            placed(2 * height * (1 - odd) + row, near.at[d], row)
+        mark = marks[d][marks[d].shape[0] - MARKS :, :].astype(F32)
         for k in range(count):
-            gates[pl.ds(at * count + k, 1), :] = (1.0 - marks[k : k + 1, :]) * rates
+            gates[pl.ds(at * count + k, 1), :] = (1.0 - mark[k : k + 1, :]) * rates
     for d, block in enumerate((w0, w1, w2, w3)):
         for i in range(3):
             for j in range(3):
@@ -215,24 +199,21 @@
         hid[row] = values.astype(BF16)
 
 
-def mix_kernel(dims, hid, q0, g1, g2, g3, x0, x123, c0, cx0, cx123, p0, p1, p2, p3, a, w, part):
+def mix_kernel(dims, hid, *refs):
     count, height, width = dims
-    z, r = lax.axis_index("tm"), lax.axis_index("row")
-    outs, lanes = q0.shape[2], q0.shape[3]
-    held = (
-        (q0, g1, g2, g3),
-        tuple(c0.at[e] for e in range(4)),
-        (x0,) + tuple(x123.at[e] for e in range(3)),
-        (cx0,) + tuple(cx123.at[e] for e in range(3)),
-    )
-    for d in range(4):
+    filters, (p0, p1, p2, p3, a, w, part) = refs[:-7], refs[-7:]
+    held = []
+    for ref in filters:
+        held += [ref.at[e] for e in range(ref.shape[0])] if len(ref.shape) == 3 else [ref]
+    z, core = lax.axis_index("tm"), lax.rem(lax.axis_index("row"), 2)
+    outs, lanes = (held[0].shape[0] - MARKS) // 9, held[0].shape[1]
+    for d in range(2):
         for e in range(4):
-            slot = (z ^ e) * 4 + (r ^ d)
+            slot = (z ^ e) * 2 + (core ^ d)
             here = pl.ds(pl.multiple_of(slot * outs, outs), outs)
-            for i in range(3):
-                for j in range(3):
-                    tap = 3 * i + j
-                    w[here, tap * lanes : (tap + 1) * lanes] = held[d][e][i, j]
+            for tap in range(9):
+                rows = held[4 * d + e][tap * outs : (tap + 1) * outs, :]
+                w[here, tap * lanes : (tap + 1) * lanes] = rows
     for row in range(height + 2):
         values = hid[row].astype(F32)
         for j in range(3):
@@ -251,8 +232,17 @@
             out[row] = part[row, here, :].astype(out.dtype)
 
 
-def sum_kernel(width, p0, p1, p2, p3, out):
-    total = p0[...] + p1[...].astype(F32) + p2[...].astype(F32) + p3[...].astype(F32)
+def sum_kernel(width, a0, a1, a2, a3, b0, b1, b2, b3, out):
+    near = a0[...] + a1[...].astype(F32) + a2[...].astype(F32) + a3[...].astype(F32)
+    far = b0[...] + b1[...].astype(F32) + b2[...].astype(F32) + b3[...].astype(F32)
+    first = lax.axis_index("row") < 2
+    low, high = jnp.where(first, near, far), jnp.where(first, far, near)
+    wide = low.shape[2] // 4
+    parts = []
+    for n in range(4):
+        here = slice(n * wide, (n + 1) * wide)
+        parts += [low[:, :, here], high[:, :, here]]
+    total = jnp.concatenate(parts, axis=2)
     for row in range(total.shape[0]):
         for k in range(total.shape[1] // width):
             out[k, row] = total[row, k * width : (k + 1) * width].astype(BF16)
@@ -282,34 +272,25 @@
     lanes = channels // 4
     outs = w_out.shape[3]
     shape = jax.ShapeDtypeStruct
+    f0 = frames.reshape(count * height * width, channels)
+    f2 = swapped(f0, "tm", 2)
+    f1 = swapped(f0, "tm", 1)
     w0 = w_in.transpose(0, 1, 3, 2)
     w2 = swapped(w0, "row", 2)
     w1 = swapped(w0, "row", 1)
-    f0 = call(
-        payload_kernel,
-        shape((height * blocks + MARKS, channels), BF16),
-        [
-            pltpu.VMEM(frames.shape, BF16),
-            pltpu.SMEM(resets.shape, resets.dtype),
-            pltpu.SemaphoreType.DMA((2,)),
-        ],
-        frames,
-        resets,
-        specs=[ANY, ANY],
-    )
-    f2 = swapped(f0, "tm", 2)
-    f1 = swapped(f0, "tm", 1)
-    piece = shape((3, 3, outs, lanes), BF16)
-    q0, q1, q2, q3 = call(pieces_kernel, (piece,) * 4, [], w_out.transpose(0, 1, 3, 2))
+    f3 = swapped(f2, "tm", 1)
+    e012 = across(jnp.stack([f0, f1, f2]))
+    e3 = across(f3)
+    near = swapped(jnp.stack([f0, f1, f2, f3]), "row", 1)
+    marks = jnp.pad(resets.astype(BF16), (0, MARKS - count))
+    marks = jnp.broadcast_to(marks[:, None], (MARKS, lanes))
+    piece = shape((9 * outs + MARKS, lanes), BF16)
+    q0, q1, q2, q3 = call(pieces_kernel, (piece,) * 4, [], w_out.transpose(0, 1, 3, 2), marks)
     x0 = swapped(q0, "row", 2)
+    g1 = swapped(q1, "tm", 1)
     g2 = swapped(q2, "tm", 2)
     g3 = swapped(q3, "tm", 3)
-    f3 = swapped(f2, "tm", 1)
-    e012 = across(jnp.stack([f0, f1, f2]))
-    g1 = swapped(q1, "tm", 1)
     w3 = swapped(w2, "row", 1)
-    e3 = across(f3)
-    near = swapped(jnp.stack([f0, f1, f2, f3]), "row", 1)
     x123 = swapped(jnp.stack([g1, g2, g3]), "row", 2)
     c0 = swapped(jnp.stack([q0, g1, g2, g3]), "row", 1)
     cx0 = swapped(x0, "row", 1)
@@ -327,6 +308,10 @@
         f1,
         f2,
         f3,
+        q0,
+        g1,
+        g2,
+        g3,
         e012,
         e3,
         near,
@@ -338,36 +323,28 @@
         flops=2 * (height + 2) * slab * 9 * channels * lanes,
     )
     cx123 = swapped(x123, "row", 1)
-    part = functools.partial(shape, (height, blocks, channels))
-    parts = call(
-        functools.partial(mix_kernel, (count, height, width)),
-        (part(F32), part(BF16), part(BF16), part(BF16)),
-        [
-            pltpu.VMEM((height, slab, 9 * lanes), BF16),
-            pltpu.VMEM((channels, 9 * lanes), BF16),
-            pltpu.VMEM((height, slab, channels), F32),
-        ],
-        hidden,
-        q0,
-        g1,
-        g2,
-        g3,
-        x0,
-        x123,
-        c0,
-        cx0,
-        cx123,
-        flops=2 * height * slab * 9 * channels * lanes,
-    )
-    received = {d: swapped(parts[d], "tm", d) for d in (3, 2, 1)}
+    half = channels // 2
+    part = functools.partial(shape, (height, blocks, half))
+
+    def mixed(*filters):
+        parts = call(
+            functools.partial(mix_kernel, (count, height, width)),
+            (part(F32), part(BF16), part(BF16), part(BF16)),
+            [
+                pltpu.VMEM((height, slab, 9 * lanes), BF16),
+                pltpu.VMEM((half, 9 * lanes), BF16),
+                pltpu.VMEM((height, slab, half), F32),
+            ],
+            hidden,
+            *filters,
+            flops=2 * height * slab * 9 * half * lanes,
+        )
+        return parts[:1] + tuple(swapped(parts[d], "tm", d) for d in (1, 2, 3))
+
+    own_sums = mixed(q0, g1, g2, g3, c0)
+    far_sums = mixed(x0, x123, cx0, cx123)
     return call(
-        functools.partial(sum_kernel, width),
-        shape(frames.shape, BF16),
-        [],
-        parts[0],
-        received[1],
-        received[2],
-        received[3],
+        functools.partial(sum_kernel, width), shape(frames.shape, BF16), [], *own_sums, *far_sums
     )
 
 

time: 49.8 us -> 53.9 us (1.082)
  starting transfers between devices: 29.5 us -> 37.6 us
  waiting for transfers between devices: 13 us -> 10.9 us
  local copies, waits for them, and re-layouts: 2.52 us -> 1.06 us
    ppermute x18 -> x21, starting transfers between devices: 28.1 us -> 36.2 us  [swapped(): return lax.ppermute(array, axis, [(i, i ^ distance) for i in range(size)])]
    ppermute x18 -> x21, waiting for transfers between devices: 13 us -> 10.9 us  [swapped(): return lax.ppermute(array, axis, [(i, i ^ distance) for i in range(size)])]
    unnamed x10, local copies, waits for them, and re-layouts: 2.52 us -> 0.98 us
  transfers between devices with their start and end apart: 20 -> 23, of which waited for: 6 -> 6; matrix products, arithmetic and copies ran while one was open for 0% -> 0% of each run, Pallas kernels for 3% -> 6%
where the time goes in v1:
time: 53.9 us; the launch traced here: 53.8 us
  starting transfers between devices  37.6 us (70%)
  waiting for transfers between devices  10.9 us (20%)
  Pallas kernels  3.93 us (7%)
  local copies, waits for them, and re-layouts  1.06 us (2%)
    ppermute x21, starting transfers between devices, swapped(): return lax.ppermute(array, axis, [(i, i ^ distance) for i in range(size)])  36.2 us
    ppermute x21, waiting for transfers between devices, swapped(): return lax.ppermute(array, axis, [(i, i ^ distance) for i in range(size)])  10.9 us
    pallas_call x5, Pallas kernels, call(): pl.pallas_call(kernel, out_shape=outs, in_specs=specs or [VMEM] * len(arg...  3.93 us
    ppermute x2, starting transfers between devices, across(): return lax.ppermute(array, 'row', pairs + [(j, i) for i, j in pairs])  1.35 us
  transfers between devices with their start and end apart: 23, of which 6 were waited for; matrix products, arithmetic and copies ran while one was open for 0% of the time, Pallas kernels for 6%

profile of v1, /device:TPU:0, one launch (start us, length us, event | category | flops | bytes accessed | tf_op | source)
XLA Modules:
  0.0 53.8 jit_solution(4488899429136365207)
XLA Ops:
  0.0 4.1 %collective-permute-start.1 = (bf16[96,512]{1,0:T(8,128)(2,1)}, bf16[96,512]{1,0:T(8,128)(2,1)S(1)}, u32[]{:S(2)}, u32[]{:S(2)}) collective-permute-start(bf16[96,512]{1,0:T(8,128)(2,1)} %bitcast.12), channel_id=1, source_target_pairs={{0,8},{4,12},{8,0},{12,4},{1,9},{5,13},{9,1},{13,5},{2,10},{6,14},... | collective-permute-start | bytes 294920 | tf_op jit(solution)/shard_map/ppermute | solution.py:112
  4.2 1.0 %copy-done.1 = bf16[3,3,512,32]{2,3,1,0:T(8,128)(2,1)S(1)} copy-done((bf16[3,3,512,32]{2,3,1,0:T(8,128)(2,1)S(1)}, bf16[3,3,512,32]{2,3,1,0:T(8,128)(2,1)}, u32[]{:S(2)}) %copy-start.1) | copy-done | bytes 294936
  5.2 1.6 %collective-permute-start.3 = (bf16[304,128]{1,0:T(8,128)(2,1)S(1)}, bf16[304,128]{1,0:T(8,128)(2,1)S(1)}, u32[]{:S(2)}, u32[]{:S(2)}) collective-permute-start(bf16[304,128]{1,0:T(8,128)(2,1)S(1)} %get-tuple-element.18), channel_id=1, source_target_pairs={{0,4},{4,0},{8,12},{12,8},{1,5},{5,1},{9,13},{13,9},{2,6},{6,2},{1... | collective-permute-start | bytes 233480 | tf_op jit(solution)/shard_map/ppermute | solution.py:112
  6.8 0.7 %collective-permute-start.4 = (bf16[304,128]{1,0:T(8,128)(2,1)S(1)}, bf16[304,128]{1,0:T(8,128)(2,1)S(1)}, u32[]{:S(2)}, u32[]{:S(2)}) collective-permute-start(bf16[304,128]{1,0:T(8,128)(2,1)S(1)} %get-tuple-element.19), channel_id=1, source_target_pairs={{0,8},{4,12},{8,0},{12,4},{1,9},{5,13},{9,1},{13,5},{2,10},{6,14},... | collective-permute-start | bytes 233480 | tf_op jit(solution)/shard_map/ppermute | solution.py:112
  7.5 2.2 %collective-permute-start.5 = (bf16[304,128]{1,0:T(8,128)(2,1)S(1)}, bf16[304,128]{1,0:T(8,128)(2,1)S(1)}, u32[]{:S(2)}, u32[]{:S(2)}) collective-permute-start(bf16[304,128]{1,0:T(8,128)(2,1)S(1)} %get-tuple-element.20), channel_id=1, source_target_pairs={{0,12},{4,8},{8,4},{12,0},{1,13},{5,9},{9,5},{13,1},{2,14},{6,10},... | collective-permute-start | bytes 233480 | tf_op jit(solution)/shard_map/ppermute | solution.py:112
  9.6 0.7 %collective-permute-start = (bf16[96,512]{1,0:T(8,128)(2,1)S(1)}, bf16[96,512]{1,0:T(8,128)(2,1)S(1)}, u32[]{:S(2)}, u32[]{:S(2)}) collective-permute-start(bf16[96,512]{1,0:T(8,128)(2,1)S(1)} %bitcast.13), channel_id=1, source_target_pairs={{0,4},{4,0},{8,12},{12,8},{1,5},{5,1},{9,13},{13,9},{2,6},{6,2},{1... | collective-permute-start | bytes 294920 | tf_op jit(solution)/shard_map/ppermute | solution.py:112
  10.3 0.1 collective-permute-done.3.m1.refs_1_
  10.5 1.5 %collective-permute-start.10 = (bf16[3,3,32,512]{3,2,1,0:T(8,128)(2,1)}, bf16[3,3,32,512]{3,2,1,0:T(8,128)(2,1)S(1)}, u32[]{:S(2)}, u32[]{:S(2)}) collective-permute-start(bf16[3,3,32,512]{3,2,1,0:T(8,128)(2,1)} %bitcast.30), channel_id=1, source_target_pairs={{0,2},{1,3},{2,0},{3,1},{4,6},{5,7},{6,4},{7,5},{8,10},{9,11},{10,... | collective-permute-start | bytes 884744 | tf_op jit(solution)/shard_map/ppermute | solution.py:112
  12.0 3.3 %collective-permute-done.4.m2.refs_2_ = bf16[304,128]{1,0:T(8,128)(2,1)S(1)} collective-permute-done((bf16[304,128]{1,0:T(8,128)(2,1)S(1)}, bf16[304,128]{1,0:T(8,128)(2,1)S(1)}, u32[]{:S(2)}, u32[]{:S(2)}) %collective-permute-start.4) | collective-permute-done | bytes 77856 | tf_op jit(solution)/shard_map/ppermute | solution.py:112
  15.3 1.5 %collective-permute-start.16 = (bf16[304,128]{1,0:T(8,128)(2,1)S(1)}, bf16[304,128]{1,0:T(8,128)(2,1)S(1)}, u32[]{:S(2)}, u32[]{:S(2)}) collective-permute-start(bf16[304,128]{1,0:T(8,128)(2,1)S(1)} %get-tuple-element.17.m0.refs_0_), channel_id=1, source_target_pairs={{0,2},{1,3},{2,0},{3,1},{4,6},{5,7},{6,4},{7,5},{8,10},{9,11},{10,... | collective-permute-start | bytes 233480 | tf_op jit(solution)/shard_map/ppermute | solution.py:112
  16.8 1.5 %collective-permute-start.2 = (bf16[96,512]{1,0:T(8,128)(2,1)S(1)}, bf16[96,512]{1,0:T(8,128)(2,1)S(1)}, u32[]{:S(2)}, u32[]{:S(2)}) collective-permute-start(bf16[96,512]{1,0:T(8,128)(2,1)S(1)} %collective-permute-done.1.f2), channel_id=1, source_target_pairs={{0,4},{4,0},{8,12},{12,8},{1,5},{5,1},{9,13},{13,9},{2,6},{6,2},{1... | collective-permute-start | bytes 294920 | tf_op jit(solution)/shard_map/ppermute | solution.py:112
  18.3 0.6 %collective-permute-start.17 = (bf16[3,304,128]{2,1,0:T(8,128)(2,1)S(1)}, bf16[3,304,128]{2,1,0:T(8,128)(2,1)S(1)}, u32[]{:S(2)}, u32[]{:S(2)}) collective-permute-start(bf16[3,304,128]{2,1,0:T(8,128)(2,1)S(1)} %pad_maximum_fusion.3), channel_id=1, source_target_pairs={{0,2},{1,3},{2,0},{3,1},{4,6},{5,7},{6,4},{7,5},{8,10},{9,11},{10,... | collective-permute-start | bytes 700424 | tf_op jit(solution)/shard_map/ppermute | solution.py:112
  18.9 2.8 %collective-permute-done.2.f3 = bf16[96,512]{1,0:T(8,128)(2,1)S(1)} collective-permute-done((bf16[96,512]{1,0:T(8,128)(2,1)S(1)}, bf16[96,512]{1,0:T(8,128)(2,1)S(1)}, u32[]{:S(2)}, u32[]{:S(2)}) %collective-permute-start.2) | collective-permute-done | bytes 98336 | tf_op jit(solution)/shard_map/ppermute | solution.py:112
  21.9 0.7 %collective-permute-start.7 = (bf16[96,512]{1,0:T(8,128)(2,1)S(1)}, bf16[96,512]{1,0:T(8,128)(2,1)S(1)}, u32[]{:S(2)}, u32[]{:S(2)}) collective-permute-start(bf16[96,512]{1,0:T(8,128)(2,1)S(1)} %collective-permute-done.2.f3), channel_id=1, source_target_pairs={{1,2},{2,1},{5,6},{6,5},{9,10},{10,9},{13,14},{14,13},{17,18},{18,... | collective-permute-start | bytes 294920 | tf_op jit(solution)/shard_map/ppermute | solution.py:117
  22.6 0.7 %collective-permute-start.6 = (bf16[3,96,512]{2,1,0:T(8,128)(2,1)S(1)}, bf16[3,96,512]{2,1,0:T(8,128)(2,1)S(1)}, u32[]{:S(2)}, u32[]{:S(2)}) collective-permute-start(bf16[3,96,512]{2,1,0:T(8,128)(2,1)S(1)} %pad_maximum_fusion.2), channel_id=1, source_target_pairs={{1,2},{2,1},{5,6},{6,5},{9,10},{10,9},{13,14},{14,13},{17,18},{18,... | collective-permute-start | bytes 884744 | tf_op jit(solution)/shard_map/ppermute | solution.py:117
  23.3 7.1 %collective-permute-start.11 = (bf16[3,3,32,512]{3,2,1,0:T(8,128)(2,1)S(1)}, bf16[3,3,32,512]{3,2,1,0:T(8,128)(2,1)S(1)}, u32[]{:S(2)}, u32[]{:S(2)}) collective-permute-start(bf16[3,3,32,512]{3,2,1,0:T(8,128)(2,1)S(1)} %collective-permute-done.10.w2), channel_id=1, source_target_pairs={{0,1},{1,0},{2,3},{3,2},{4,5},{5,4},{6,7},{7,6},{8,9},{9,8},{10,11... | collective-permute-start | bytes 884744 | tf_op jit(solution)/shard_map/ppermute | solution.py:112
  30.5 0.1 collective-permute-start.12
  30.6 0.5 collective-permute-start.19
  31.1 5.2 %collective-permute-start.18 = (bf16[304,128]{1,0:T(8,128)(2,1)S(1)}, bf16[304,128]{1,0:T(8,128)(2,1)S(1)}, u32[]{:S(2)}, u32[]{:S(2)}) collective-permute-start(bf16[304,128]{1,0:T(8,128)(2,1)S(1)} %collective-permute-done.16.refs_0_), channel_id=1, source_target_pairs={{0,1},{1,0},{2,3},{3,2},{4,5},{5,4},{6,7},{7,6},{8,9},{9,8},{10,11... | collective-permute-start | bytes 233480 | tf_op jit(solution)/shard_map/ppermute | solution.py:112
  36.4 1.7 %shard_map.56.hid = bf16[4,192,128]{2,1,0:T(8,128)(2,1)S(1)} custom-call(bf16[96,512]{1,0:T(8,128)(2,1)S(1)} %bitcast.16, bf16[96,512]{1,0:T(8,128)(2,1)S(1)} %collective-permute-done.f1, bf16[96,512]{1,0:T(8,128)(2,1)S(1)} %collective-permute-done.1.f2, bf16[96,512]{1,0:T(8,128)(2,1)S(1)} %collective-permute-done.2.f3, ...), custom_call_target="tpu_custom_call" | custom-call | flops 905969664 | bytes 2672640 | tf_op jit(solution)/shard_map/pallas_call | solution.py:253
  38.1 0.7 %shard_map.58 = (f32[2,48,256]{2,1,0:T(8,128)S(1)}, bf16[2,48,256]{2,1,0:T(8,128)(2,1)S(1)}, bf16[2,48,256]{2,1,0:T(8,128)(2,1)S(1)}, bf16[2,48,256]{2,1,0:T(8,128)(2,1)S(1)}) custom-call(bf16[4,192,128]{2,1,0:T(8,128)(2,1)S(1)} %shard_map.56.hid, bf16[304,128]{1,0:T(8,128)(2,1)S(1)} %collective-permute-done.16.refs_0_, ...), custom_call_target="tpu_custom_call" | custom-call | flops 226492416 | bytes 819200 | tf_op jit(solution)/shard_map/pallas_call | solution.py:253
  38.8 1.2 %collective-permute-start.20 = (bf16[2,48,256]{2,1,0:T(8,128)(2,1)S(1)}, bf16[2,48,256]{2,1,0:T(8,128)(2,1)S(1)}, u32[]{:S(2)}, u32[]{:S(2)}) collective-permute-start(bf16[2,48,256]{2,1,0:T(8,128)(2,1)S(1)} %get-tuple-element.26), channel_id=1, source_target_pairs={{0,4},{4,0},{8,12},{12,8},{1,5},{5,1},{9,13},{13,9},{2,6},{6,2},{1... | collective-permute-start | bytes 147464 | tf_op jit(solution)/shard_map/ppermute | solution.py:112
  40.0 1.9 %collective-permute-start.21 = (bf16[2,48,256]{2,1,0:T(8,128)(2,1)S(1)}, bf16[2,48,256]{2,1,0:T(8,128)(2,1)S(1)}, u32[]{:S(2)}, u32[]{:S(2)}) collective-permute-start(bf16[2,48,256]{2,1,0:T(8,128)(2,1)S(1)} %get-tuple-element.27), channel_id=1, source_target_pairs={{0,8},{4,12},{8,0},{12,4},{1,9},{5,13},{9,1},{13,5},{2,10},{6,14},... | collective-permute-start | bytes 147464 | tf_op jit(solution)/shard_map/ppermute | solution.py:112
  41.9 1.3 %collective-permute-start.22 = (bf16[2,48,256]{2,1,0:T(8,128)(2,1)S(1)}, bf16[2,48,256]{2,1,0:T(8,128)(2,1)S(1)}, u32[]{:S(2)}, u32[]{:S(2)}) collective-permute-start(bf16[2,48,256]{2,1,0:T(8,128)(2,1)S(1)} %get-tuple-element.28), channel_id=1, source_target_pairs={{0,12},{4,8},{8,4},{12,0},{1,13},{5,9},{9,5},{13,1},{2,14},{6,10},... | collective-permute-start | bytes 147464 | tf_op jit(solution)/shard_map/ppermute | solution.py:112
  43.2 0.7 %shard_map.57 = (f32[2,48,256]{2,1,0:T(8,128)S(1)}, bf16[2,48,256]{2,1,0:T(8,128)(2,1)S(1)}, bf16[2,48,256]{2,1,0:T(8,128)(2,1)S(1)}, bf16[2,48,256]{2,1,0:T(8,128)(2,1)S(1)}) custom-call(bf16[4,192,128]{2,1,0:T(8,128)(2,1)S(1)} %shard_map.56.hid, bf16[304,128]{1,0:T(8,128)(2,1)S(1)} %get-tuple-element.17.m0.refs_0_, ...), custom_call_target="tpu_custom_call" | custom-call | flops 226492416 | bytes 819200 | tf_op jit(solution)/shard_map/pallas_call | solution.py:253
  44.0 0.6 %collective-permute-start.13 = (bf16[2,48,256]{2,1,0:T(8,128)(2,1)S(1)}, bf16[2,48,256]{2,1,0:T(8,128)(2,1)S(1)}, u32[]{:S(2)}, u32[]{:S(2)}) collective-permute-start(bf16[2,48,256]{2,1,0:T(8,128)(2,1)S(1)} %get-tuple-element.22), channel_id=1, source_target_pairs={{0,4},{4,0},{8,12},{12,8},{1,5},{5,1},{9,13},{13,9},{2,6},{6,2},{1... | collective-permute-start | bytes 147464 | tf_op jit(solution)/shard_map/ppermute | solution.py:112
  44.5 2.6 %collective-permute-start.14 = (bf16[2,48,256]{2,1,0:T(8,128)(2,1)S(1)}, bf16[2,48,256]{2,1,0:T(8,128)(2,1)S(1)}, u32[]{:S(2)}, u32[]{:S(2)}) collective-permute-start(bf16[2,48,256]{2,1,0:T(8,128)(2,1)S(1)} %get-tuple-element.23), channel_id=1, source_target_pairs={{0,8},{4,12},{8,0},{12,4},{1,9},{5,13},{9,1},{13,5},{2,10},{6,14},... | collective-permute-start | bytes 147464 | tf_op jit(solution)/shard_map/ppermute | solution.py:112
  47.1 1.3 %collective-permute-start.15 = (bf16[2,48,256]{2,1,0:T(8,128)(2,1)S(1)}, bf16[2,48,256]{2,1,0:T(8,128)(2,1)S(1)}, u32[]{:S(2)}, u32[]{:S(2)}) collective-permute-start(bf16[2,48,256]{2,1,0:T(8,128)(2,1)S(1)} %get-tuple-element.24), channel_id=1, source_target_pairs={{0,12},{4,8},{8,4},{12,0},{1,13},{5,9},{9,5},{13,1},{2,14},{6,10},... | collective-permute-start | bytes 147464 | tf_op jit(solution)/shard_map/ppermute | solution.py:112
  48.4 0.3 collective-permute-done.13.a1
  48.8 1.3 %collective-permute-done.14.a2 = bf16[2,48,256]{2,1,0:T(8,128)(2,1)S(1)} collective-permute-done((bf16[2,48,256]{2,1,0:T(8,128)(2,1)S(1)}, bf16[2,48,256]{2,1,0:T(8,128)(2,1)S(1)}, u32[]{:S(2)}, u32[]{:S(2)}) %collective-permute-start.14) | collective-permute-done | bytes 49184 | tf_op jit(solution)/shard_map/ppermute | solution.py:112
  50.1 2.9 %collective-permute-done.15.a3 = bf16[2,48,256]{2,1,0:T(8,128)(2,1)S(1)} collective-permute-done((bf16[2,48,256]{2,1,0:T(8,128)(2,1)S(1)}, bf16[2,48,256]{2,1,0:T(8,128)(2,1)S(1)}, u32[]{:S(2)}, u32[]{:S(2)}) %collective-permute-start.15) | collective-permute-done | bytes 49184 | tf_op jit(solution)/shard_map/ppermute | solution.py:112
  53.0 0.8 %shard_map.59 = bf16[2,2,24,512]{3,2,1,0:T(8,128)(2,1)} custom-call(f32[2,48,256]{2,1,0:T(8,128)S(1)} %get-tuple-element.21.a0, bf16[2,48,256]{2,1,0:T(8,128)(2,1)S(1)} %collective-permute-done.13.a1, bf16[2,48,256]{2,1,0:T(8,128)(2,1)S(1)} %collective-permute-done.14.a2, bf16[2,48,256]{2,1,0:T(8,128)(2,1)S(1)} %collective-permute-done.15.a3, ...), custom_call_target="tpu_custom_call" | custom-call | bytes 491520 | tf_op jit(solution)/shard_map/pallas_call | solution.py:253
  (36 shorter events, 0.4 us)
Async XLA Ops:
  0.0 4.1 %copy-start.4 = (s32[2]{0:T(128)S(1)}, s32[2]{0:T(128)}, u32[]{:S(2)}) copy-start(s32[2]{0:T(128)} %param.9) | copy-start | bytes 28
  0.0 16.8 %collective-permute-start.1 = (bf16[96,512]{1,0:T(8,128)(2,1)}, bf16[96,512]{1,0:T(8,128)(2,1)S(1)}, u32[]{:S(2)}, u32[]{:S(2)}) collective-permute-start(bf16[96,512]{1,0:T(8,128)(2,1)} %bitcast.12), channel_id=1, source_target_pairs={{0,8},{4,12},{8,0},{12,4},{1,9},{5,13},{9,1},{13,5},{2,10},{6,14},... | collective-permute-start | bytes 294920 | tf_op jit(solution)/shard_map/ppermute | solution.py:112
  4.2 1.0 %copy-start.1 = (bf16[3,3,512,32]{2,3,1,0:T(8,128)(2,1)S(1)}, bf16[3,3,512,32]{2,3,1,0:T(8,128)(2,1)}, u32[]{:S(2)}) copy-start(bf16[3,3,512,32]{2,3,1,0:T(8,128)(2,1)} %param.7) | copy-start | bytes 884740
  5.1 4.5 %copy-start = (bf16[2,2,24,512]{3,2,1,0:T(8,128)(2,1)S(1)}, bf16[2,2,24,512]{3,2,1,0:T(8,128)(2,1)}, u32[]{:S(2)}) copy-start(bf16[2,2,24,512]{3,2,1,0:T(8,128)(2,1)} %param.5) | copy-start | bytes 294916
  5.2 5.3 %collective-permute-start.3 = (bf16[304,128]{1,0:T(8,128)(2,1)S(1)}, bf16[304,128]{1,0:T(8,128)(2,1)S(1)}, u32[]{:S(2)}, u32[]{:S(2)}) collective-permute-start(bf16[304,128]{1,0:T(8,128)(2,1)S(1)} %get-tuple-element.18), channel_id=1, source_target_pairs={{0,4},{4,0},{8,12},{12,8},{1,5},{5,1},{9,13},{13,9},{2,6},{6,2},{1... | collective-permute-start | bytes 233480 | tf_op jit(solution)/shard_map/ppermute | solution.py:112
  6.8 8.5 %collective-permute-start.4 = (bf16[304,128]{1,0:T(8,128)(2,1)S(1)}, bf16[304,128]{1,0:T(8,128)(2,1)S(1)}, u32[]{:S(2)}, u32[]{:S(2)}) collective-permute-start(bf16[304,128]{1,0:T(8,128)(2,1)S(1)} %get-tuple-element.19), channel_id=1, source_target_pairs={{0,8},{4,12},{8,0},{12,4},{1,9},{5,13},{9,1},{13,5},{2,10},{6,14},... | collective-permute-start | bytes 233480 | tf_op jit(solution)/shard_map/ppermute | solution.py:112
  7.5 7.8 %collective-permute-start.5 = (bf16[304,128]{1,0:T(8,128)(2,1)S(1)}, bf16[304,128]{1,0:T(8,128)(2,1)S(1)}, u32[]{:S(2)}, u32[]{:S(2)}) collective-permute-start(bf16[304,128]{1,0:T(8,128)(2,1)S(1)} %get-tuple-element.20), channel_id=1, source_target_pairs={{0,12},{4,8},{8,4},{12,0},{1,13},{5,9},{9,5},{13,1},{2,14},{6,10},... | collective-permute-start | bytes 233480 | tf_op jit(solution)/shard_map/ppermute | solution.py:112
  9.6 8.7 %collective-permute-start = (bf16[96,512]{1,0:T(8,128)(2,1)S(1)}, bf16[96,512]{1,0:T(8,128)(2,1)S(1)}, u32[]{:S(2)}, u32[]{:S(2)}) collective-permute-start(bf16[96,512]{1,0:T(8,128)(2,1)S(1)} %bitcast.13), channel_id=1, source_target_pairs={{0,4},{4,0},{8,12},{12,8},{1,5},{5,1},{9,13},{13,9},{2,6},{6,2},{1... | collective-permute-start | bytes 294920 | tf_op jit(solution)/shard_map/ppermute | solution.py:112
  10.5 12.8 %collective-permute-start.10 = (bf16[3,3,32,512]{3,2,1,0:T(8,128)(2,1)}, bf16[3,3,32,512]{3,2,1,0:T(8,128)(2,1)S(1)}, u32[]{:S(2)}, u32[]{:S(2)}) collective-permute-start(bf16[3,3,32,512]{3,2,1,0:T(8,128)(2,1)} %bitcast.30), channel_id=1, source_target_pairs={{0,2},{1,3},{2,0},{3,1},{4,6},{5,7},{6,4},{7,5},{8,10},{9,11},{10,... | collective-permute-start | bytes 884744 | tf_op jit(solution)/shard_map/ppermute | solution.py:112
  15.3 15.2 %collective-permute-start.9 = (bf16[3,3,32,512]{3,2,1,0:T(8,128)(2,1)}, bf16[3,3,32,512]{3,2,1,0:T(8,128)(2,1)S(1)}, u32[]{:S(2)}, u32[]{:S(2)}) collective-permute-start(bf16[3,3,32,512]{3,2,1,0:T(8,128)(2,1)} %bitcast.31), channel_id=1, source_target_pairs={{0,1},{1,0},{2,3},{3,2},{4,5},{5,4},{6,7},{7,6},{8,9},{9,8},{10,11... | collective-permute-start | bytes 884744 | tf_op jit(solution)/shard_map/ppermute | solution.py:112
  15.3 6.6 %collective-permute-start.16 = (bf16[304,128]{1,0:T(8,128)(2,1)S(1)}, bf16[304,128]{1,0:T(8,128)(2,1)S(1)}, u32[]{:S(2)}, u32[]{:S(2)}) collective-permute-start(bf16[304,128]{1,0:T(8,128)(2,1)S(1)} %get-tuple-element.17.m0.refs_0_), channel_id=1, source_target_pairs={{0,2},{1,3},{2,0},{3,1},{4,6},{5,7},{6,4},{7,5},{8,10},{9,11},{10,... | collective-permute-start | bytes 233480 | tf_op jit(solution)/shard_map/ppermute | solution.py:112
  16.8 4.9 %collective-permute-start.2 = (bf16[96,512]{1,0:T(8,128)(2,1)S(1)}, bf16[96,512]{1,0:T(8,128)(2,1)S(1)}, u32[]{:S(2)}, u32[]{:S(2)}) collective-permute-start(bf16[96,512]{1,0:T(8,128)(2,1)S(1)} %collective-permute-done.1.f2), channel_id=1, source_target_pairs={{0,4},{4,0},{8,12},{12,8},{1,5},{5,1},{9,13},{13,9},{2,6},{6,2},{1... | collective-permute-start | bytes 294920 | tf_op jit(solution)/shard_map/ppermute | solution.py:112
  18.3 12.3 %collective-permute-start.17 = (bf16[3,304,128]{2,1,0:T(8,128)(2,1)S(1)}, bf16[3,304,128]{2,1,0:T(8,128)(2,1)S(1)}, u32[]{:S(2)}, u32[]{:S(2)}) collective-permute-start(bf16[3,304,128]{2,1,0:T(8,128)(2,1)S(1)} %pad_maximum_fusion.3), channel_id=1, source_target_pairs={{0,2},{1,3},{2,0},{3,1},{4,6},{5,7},{6,4},{7,5},{8,10},{9,11},{10,... | collective-permute-start | bytes 700424 | tf_op jit(solution)/shard_map/ppermute | solution.py:112
  21.8 14.5 %collective-permute-start.8 = (bf16[4,96,512]{2,1,0:T(8,128)(2,1)S(1)}, bf16[4,96,512]{2,1,0:T(8,128)(2,1)S(1)}, u32[]{:S(2)}, u32[]{:S(2)}) collective-permute-start(bf16[4,96,512]{2,1,0:T(8,128)(2,1)S(1)} %pad_maximum_fusion), channel_id=1, source_target_pairs={{0,1},{1,0},{2,3},{3,2},{4,5},{5,4},{6,7},{7,6},{8,9},{9,8},{10,11... | collective-permute-start | bytes 1179656 | tf_op jit(solution)/shard_map/ppermute | solution.py:112
  21.9 0.7 %collective-permute-start.7 = (bf16[96,512]{1,0:T(8,128)(2,1)S(1)}, bf16[96,512]{1,0:T(8,128)(2,1)S(1)}, u32[]{:S(2)}, u32[]{:S(2)}) collective-permute-start(bf16[96,512]{1,0:T(8,128)(2,1)S(1)} %collective-permute-done.2.f3), channel_id=1, source_target_pairs={{1,2},{2,1},{5,6},{6,5},{9,10},{10,9},{13,14},{14,13},{17,18},{18,... | collective-permute-start | bytes 294920 | tf_op jit(solution)/shard_map/ppermute | solution.py:117
  22.6 8.5 %collective-permute-start.6 = (bf16[3,96,512]{2,1,0:T(8,128)(2,1)S(1)}, bf16[3,96,512]{2,1,0:T(8,128)(2,1)S(1)}, u32[]{:S(2)}, u32[]{:S(2)}) collective-permute-start(bf16[3,96,512]{2,1,0:T(8,128)(2,1)S(1)} %pad_maximum_fusion.2), channel_id=1, source_target_pairs={{1,2},{2,1},{5,6},{6,5},{9,10},{10,9},{13,14},{14,13},{17,18},{18,... | collective-permute-start | bytes 884744 | tf_op jit(solution)/shard_map/ppermute | solution.py:117
  23.3 13.0 %collective-permute-start.11 = (bf16[3,3,32,512]{3,2,1,0:T(8,128)(2,1)S(1)}, bf16[3,3,32,512]{3,2,1,0:T(8,128)(2,1)S(1)}, u32[]{:S(2)}, u32[]{:S(2)}) collective-permute-start(bf16[3,3,32,512]{3,2,1,0:T(8,128)(2,1)S(1)} %collective-permute-done.10.w2), channel_id=1, source_target_pairs={{0,1},{1,0},{2,3},{3,2},{4,5},{5,4},{6,7},{7,6},{8,9},{9,8},{10,11... | collective-permute-start | bytes 884744 | tf_op jit(solution)/shard_map/ppermute | solution.py:112
  30.5 5.9 %copy-start.2 = (bf16[3,3,512,32]{2,3,1,0:T(8,128)(2,1)S(1)}, bf16[3,3,512,32]{2,3,1,0:T(8,128)(2,1)}, u32[]{:S(2)}) copy-start(bf16[3,3,512,32]{2,3,1,0:T(8,128)(2,1)} %param.6) | copy-start | bytes 884740
  30.5 5.9 %copy-start.3 = (s32[512]{0:T(512)S(1)}, s32[512]{0:T(512)}, u32[]{:S(2)}) copy-start(s32[512]{0:T(512)} %param.8) | copy-start | bytes 6148
  30.5 12.7 %collective-permute-start.12 = (bf16[4,304,128]{2,1,0:T(8,128)(2,1)S(1)}, bf16[4,304,128]{2,1,0:T(8,128)(2,1)S(1)}, u32[]{:S(2)}, u32[]{:S(2)}) collective-permute-start(bf16[4,304,128]{2,1,0:T(8,128)(2,1)S(1)} %pad_maximum_fusion.1), channel_id=1, source_target_pairs={{0,1},{1,0},{2,3},{3,2},{4,5},{5,4},{6,7},{7,6},{8,9},{9,8},{10,11... | collective-permute-start | bytes 933896 | tf_op jit(solution)/shard_map/ppermute | solution.py:112
  30.6 7.4 %collective-permute-start.19 = (bf16[3,304,128]{2,1,0:T(8,128)(2,1)S(1)}, bf16[3,304,128]{2,1,0:T(8,128)(2,1)S(1)}, u32[]{:S(2)}, u32[]{:S(2)}) collective-permute-start(bf16[3,304,128]{2,1,0:T(8,128)(2,1)S(1)} %collective-permute-done.17.refs_1_), channel_id=1, source_target_pairs={{0,1},{1,0},{2,3},{3,2},{4,5},{5,4},{6,7},{7,6},{8,9},{9,8},{10,11... | collective-permute-start | bytes 700424 | tf_op jit(solution)/shard_map/ppermute | solution.py:112
  31.1 7.0 %collective-permute-start.18 = (bf16[304,128]{1,0:T(8,128)(2,1)S(1)}, bf16[304,128]{1,0:T(8,128)(2,1)S(1)}, u32[]{:S(2)}, u32[]{:S(2)}) collective-permute-start(bf16[304,128]{1,0:T(8,128)(2,1)S(1)} %collective-permute-done.16.refs_0_), channel_id=1, source_target_pairs={{0,1},{1,0},{2,3},{3,2},{4,5},{5,4},{6,7},{7,6},{8,9},{9,8},{10,11... | collective-permute-start | bytes 233480 | tf_op jit(solution)/shard_map/ppermute | solution.py:112
  38.8 8.3 %collective-permute-start.20 = (bf16[2,48,256]{2,1,0:T(8,128)(2,1)S(1)}, bf16[2,48,256]{2,1,0:T(8,128)(2,1)S(1)}, u32[]{:S(2)}, u32[]{:S(2)}) collective-permute-start(bf16[2,48,256]{2,1,0:T(8,128)(2,1)S(1)} %get-tuple-element.26), channel_id=1, source_target_pairs={{0,4},{4,0},{8,12},{12,8},{1,5},{5,1},{9,13},{13,9},{2,6},{6,2},{1... | collective-permute-start | bytes 147464 | tf_op jit(solution)/shard_map/ppermute | solution.py:112
  40.0 8.4 %collective-permute-start.21 = (bf16[2,48,256]{2,1,0:T(8,128)(2,1)S(1)}, bf16[2,48,256]{2,1,0:T(8,128)(2,1)S(1)}, u32[]{:S(2)}, u32[]{:S(2)}) collective-permute-start(bf16[2,48,256]{2,1,0:T(8,128)(2,1)S(1)} %get-tuple-element.27), channel_id=1, source_target_pairs={{0,8},{4,12},{8,0},{12,4},{1,9},{5,13},{9,1},{13,5},{2,10},{6,14},... | collective-permute-start | bytes 147464 | tf_op jit(solution)/shard_map/ppermute | solution.py:112
  41.9 6.5 %collective-permute-start.22 = (bf16[2,48,256]{2,1,0:T(8,128)(2,1)S(1)}, bf16[2,48,256]{2,1,0:T(8,128)(2,1)S(1)}, u32[]{:S(2)}, u32[]{:S(2)}) collective-permute-start(bf16[2,48,256]{2,1,0:T(8,128)(2,1)S(1)} %get-tuple-element.28), channel_id=1, source_target_pairs={{0,12},{4,8},{8,4},{12,0},{1,13},{5,9},{9,5},{13,1},{2,14},{6,10},... | collective-permute-start | bytes 147464 | tf_op jit(solution)/shard_map/ppermute | solution.py:112
  44.0 4.8 %collective-permute-start.13 = (bf16[2,48,256]{2,1,0:T(8,128)(2,1)S(1)}, bf16[2,48,256]{2,1,0:T(8,128)(2,1)S(1)}, u32[]{:S(2)}, u32[]{:S(2)}) collective-permute-start(bf16[2,48,256]{2,1,0:T(8,128)(2,1)S(1)} %get-tuple-element.22), channel_id=1, source_target_pairs={{0,4},{4,0},{8,12},{12,8},{1,5},{5,1},{9,13},{13,9},{2,6},{6,2},{1... | collective-permute-start | bytes 147464 | tf_op jit(solution)/shard_map/ppermute | solution.py:112
  44.5 5.5 %collective-permute-start.14 = (bf16[2,48,256]{2,1,0:T(8,128)(2,1)S(1)}, bf16[2,48,256]{2,1,0:T(8,128)(2,1)S(1)}, u32[]{:S(2)}, u32[]{:S(2)}) collective-permute-start(bf16[2,48,256]{2,1,0:T(8,128)(2,1)S(1)} %get-tuple-element.23), channel_id=1, source_target_pairs={{0,8},{4,12},{8,0},{12,4},{1,9},{5,13},{9,1},{13,5},{2,10},{6,14},... | collective-permute-start | bytes 147464 | tf_op jit(solution)/shard_map/ppermute | solution.py:112
  47.1 5.9 %collective-permute-start.15 = (bf16[2,48,256]{2,1,0:T(8,128)(2,1)S(1)}, bf16[2,48,256]{2,1,0:T(8,128)(2,1)S(1)}, u32[]{:S(2)}, u32[]{:S(2)}) collective-permute-start(bf16[2,48,256]{2,1,0:T(8,128)(2,1)S(1)} %get-tuple-element.24), channel_id=1, source_target_pairs={{0,12},{4,8},{8,4},{12,0},{1,13},{5,9},{9,5},{13,1},{2,14},{6,10},... | collective-permute-start | bytes 147464 | tf_op jit(solution)/shard_map/ppermute | solution.py:112

commit v2 on v1

--- a/solution.py
+++ b/solution.py
@@ -110,6 +110,10 @@
 def swapped(array, axis, distance):
     size = lax.axis_size(axis)
     return lax.ppermute(array, axis, [(i, i ^ distance) for i in range(size)])
+
+
+def stacked(*arrays):
+    return jnp.stack(arrays)
 
 
 def across(array):
@@ -279,9 +283,9 @@
     w2 = swapped(w0, "row", 2)
     w1 = swapped(w0, "row", 1)
     f3 = swapped(f2, "tm", 1)
-    e012 = across(jnp.stack([f0, f1, f2]))
+    e012 = across(stacked(f0, f1, f2))
     e3 = across(f3)
-    near = swapped(jnp.stack([f0, f1, f2, f3]), "row", 1)
+    near = swapped(stacked(f0, f1, f2, f3), "row", 1)
     marks = jnp.pad(resets.astype(BF16), (0, MARKS - count))
     marks = jnp.broadcast_to(marks[:, None], (MARKS, lanes))
     piece = shape((9 * outs + MARKS, lanes), BF16)
@@ -291,8 +295,8 @@
     g2 = swapped(q2, "tm", 2)
     g3 = swapped(q3, "tm", 3)
     w3 = swapped(w2, "row", 1)
-    x123 = swapped(jnp.stack([g1, g2, g3]), "row", 2)
-    c0 = swapped(jnp.stack([q0, g1, g2, g3]), "row", 1)
+    x123 = swapped(stacked(g1, g2, g3), "row", 2)
+    c0 = swapped(stacked(q0, g1, g2, g3), "row", 1)
     cx0 = swapped(x0, "row", 1)
     slab = total * width
     hidden = call(

time: 53.9 us -> 53.9 us (level)
  no operation moved by 1% of the time
where the time goes in v2:
time: 53.9 us; the launch traced here: 53.8 us
  starting transfers between devices  37.6 us (70%)
  waiting for transfers between devices  10.9 us (20%)
  Pallas kernels  3.93 us (7%)
  local copies, waits for them, and re-layouts  1.06 us (2%)
    ppermute x21, starting transfers between devices, swapped(): return lax.ppermute(array, axis, [(i, i ^ distance) for i in range(size)])  36.2 us
    ppermute x21, waiting for transfers between devices, swapped(): return lax.ppermute(array, axis, [(i, i ^ distance) for i in range(size)])  10.9 us
    pallas_call x5, Pallas kernels, call(): pl.pallas_call(kernel, out_shape=outs, in_specs=specs or [VMEM] * len(arg...  3.93 us
    ppermute x2, starting transfers between devices, across(): return lax.ppermute(array, 'row', pairs + [(j, i) for i, j in pairs])  1.35 us
  transfers between devices with their start and end apart: 23, of which 6 were waited for; matrix products, arithmetic and copies ran while one was open for 0% of the time, Pallas kernels for 6%

profile of v2, /device:TPU:0, one launch (start us, length us, event | category | flops | bytes accessed | tf_op | source)
XLA Modules:
  0.0 53.8 jit_solution(4488899429136365207)
XLA Ops:
  0.0 4.1 %collective-permute-start.1 = (bf16[96,512]{1,0:T(8,128)(2,1)}, bf16[96,512]{1,0:T(8,128)(2,1)S(1)}, u32[]{:S(2)}, u32[]{:S(2)}) collective-permute-start(bf16[96,512]{1,0:T(8,128)(2,1)} %bitcast.12), channel_id=1, source_target_pairs={{0,8},{4,12},{8,0},{12,4},{1,9},{5,13},{9,1},{13,5},{2,10},{6,14},... | collective-permute-start | bytes 294920 | tf_op jit(solution)/shard_map/ppermute | solution.py:112
  4.2 1.0 %copy-done.1 = bf16[3,3,512,32]{2,3,1,0:T(8,128)(2,1)S(1)} copy-done((bf16[3,3,512,32]{2,3,1,0:T(8,128)(2,1)S(1)}, bf16[3,3,512,32]{2,3,1,0:T(8,128)(2,1)}, u32[]{:S(2)}) %copy-start.1) | copy-done | bytes 294936
  5.2 1.6 %collective-permute-start.3 = (bf16[304,128]{1,0:T(8,128)(2,1)S(1)}, bf16[304,128]{1,0:T(8,128)(2,1)S(1)}, u32[]{:S(2)}, u32[]{:S(2)}) collective-permute-start(bf16[304,128]{1,0:T(8,128)(2,1)S(1)} %get-tuple-element.18), channel_id=1, source_target_pairs={{0,4},{4,0},{8,12},{12,8},{1,5},{5,1},{9,13},{13,9},{2,6},{6,2},{1... | collective-permute-start | bytes 233480 | tf_op jit(solution)/shard_map/ppermute | solution.py:112
  6.8 0.7 %collective-permute-start.4 = (bf16[304,128]{1,0:T(8,128)(2,1)S(1)}, bf16[304,128]{1,0:T(8,128)(2,1)S(1)}, u32[]{:S(2)}, u32[]{:S(2)}) collective-permute-start(bf16[304,128]{1,0:T(8,128)(2,1)S(1)} %get-tuple-element.19), channel_id=1, source_target_pairs={{0,8},{4,12},{8,0},{12,4},{1,9},{5,13},{9,1},{13,5},{2,10},{6,14},... | collective-permute-start | bytes 233480 | tf_op jit(solution)/shard_map/ppermute | solution.py:112
  7.5 2.2 %collective-permute-start.5 = (bf16[304,128]{1,0:T(8,128)(2,1)S(1)}, bf16[304,128]{1,0:T(8,128)(2,1)S(1)}, u32[]{:S(2)}, u32[]{:S(2)}) collective-permute-start(bf16[304,128]{1,0:T(8,128)(2,1)S(1)} %get-tuple-element.20), channel_id=1, source_target_pairs={{0,12},{4,8},{8,4},{12,0},{1,13},{5,9},{9,5},{13,1},{2,14},{6,10},... | collective-permute-start | bytes 233480 | tf_op jit(solution)/shard_map/ppermute | solution.py:112
  9.6 0.7 %collective-permute-start = (bf16[96,512]{1,0:T(8,128)(2,1)S(1)}, bf16[96,512]{1,0:T(8,128)(2,1)S(1)}, u32[]{:S(2)}, u32[]{:S(2)}) collective-permute-start(bf16[96,512]{1,0:T(8,128)(2,1)S(1)} %bitcast.13), channel_id=1, source_target_pairs={{0,4},{4,0},{8,12},{12,8},{1,5},{5,1},{9,13},{13,9},{2,6},{6,2},{1... | collective-permute-start | bytes 294920 | tf_op jit(solution)/shard_map/ppermute | solution.py:112
  10.3 0.1 collective-permute-done.3.m1.refs_1_
  10.5 1.5 %collective-permute-start.10 = (bf16[3,3,32,512]{3,2,1,0:T(8,128)(2,1)}, bf16[3,3,32,512]{3,2,1,0:T(8,128)(2,1)S(1)}, u32[]{:S(2)}, u32[]{:S(2)}) collective-permute-start(bf16[3,3,32,512]{3,2,1,0:T(8,128)(2,1)} %bitcast.30), channel_id=1, source_target_pairs={{0,2},{1,3},{2,0},{3,1},{4,6},{5,7},{6,4},{7,5},{8,10},{9,11},{10,... | collective-permute-start | bytes 884744 | tf_op jit(solution)/shard_map/ppermute | solution.py:112
  12.0 3.3 %collective-permute-done.4.m2.refs_2_ = bf16[304,128]{1,0:T(8,128)(2,1)S(1)} collective-permute-done((bf16[304,128]{1,0:T(8,128)(2,1)S(1)}, bf16[304,128]{1,0:T(8,128)(2,1)S(1)}, u32[]{:S(2)}, u32[]{:S(2)}) %collective-permute-start.4) | collective-permute-done | bytes 77856 | tf_op jit(solution)/shard_map/ppermute | solution.py:112
  15.3 1.5 %collective-permute-start.16 = (bf16[304,128]{1,0:T(8,128)(2,1)S(1)}, bf16[304,128]{1,0:T(8,128)(2,1)S(1)}, u32[]{:S(2)}, u32[]{:S(2)}) collective-permute-start(bf16[304,128]{1,0:T(8,128)(2,1)S(1)} %get-tuple-element.17.m0.refs_0_), channel_id=1, source_target_pairs={{0,2},{1,3},{2,0},{3,1},{4,6},{5,7},{6,4},{7,5},{8,10},{9,11},{10,... | collective-permute-start | bytes 233480 | tf_op jit(solution)/shard_map/ppermute | solution.py:112
  16.8 1.5 %collective-permute-start.2 = (bf16[96,512]{1,0:T(8,128)(2,1)S(1)}, bf16[96,512]{1,0:T(8,128)(2,1)S(1)}, u32[]{:S(2)}, u32[]{:S(2)}) collective-permute-start(bf16[96,512]{1,0:T(8,128)(2,1)S(1)} %collective-permute-done.1.f2), channel_id=1, source_target_pairs={{0,4},{4,0},{8,12},{12,8},{1,5},{5,1},{9,13},{13,9},{2,6},{6,2},{1... | collective-permute-start | bytes 294920 | tf_op jit(solution)/shard_map/ppermute | solution.py:112
  18.3 0.6 %collective-permute-start.17 = (bf16[3,304,128]{2,1,0:T(8,128)(2,1)S(1)}, bf16[3,304,128]{2,1,0:T(8,128)(2,1)S(1)}, u32[]{:S(2)}, u32[]{:S(2)}) collective-permute-start(bf16[3,304,128]{2,1,0:T(8,128)(2,1)S(1)} %pad_maximum_fusion.3), channel_id=1, source_target_pairs={{0,2},{1,3},{2,0},{3,1},{4,6},{5,7},{6,4},{7,5},{8,10},{9,11},{10,... | collective-permute-start | bytes 700424 | tf_op jit(solution)/shard_map/ppermute | solution.py:112
  18.9 2.8 %collective-permute-done.2.f3 = bf16[96,512]{1,0:T(8,128)(2,1)S(1)} collective-permute-done((bf16[96,512]{1,0:T(8,128)(2,1)S(1)}, bf16[96,512]{1,0:T(8,128)(2,1)S(1)}, u32[]{:S(2)}, u32[]{:S(2)}) %collective-permute-start.2) | collective-permute-done | bytes 98336 | tf_op jit(solution)/shard_map/ppermute | solution.py:112
  21.9 0.7 %collective-permute-start.7 = (bf16[96,512]{1,0:T(8,128)(2,1)S(1)}, bf16[96,512]{1,0:T(8,128)(2,1)S(1)}, u32[]{:S(2)}, u32[]{:S(2)}) collective-permute-start(bf16[96,512]{1,0:T(8,128)(2,1)S(1)} %collective-permute-done.2.f3), channel_id=1, source_target_pairs={{1,2},{2,1},{5,6},{6,5},{9,10},{10,9},{13,14},{14,13},{17,18},{18,... | collective-permute-start | bytes 294920 | tf_op jit(solution)/shard_map/ppermute | solution.py:121
  22.6 0.7 %collective-permute-start.6 = (bf16[3,96,512]{2,1,0:T(8,128)(2,1)S(1)}, bf16[3,96,512]{2,1,0:T(8,128)(2,1)S(1)}, u32[]{:S(2)}, u32[]{:S(2)}) collective-permute-start(bf16[3,96,512]{2,1,0:T(8,128)(2,1)S(1)} %pad_maximum_fusion.2), channel_id=1, source_target_pairs={{1,2},{2,1},{5,6},{6,5},{9,10},{10,9},{13,14},{14,13},{17,18},{18,... | collective-permute-start | bytes 884744 | tf_op jit(solution)/shard_map/ppermute | solution.py:121
  23.3 7.1 %collective-permute-start.11 = (bf16[3,3,32,512]{3,2,1,0:T(8,128)(2,1)S(1)}, bf16[3,3,32,512]{3,2,1,0:T(8,128)(2,1)S(1)}, u32[]{:S(2)}, u32[]{:S(2)}) collective-permute-start(bf16[3,3,32,512]{3,2,1,0:T(8,128)(2,1)S(1)} %collective-permute-done.10.w2), channel_id=1, source_target_pairs={{0,1},{1,0},{2,3},{3,2},{4,5},{5,4},{6,7},{7,6},{8,9},{9,8},{10,11... | collective-permute-start | bytes 884744 | tf_op jit(solution)/shard_map/ppermute | solution.py:112
  30.5 0.1 collective-permute-start.12
  30.6 0.5 collective-permute-start.19
  31.1 5.2 %collective-permute-start.18 = (bf16[304,128]{1,0:T(8,128)(2,1)S(1)}, bf16[304,128]{1,0:T(8,128)(2,1)S(1)}, u32[]{:S(2)}, u32[]{:S(2)}) collective-permute-start(bf16[304,128]{1,0:T(8,128)(2,1)S(1)} %collective-permute-done.16.refs_0_), channel_id=1, source_target_pairs={{0,1},{1,0},{2,3},{3,2},{4,5},{5,4},{6,7},{7,6},{8,9},{9,8},{10,11... | collective-permute-start | bytes 233480 | tf_op jit(solution)/shard_map/ppermute | solution.py:112
  36.4 1.7 %shard_map.56.hid = bf16[4,192,128]{2,1,0:T(8,128)(2,1)S(1)} custom-call(bf16[96,512]{1,0:T(8,128)(2,1)S(1)} %bitcast.16, bf16[96,512]{1,0:T(8,128)(2,1)S(1)} %collective-permute-done.f1, bf16[96,512]{1,0:T(8,128)(2,1)S(1)} %collective-permute-done.1.f2, bf16[96,512]{1,0:T(8,128)(2,1)S(1)} %collective-permute-done.2.f3, ...), custom_call_target="tpu_custom_call" | custom-call | flops 905969664 | bytes 2672640 | tf_op jit(solution)/shard_map/pallas_call | solution.py:257
  38.1 0.7 %shard_map.58 = (f32[2,48,256]{2,1,0:T(8,128)S(1)}, bf16[2,48,256]{2,1,0:T(8,128)(2,1)S(1)}, bf16[2,48,256]{2,1,0:T(8,128)(2,1)S(1)}, bf16[2,48,256]{2,1,0:T(8,128)(2,1)S(1)}) custom-call(bf16[4,192,128]{2,1,0:T(8,128)(2,1)S(1)} %shard_map.56.hid, bf16[304,128]{1,0:T(8,128)(2,1)S(1)} %collective-permute-done.16.refs_0_, ...), custom_call_target="tpu_custom_call" | custom-call | flops 226492416 | bytes 819200 | tf_op jit(solution)/shard_map/pallas_call | solution.py:257
  38.8 1.2 %collective-permute-start.20 = (bf16[2,48,256]{2,1,0:T(8,128)(2,1)S(1)}, bf16[2,48,256]{2,1,0:T(8,128)(2,1)S(1)}, u32[]{:S(2)}, u32[]{:S(2)}) collective-permute-start(bf16[2,48,256]{2,1,0:T(8,128)(2,1)S(1)} %get-tuple-element.26), channel_id=1, source_target_pairs={{0,4},{4,0},{8,12},{12,8},{1,5},{5,1},{9,13},{13,9},{2,6},{6,2},{1... | collective-permute-start | bytes 147464 | tf_op jit(solution)/shard_map/ppermute | solution.py:112
  40.0 1.9 %collective-permute-start.21 = (bf16[2,48,256]{2,1,0:T(8,128)(2,1)S(1)}, bf16[2,48,256]{2,1,0:T(8,128)(2,1)S(1)}, u32[]{:S(2)}, u32[]{:S(2)}) collective-permute-start(bf16[2,48,256]{2,1,0:T(8,128)(2,1)S(1)} %get-tuple-element.27), channel_id=1, source_target_pairs={{0,8},{4,12},{8,0},{12,4},{1,9},{5,13},{9,1},{13,5},{2,10},{6,14},... | collective-permute-start | bytes 147464 | tf_op jit(solution)/shard_map/ppermute | solution.py:112
  41.9 1.3 %collective-permute-start.22 = (bf16[2,48,256]{2,1,0:T(8,128)(2,1)S(1)}, bf16[2,48,256]{2,1,0:T(8,128)(2,1)S(1)}, u32[]{:S(2)}, u32[]{:S(2)}) collective-permute-start(bf16[2,48,256]{2,1,0:T(8,128)(2,1)S(1)} %get-tuple-element.28), channel_id=1, source_target_pairs={{0,12},{4,8},{8,4},{12,0},{1,13},{5,9},{9,5},{13,1},{2,14},{6,10},... | collective-permute-start | bytes 147464 | tf_op jit(solution)/shard_map/ppermute | solution.py:112
  43.2 0.7 %shard_map.57 = (f32[2,48,256]{2,1,0:T(8,128)S(1)}, bf16[2,48,256]{2,1,0:T(8,128)(2,1)S(1)}, bf16[2,48,256]{2,1,0:T(8,128)(2,1)S(1)}, bf16[2,48,256]{2,1,0:T(8,128)(2,1)S(1)}) custom-call(bf16[4,192,128]{2,1,0:T(8,128)(2,1)S(1)} %shard_map.56.hid, bf16[304,128]{1,0:T(8,128)(2,1)S(1)} %get-tuple-element.17.m0.refs_0_, ...), custom_call_target="tpu_custom_call" | custom-call | flops 226492416 | bytes 819200 | tf_op jit(solution)/shard_map/pallas_call | solution.py:257
  44.0 0.6 %collective-permute-start.13 = (bf16[2,48,256]{2,1,0:T(8,128)(2,1)S(1)}, bf16[2,48,256]{2,1,0:T(8,128)(2,1)S(1)}, u32[]{:S(2)}, u32[]{:S(2)}) collective-permute-start(bf16[2,48,256]{2,1,0:T(8,128)(2,1)S(1)} %get-tuple-element.22), channel_id=1, source_target_pairs={{0,4},{4,0},{8,12},{12,8},{1,5},{5,1},{9,13},{13,9},{2,6},{6,2},{1... | collective-permute-start | bytes 147464 | tf_op jit(solution)/shard_map/ppermute | solution.py:112
  44.5 2.6 %collective-permute-start.14 = (bf16[2,48,256]{2,1,0:T(8,128)(2,1)S(1)}, bf16[2,48,256]{2,1,0:T(8,128)(2,1)S(1)}, u32[]{:S(2)}, u32[]{:S(2)}) collective-permute-start(bf16[2,48,256]{2,1,0:T(8,128)(2,1)S(1)} %get-tuple-element.23), channel_id=1, source_target_pairs={{0,8},{4,12},{8,0},{12,4},{1,9},{5,13},{9,1},{13,5},{2,10},{6,14},... | collective-permute-start | bytes 147464 | tf_op jit(solution)/shard_map/ppermute | solution.py:112
  47.1 1.3 %collective-permute-start.15 = (bf16[2,48,256]{2,1,0:T(8,128)(2,1)S(1)}, bf16[2,48,256]{2,1,0:T(8,128)(2,1)S(1)}, u32[]{:S(2)}, u32[]{:S(2)}) collective-permute-start(bf16[2,48,256]{2,1,0:T(8,128)(2,1)S(1)} %get-tuple-element.24), channel_id=1, source_target_pairs={{0,12},{4,8},{8,4},{12,0},{1,13},{5,9},{9,5},{13,1},{2,14},{6,10},... | collective-permute-start | bytes 147464 | tf_op jit(solution)/shard_map/ppermute | solution.py:112
  48.4 0.3 collective-permute-done.13.a1
  48.8 1.3 %collective-permute-done.14.a2 = bf16[2,48,256]{2,1,0:T(8,128)(2,1)S(1)} collective-permute-done((bf16[2,48,256]{2,1,0:T(8,128)(2,1)S(1)}, bf16[2,48,256]{2,1,0:T(8,128)(2,1)S(1)}, u32[]{:S(2)}, u32[]{:S(2)}) %collective-permute-start.14) | collective-permute-done | bytes 49184 | tf_op jit(solution)/shard_map/ppermute | solution.py:112
  50.1 2.9 %collective-permute-done.15.a3 = bf16[2,48,256]{2,1,0:T(8,128)(2,1)S(1)} collective-permute-done((bf16[2,48,256]{2,1,0:T(8,128)(2,1)S(1)}, bf16[2,48,256]{2,1,0:T(8,128)(2,1)S(1)}, u32[]{:S(2)}, u32[]{:S(2)}) %collective-permute-start.15) | collective-permute-done | bytes 49184 | tf_op jit(solution)/shard_map/ppermute | solution.py:112
  53.0 0.8 %shard_map.59 = bf16[2,2,24,512]{3,2,1,0:T(8,128)(2,1)} custom-call(f32[2,48,256]{2,1,0:T(8,128)S(1)} %get-tuple-element.21.a0, bf16[2,48,256]{2,1,0:T(8,128)(2,1)S(1)} %collective-permute-done.13.a1, bf16[2,48,256]{2,1,0:T(8,128)(2,1)S(1)} %collective-permute-done.14.a2, bf16[2,48,256]{2,1,0:T(8,128)(2,1)S(1)} %collective-permute-done.15.a3, ...), custom_call_target="tpu_custom_call" | custom-call | bytes 491520 | tf_op jit(solution)/shard_map/pallas_call | solution.py:257
  (36 shorter events, 0.4 us)
Async XLA Ops:
  0.0 4.1 %copy-start.4 = (s32[2]{0:T(128)S(1)}, s32[2]{0:T(128)}, u32[]{:S(2)}) copy-start(s32[2]{0:T(128)} %param.9) | copy-start | bytes 28
  0.0 16.8 %collective-permute-start.1 = (bf16[96,512]{1,0:T(8,128)(2,1)}, bf16[96,512]{1,0:T(8,128)(2,1)S(1)}, u32[]{:S(2)}, u32[]{:S(2)}) collective-permute-start(bf16[96,512]{1,0:T(8,128)(2,1)} %bitcast.12), channel_id=1, source_target_pairs={{0,8},{4,12},{8,0},{12,4},{1,9},{5,13},{9,1},{13,5},{2,10},{6,14},... | collective-permute-start | bytes 294920 | tf_op jit(solution)/shard_map/ppermute | solution.py:112
  4.2 1.0 %copy-start.1 = (bf16[3,3,512,32]{2,3,1,0:T(8,128)(2,1)S(1)}, bf16[3,3,512,32]{2,3,1,0:T(8,128)(2,1)}, u32[]{:S(2)}) copy-start(bf16[3,3,512,32]{2,3,1,0:T(8,128)(2,1)} %param.7) | copy-start | bytes 884740
  5.1 4.5 %copy-start = (bf16[2,2,24,512]{3,2,1,0:T(8,128)(2,1)S(1)}, bf16[2,2,24,512]{3,2,1,0:T(8,128)(2,1)}, u32[]{:S(2)}) copy-start(bf16[2,2,24,512]{3,2,1,0:T(8,128)(2,1)} %param.5) | copy-start | bytes 294916
  5.2 5.3 %collective-permute-start.3 = (bf16[304,128]{1,0:T(8,128)(2,1)S(1)}, bf16[304,128]{1,0:T(8,128)(2,1)S(1)}, u32[]{:S(2)}, u32[]{:S(2)}) collective-permute-start(bf16[304,128]{1,0:T(8,128)(2,1)S(1)} %get-tuple-element.18), channel_id=1, source_target_pairs={{0,4},{4,0},{8,12},{12,8},{1,5},{5,1},{9,13},{13,9},{2,6},{6,2},{1... | collective-permute-start | bytes 233480 | tf_op jit(solution)/shard_map/ppermute | solution.py:112
  6.8 8.5 %collective-permute-start.4 = (bf16[304,128]{1,0:T(8,128)(2,1)S(1)}, bf16[304,128]{1,0:T(8,128)(2,1)S(1)}, u32[]{:S(2)}, u32[]{:S(2)}) collective-permute-start(bf16[304,128]{1,0:T(8,128)(2,1)S(1)} %get-tuple-element.19), channel_id=1, source_target_pairs={{0,8},{4,12},{8,0},{12,4},{1,9},{5,13},{9,1},{13,5},{2,10},{6,14},... | collective-permute-start | bytes 233480 | tf_op jit(solution)/shard_map/ppermute | solution.py:112
  7.5 7.8 %collective-permute-start.5 = (bf16[304,128]{1,0:T(8,128)(2,1)S(1)}, bf16[304,128]{1,0:T(8,128)(2,1)S(1)}, u32[]{:S(2)}, u32[]{:S(2)}) collective-permute-start(bf16[304,128]{1,0:T(8,128)(2,1)S(1)} %get-tuple-element.20), channel_id=1, source_target_pairs={{0,12},{4,8},{8,4},{12,0},{1,13},{5,9},{9,5},{13,1},{2,14},{6,10},... | collective-permute-start | bytes 233480 | tf_op jit(solution)/shard_map/ppermute | solution.py:112
  9.6 8.7 %collective-permute-start = (bf16[96,512]{1,0:T(8,128)(2,1)S(1)}, bf16[96,512]{1,0:T(8,128)(2,1)S(1)}, u32[]{:S(2)}, u32[]{:S(2)}) collective-permute-start(bf16[96,512]{1,0:T(8,128)(2,1)S(1)} %bitcast.13), channel_id=1, source_target_pairs={{0,4},{4,0},{8,12},{12,8},{1,5},{5,1},{9,13},{13,9},{2,6},{6,2},{1... | collective-permute-start | bytes 294920 | tf_op jit(solution)/shard_map/ppermute | solution.py:112
  10.5 12.8 %collective-permute-start.10 = (bf16[3,3,32,512]{3,2,1,0:T(8,128)(2,1)}, bf16[3,3,32,512]{3,2,1,0:T(8,128)(2,1)S(1)}, u32[]{:S(2)}, u32[]{:S(2)}) collective-permute-start(bf16[3,3,32,512]{3,2,1,0:T(8,128)(2,1)} %bitcast.30), channel_id=1, source_target_pairs={{0,2},{1,3},{2,0},{3,1},{4,6},{5,7},{6,4},{7,5},{8,10},{9,11},{10,... | collective-permute-start | bytes 884744 | tf_op jit(solution)/shard_map/ppermute | solution.py:112
  15.3 15.2 %collective-permute-start.9 = (bf16[3,3,32,512]{3,2,1,0:T(8,128)(2,1)}, bf16[3,3,32,512]{3,2,1,0:T(8,128)(2,1)S(1)}, u32[]{:S(2)}, u32[]{:S(2)}) collective-permute-start(bf16[3,3,32,512]{3,2,1,0:T(8,128)(2,1)} %bitcast.31), channel_id=1, source_target_pairs={{0,1},{1,0},{2,3},{3,2},{4,5},{5,4},{6,7},{7,6},{8,9},{9,8},{10,11... | collective-permute-start | bytes 884744 | tf_op jit(solution)/shard_map/ppermute | solution.py:112
  15.3 6.6 %collective-permute-start.16 = (bf16[304,128]{1,0:T(8,128)(2,1)S(1)}, bf16[304,128]{1,0:T(8,128)(2,1)S(1)}, u32[]{:S(2)}, u32[]{:S(2)}) collective-permute-start(bf16[304,128]{1,0:T(8,128)(2,1)S(1)} %get-tuple-element.17.m0.refs_0_), channel_id=1, source_target_pairs={{0,2},{1,3},{2,0},{3,1},{4,6},{5,7},{6,4},{7,5},{8,10},{9,11},{10,... | collective-permute-start | bytes 233480 | tf_op jit(solution)/shard_map/ppermute | solution.py:112
  16.8 4.9 %collective-permute-start.2 = (bf16[96,512]{1,0:T(8,128)(2,1)S(1)}, bf16[96,512]{1,0:T(8,128)(2,1)S(1)}, u32[]{:S(2)}, u32[]{:S(2)}) collective-permute-start(bf16[96,512]{1,0:T(8,128)(2,1)S(1)} %collective-permute-done.1.f2), channel_id=1, source_target_pairs={{0,4},{4,0},{8,12},{12,8},{1,5},{5,1},{9,13},{13,9},{2,6},{6,2},{1... | collective-permute-start | bytes 294920 | tf_op jit(solution)/shard_map/ppermute | solution.py:112
  18.3 12.3 %collective-permute-start.17 = (bf16[3,304,128]{2,1,0:T(8,128)(2,1)S(1)}, bf16[3,304,128]{2,1,0:T(8,128)(2,1)S(1)}, u32[]{:S(2)}, u32[]{:S(2)}) collective-permute-start(bf16[3,304,128]{2,1,0:T(8,128)(2,1)S(1)} %pad_maximum_fusion.3), channel_id=1, source_target_pairs={{0,2},{1,3},{2,0},{3,1},{4,6},{5,7},{6,4},{7,5},{8,10},{9,11},{10,... | collective-permute-start | bytes 700424 | tf_op jit(solution)/shard_map/ppermute | solution.py:112
  21.8 14.5 %collective-permute-start.8 = (bf16[4,96,512]{2,1,0:T(8,128)(2,1)S(1)}, bf16[4,96,512]{2,1,0:T(8,128)(2,1)S(1)}, u32[]{:S(2)}, u32[]{:S(2)}) collective-permute-start(bf16[4,96,512]{2,1,0:T(8,128)(2,1)S(1)} %pad_maximum_fusion), channel_id=1, source_target_pairs={{0,1},{1,0},{2,3},{3,2},{4,5},{5,4},{6,7},{7,6},{8,9},{9,8},{10,11... | collective-permute-start | bytes 1179656 | tf_op jit(solution)/shard_map/ppermute | solution.py:112
  21.9 0.7 %collective-permute-start.7 = (bf16[96,512]{1,0:T(8,128)(2,1)S(1)}, bf16[96,512]{1,0:T(8,128)(2,1)S(1)}, u32[]{:S(2)}, u32[]{:S(2)}) collective-permute-start(bf16[96,512]{1,0:T(8,128)(2,1)S(1)} %collective-permute-done.2.f3), channel_id=1, source_target_pairs={{1,2},{2,1},{5,6},{6,5},{9,10},{10,9},{13,14},{14,13},{17,18},{18,... | collective-permute-start | bytes 294920 | tf_op jit(solution)/shard_map/ppermute | solution.py:121
  22.6 8.5 %collective-permute-start.6 = (bf16[3,96,512]{2,1,0:T(8,128)(2,1)S(1)}, bf16[3,96,512]{2,1,0:T(8,128)(2,1)S(1)}, u32[]{:S(2)}, u32[]{:S(2)}) collective-permute-start(bf16[3,96,512]{2,1,0:T(8,128)(2,1)S(1)} %pad_maximum_fusion.2), channel_id=1, source_target_pairs={{1,2},{2,1},{5,6},{6,5},{9,10},{10,9},{13,14},{14,13},{17,18},{18,... | collective-permute-start | bytes 884744 | tf_op jit(solution)/shard_map/ppermute | solution.py:121
  23.3 13.0 %collective-permute-start.11 = (bf16[3,3,32,512]{3,2,1,0:T(8,128)(2,1)S(1)}, bf16[3,3,32,512]{3,2,1,0:T(8,128)(2,1)S(1)}, u32[]{:S(2)}, u32[]{:S(2)}) collective-permute-start(bf16[3,3,32,512]{3,2,1,0:T(8,128)(2,1)S(1)} %collective-permute-done.10.w2), channel_id=1, source_target_pairs={{0,1},{1,0},{2,3},{3,2},{4,5},{5,4},{6,7},{7,6},{8,9},{9,8},{10,11... | collective-permute-start | bytes 884744 | tf_op jit(solution)/shard_map/ppermute | solution.py:112
  30.5 5.9 %copy-start.2 = (bf16[3,3,512,32]{2,3,1,0:T(8,128)(2,1)S(1)}, bf16[3,3,512,32]{2,3,1,0:T(8,128)(2,1)}, u32[]{:S(2)}) copy-start(bf16[3,3,512,32]{2,3,1,0:T(8,128)(2,1)} %param.6) | copy-start | bytes 884740
  30.5 5.9 %copy-start.3 = (s32[512]{0:T(512)S(1)}, s32[512]{0:T(512)}, u32[]{:S(2)}) copy-start(s32[512]{0:T(512)} %param.8) | copy-start | bytes 6148
  30.5 12.7 %collective-permute-start.12 = (bf16[4,304,128]{2,1,0:T(8,128)(2,1)S(1)}, bf16[4,304,128]{2,1,0:T(8,128)(2,1)S(1)}, u32[]{:S(2)}, u32[]{:S(2)}) collective-permute-start(bf16[4,304,128]{2,1,0:T(8,128)(2,1)S(1)} %pad_maximum_fusion.1), channel_id=1, source_target_pairs={{0,1},{1,0},{2,3},{3,2},{4,5},{5,4},{6,7},{7,6},{8,9},{9,8},{10,11... | collective-permute-start | bytes 933896 | tf_op jit(solution)/shard_map/ppermute | solution.py:112
  30.6 7.4 %collective-permute-start.19 = (bf16[3,304,128]{2,1,0:T(8,128)(2,1)S(1)}, bf16[3,304,128]{2,1,0:T(8,128)(2,1)S(1)}, u32[]{:S(2)}, u32[]{:S(2)}) collective-permute-start(bf16[3,304,128]{2,1,0:T(8,128)(2,1)S(1)} %collective-permute-done.17.refs_1_), channel_id=1, source_target_pairs={{0,1},{1,0},{2,3},{3,2},{4,5},{5,4},{6,7},{7,6},{8,9},{9,8},{10,11... | collective-permute-start | bytes 700424 | tf_op jit(solution)/shard_map/ppermute | solution.py:112
  31.1 7.0 %collective-permute-start.18 = (bf16[304,128]{1,0:T(8,128)(2,1)S(1)}, bf16[304,128]{1,0:T(8,128)(2,1)S(1)}, u32[]{:S(2)}, u32[]{:S(2)}) collective-permute-start(bf16[304,128]{1,0:T(8,128)(2,1)S(1)} %collective-permute-done.16.refs_0_), channel_id=1, source_target_pairs={{0,1},{1,0},{2,3},{3,2},{4,5},{5,4},{6,7},{7,6},{8,9},{9,8},{10,11... | collective-permute-start | bytes 233480 | tf_op jit(solution)/shard_map/ppermute | solution.py:112
  38.8 8.3 %collective-permute-start.20 = (bf16[2,48,256]{2,1,0:T(8,128)(2,1)S(1)}, bf16[2,48,256]{2,1,0:T(8,128)(2,1)S(1)}, u32[]{:S(2)}, u32[]{:S(2)}) collective-permute-start(bf16[2,48,256]{2,1,0:T(8,128)(2,1)S(1)} %get-tuple-element.26), channel_id=1, source_target_pairs={{0,4},{4,0},{8,12},{12,8},{1,5},{5,1},{9,13},{13,9},{2,6},{6,2},{1... | collective-permute-start | bytes 147464 | tf_op jit(solution)/shard_map/ppermute | solution.py:112
  40.0 8.4 %collective-permute-start.21 = (bf16[2,48,256]{2,1,0:T(8,128)(2,1)S(1)}, bf16[2,48,256]{2,1,0:T(8,128)(2,1)S(1)}, u32[]{:S(2)}, u32[]{:S(2)}) collective-permute-start(bf16[2,48,256]{2,1,0:T(8,128)(2,1)S(1)} %get-tuple-element.27), channel_id=1, source_target_pairs={{0,8},{4,12},{8,0},{12,4},{1,9},{5,13},{9,1},{13,5},{2,10},{6,14},... | collective-permute-start | bytes 147464 | tf_op jit(solution)/shard_map/ppermute | solution.py:112
  41.9 6.5 %collective-permute-start.22 = (bf16[2,48,256]{2,1,0:T(8,128)(2,1)S(1)}, bf16[2,48,256]{2,1,0:T(8,128)(2,1)S(1)}, u32[]{:S(2)}, u32[]{:S(2)}) collective-permute-start(bf16[2,48,256]{2,1,0:T(8,128)(2,1)S(1)} %get-tuple-element.28), channel_id=1, source_target_pairs={{0,12},{4,8},{8,4},{12,0},{1,13},{5,9},{9,5},{13,1},{2,14},{6,10},... | collective-permute-start | bytes 147464 | tf_op jit(solution)/shard_map/ppermute | solution.py:112
  44.0 4.8 %collective-permute-start.13 = (bf16[2,48,256]{2,1,0:T(8,128)(2,1)S(1)}, bf16[2,48,256]{2,1,0:T(8,128)(2,1)S(1)}, u32[]{:S(2)}, u32[]{:S(2)}) collective-permute-start(bf16[2,48,256]{2,1,0:T(8,128)(2,1)S(1)} %get-tuple-element.22), channel_id=1, source_target_pairs={{0,4},{4,0},{8,12},{12,8},{1,5},{5,1},{9,13},{13,9},{2,6},{6,2},{1... | collective-permute-start | bytes 147464 | tf_op jit(solution)/shard_map/ppermute | solution.py:112
  44.5 5.5 %collective-permute-start.14 = (bf16[2,48,256]{2,1,0:T(8,128)(2,1)S(1)}, bf16[2,48,256]{2,1,0:T(8,128)(2,1)S(1)}, u32[]{:S(2)}, u32[]{:S(2)}) collective-permute-start(bf16[2,48,256]{2,1,0:T(8,128)(2,1)S(1)} %get-tuple-element.23), channel_id=1, source_target_pairs={{0,8},{4,12},{8,0},{12,4},{1,9},{5,13},{9,1},{13,5},{2,10},{6,14},... | collective-permute-start | bytes 147464 | tf_op jit(solution)/shard_map/ppermute | solution.py:112
  47.1 5.9 %collective-permute-start.15 = (bf16[2,48,256]{2,1,0:T(8,128)(2,1)S(1)}, bf16[2,48,256]{2,1,0:T(8,128)(2,1)S(1)}, u32[]{:S(2)}, u32[]{:S(2)}) collective-permute-start(bf16[2,48,256]{2,1,0:T(8,128)(2,1)S(1)} %get-tuple-element.24), channel_id=1, source_target_pairs={{0,12},{4,8},{8,4},{12,0},{1,13},{5,9},{9,5},{13,1},{2,14},{6,10},... | collective-permute-start | bytes 147464 | tf_op jit(solution)/shard_map/ppermute | solution.py:112

commit v3 on v2

--- a/solution.py
+++ b/solution.py
@@ -200,12 +200,17 @@
             values = jnp.where(r == 0, 0.0, values)
         if row == shown - 1:
             values = jnp.where(r == last, 0.0, values)
-        hid[row] = values.astype(BF16)
+        for j in range(3):
+            moved = shifted_columns(values, j - 1, width).astype(BF16)
+            for i in range(3):
+                if 0 <= row - i < height:
+                    tap = 3 * i + j
+                    hid[row - i, :, tap * lanes : (tap + 1) * lanes] = moved
 
 
 def mix_kernel(dims, hid, *refs):
     count, height, width = dims
-    filters, (p0, p1, p2, p3, a, w, part) = refs[:-7], refs[-7:]
+    filters, (p0, p1, p2, p3, w, part) = refs[:-6], refs[-6:]
     held = []
     for ref in filters:
         held += [ref.at[e] for e in range(ref.shape[0])] if len(ref.shape) == 3 else [ref]
@@ -218,17 +223,8 @@
             for tap in range(9):
                 rows = held[4 * d + e][tap * outs : (tap + 1) * outs, :]
                 w[here, tap * lanes : (tap + 1) * lanes] = rows
-    for row in range(height + 2):
-        values = hid[row].astype(F32)
-        for j in range(3):
-            moved = shifted_columns(values, j - 1, width).astype(BF16)
-            for i in range(3):
-                out_row = row - i
-                if 0 <= out_row < height:
-                    tap = 3 * i + j
-                    a[out_row, :, tap * lanes : (tap + 1) * lanes] = moved
-    for row in range(height):
-        part[row] = dot_nt(a[row], w[...])
+    slab = hid.shape[1]
+    part[...] = dot_nt(hid[...].reshape(height * slab, hid.shape[2]), w[...]).reshape(part.shape)
     blocks = count * width
     for d, out in enumerate((p0, p1, p2, p3)):
         here = pl.ds(pl.multiple_of((z ^ d) * blocks, blocks), blocks)
@@ -301,7 +297,7 @@
     slab = total * width
     hidden = call(
         functools.partial(drive_kernel, (count, height, width, total)),
-        shape((height + 2, slab, lanes), BF16),
+        shape((height, slab, 9 * lanes), BF16),
         [
             pltpu.VMEM((3 * height, slab, channels), BF16),
             pltpu.VMEM((3, 3, 4, w_in.shape[3], channels), BF16),
@@ -335,7 +331,6 @@
             functools.partial(mix_kernel, (count, height, width)),
             (part(F32), part(BF16), part(BF16), part(BF16)),
             [
-                pltpu.VMEM((height, slab, 9 * lanes), BF16),
                 pltpu.VMEM((half, 9 * lanes), BF16),
                 pltpu.VMEM((height, slab, half), F32),
             ],

time: 53.9 us -> 53.8 us (level)
  transfers between devices with their start and end apart: 23 -> 23, of which waited for: 6 -> 7; matrix products, arithmetic and copies ran while one was open for 0% -> 0% of each run, Pallas kernels for 6% -> 6%
where the time goes in v3:
time: 53.8 us; the launch traced here: 53.7 us
  starting transfers between devices  37.6 us (70%)
  waiting for transfers between devices  10.9 us (20%)
  Pallas kernels  3.86 us (7%)
  local copies, waits for them, and re-layouts  1.06 us (2%)
    ppermute x21, starting transfers between devices, swapped(): return lax.ppermute(array, axis, [(i, i ^ distance) for i in range(size)])  36.2 us
    ppermute x21, waiting for transfers between devices, swapped(): return lax.ppermute(array, axis, [(i, i ^ distance) for i in range(size)])  10.9 us
    pallas_call x5, Pallas kernels, call(): pl.pallas_call(kernel, out_shape=outs, in_specs=specs or [VMEM] * len(arg...  3.86 us
    ppermute x2, starting transfers between devices, across(): return lax.ppermute(array, 'row', pairs + [(j, i) for i, j in pairs])  1.35 us
  transfers between devices with their start and end apart: 23, of which 7 were waited for; matrix products, arithmetic and copies ran while one was open for 0% of the time, Pallas kernels for 6%

profile of v3, /device:TPU:0, one launch (start us, length us, event | category | flops | bytes accessed | tf_op | source)
XLA Modules:
  0.0 53.7 jit_solution(6383028743741576055)
XLA Ops:
  0.0 4.1 %collective-permute-start.1 = (bf16[96,512]{1,0:T(8,128)(2,1)}, bf16[96,512]{1,0:T(8,128)(2,1)S(1)}, u32[]{:S(2)}, u32[]{:S(2)}) collective-permute-start(bf16[96,512]{1,0:T(8,128)(2,1)} %bitcast.18), channel_id=1, source_target_pairs={{0,8},{4,12},{8,0},{12,4},{1,9},{5,13},{9,1},{13,5},{2,10},{6,14},... | collective-permute-start | bytes 294920 | tf_op jit(solution)/shard_map/ppermute | solution.py:112
  4.2 1.0 %copy-done.2 = bf16[3,3,512,32]{2,3,1,0:T(8,128)(2,1)S(1)} copy-done((bf16[3,3,512,32]{2,3,1,0:T(8,128)(2,1)S(1)}, bf16[3,3,512,32]{2,3,1,0:T(8,128)(2,1)}, u32[]{:S(2)}) %copy-start.2) | copy-done | bytes 294936
  5.2 1.6 %collective-permute-start.3 = (bf16[304,128]{1,0:T(8,128)(2,1)S(1)}, bf16[304,128]{1,0:T(8,128)(2,1)S(1)}, u32[]{:S(2)}, u32[]{:S(2)}) collective-permute-start(bf16[304,128]{1,0:T(8,128)(2,1)S(1)} %get-tuple-element.18), channel_id=1, source_target_pairs={{0,4},{4,0},{8,12},{12,8},{1,5},{5,1},{9,13},{13,9},{2,6},{6,2},{1... | collective-permute-start | bytes 233480 | tf_op jit(solution)/shard_map/ppermute | solution.py:112
  6.8 0.7 %collective-permute-start.4 = (bf16[304,128]{1,0:T(8,128)(2,1)S(1)}, bf16[304,128]{1,0:T(8,128)(2,1)S(1)}, u32[]{:S(2)}, u32[]{:S(2)}) collective-permute-start(bf16[304,128]{1,0:T(8,128)(2,1)S(1)} %get-tuple-element.19), channel_id=1, source_target_pairs={{0,8},{4,12},{8,0},{12,4},{1,9},{5,13},{9,1},{13,5},{2,10},{6,14},... | collective-permute-start | bytes 233480 | tf_op jit(solution)/shard_map/ppermute | solution.py:112
  7.5 2.2 %collective-permute-start.5 = (bf16[304,128]{1,0:T(8,128)(2,1)S(1)}, bf16[304,128]{1,0:T(8,128)(2,1)S(1)}, u32[]{:S(2)}, u32[]{:S(2)}) collective-permute-start(bf16[304,128]{1,0:T(8,128)(2,1)S(1)} %get-tuple-element.20), channel_id=1, source_target_pairs={{0,12},{4,8},{8,4},{12,0},{1,13},{5,9},{9,5},{13,1},{2,14},{6,10},... | collective-permute-start | bytes 233480 | tf_op jit(solution)/shard_map/ppermute | solution.py:112
  9.6 0.7 %collective-permute-start = (bf16[96,512]{1,0:T(8,128)(2,1)S(1)}, bf16[96,512]{1,0:T(8,128)(2,1)S(1)}, u32[]{:S(2)}, u32[]{:S(2)}) collective-permute-start(bf16[96,512]{1,0:T(8,128)(2,1)S(1)} %bitcast.19), channel_id=1, source_target_pairs={{0,4},{4,0},{8,12},{12,8},{1,5},{5,1},{9,13},{13,9},{2,6},{6,2},{1... | collective-permute-start | bytes 294920 | tf_op jit(solution)/shard_map/ppermute | solution.py:112
  10.3 0.1 collective-permute-done.3.m1.refs_1_
  10.5 1.5 %collective-permute-start.10 = (bf16[3,3,32,512]{3,2,1,0:T(8,128)(2,1)}, bf16[3,3,32,512]{3,2,1,0:T(8,128)(2,1)S(1)}, u32[]{:S(2)}, u32[]{:S(2)}) collective-permute-start(bf16[3,3,32,512]{3,2,1,0:T(8,128)(2,1)} %bitcast.29), channel_id=1, source_target_pairs={{0,2},{1,3},{2,0},{3,1},{4,6},{5,7},{6,4},{7,5},{8,10},{9,11},{10,... | collective-permute-start | bytes 884744 | tf_op jit(solution)/shard_map/ppermute | solution.py:112
  12.0 3.3 %collective-permute-done.4.m2.refs_2_ = bf16[304,128]{1,0:T(8,128)(2,1)S(1)} collective-permute-done((bf16[304,128]{1,0:T(8,128)(2,1)S(1)}, bf16[304,128]{1,0:T(8,128)(2,1)S(1)}, u32[]{:S(2)}, u32[]{:S(2)}) %collective-permute-start.4) | collective-permute-done | bytes 77856 | tf_op jit(solution)/shard_map/ppermute | solution.py:112
  15.3 1.5 %collective-permute-start.16 = (bf16[304,128]{1,0:T(8,128)(2,1)S(1)}, bf16[304,128]{1,0:T(8,128)(2,1)S(1)}, u32[]{:S(2)}, u32[]{:S(2)}) collective-permute-start(bf16[304,128]{1,0:T(8,128)(2,1)S(1)} %get-tuple-element.17.m0.refs_0_), channel_id=1, source_target_pairs={{0,2},{1,3},{2,0},{3,1},{4,6},{5,7},{6,4},{7,5},{8,10},{9,11},{10,... | collective-permute-start | bytes 233480 | tf_op jit(solution)/shard_map/ppermute | solution.py:112
  16.8 1.5 %collective-permute-start.2 = (bf16[96,512]{1,0:T(8,128)(2,1)S(1)}, bf16[96,512]{1,0:T(8,128)(2,1)S(1)}, u32[]{:S(2)}, u32[]{:S(2)}) collective-permute-start(bf16[96,512]{1,0:T(8,128)(2,1)S(1)} %collective-permute-done.1.f2), channel_id=1, source_target_pairs={{0,4},{4,0},{8,12},{12,8},{1,5},{5,1},{9,13},{13,9},{2,6},{6,2},{1... | collective-permute-start | bytes 294920 | tf_op jit(solution)/shard_map/ppermute | solution.py:112
  18.3 0.6 %collective-permute-start.17 = (bf16[3,304,128]{2,1,0:T(8,128)(2,1)S(1)}, bf16[3,304,128]{2,1,0:T(8,128)(2,1)S(1)}, u32[]{:S(2)}, u32[]{:S(2)}) collective-permute-start(bf16[3,304,128]{2,1,0:T(8,128)(2,1)S(1)} %pad_maximum_fusion.3), channel_id=1, source_target_pairs={{0,2},{1,3},{2,0},{3,1},{4,6},{5,7},{6,4},{7,5},{8,10},{9,11},{10,... | collective-permute-start | bytes 700424 | tf_op jit(solution)/shard_map/ppermute | solution.py:112
  18.9 2.8 %collective-permute-done.2.f3 = bf16[96,512]{1,0:T(8,128)(2,1)S(1)} collective-permute-done((bf16[96,512]{1,0:T(8,128)(2,1)S(1)}, bf16[96,512]{1,0:T(8,128)(2,1)S(1)}, u32[]{:S(2)}, u32[]{:S(2)}) %collective-permute-start.2) | collective-permute-done | bytes 98336 | tf_op jit(solution)/shard_map/ppermute | solution.py:112
  21.9 0.7 %collective-permute-start.7 = (bf16[96,512]{1,0:T(8,128)(2,1)S(1)}, bf16[96,512]{1,0:T(8,128)(2,1)S(1)}, u32[]{:S(2)}, u32[]{:S(2)}) collective-permute-start(bf16[96,512]{1,0:T(8,128)(2,1)S(1)} %collective-permute-done.2.f3), channel_id=1, source_target_pairs={{1,2},{2,1},{5,6},{6,5},{9,10},{10,9},{13,14},{14,13},{17,18},{18,... | collective-permute-start | bytes 294920 | tf_op jit(solution)/shard_map/ppermute | solution.py:121
  22.6 0.7 %collective-permute-start.6 = (bf16[3,96,512]{2,1,0:T(8,128)(2,1)S(1)}, bf16[3,96,512]{2,1,0:T(8,128)(2,1)S(1)}, u32[]{:S(2)}, u32[]{:S(2)}) collective-permute-start(bf16[3,96,512]{2,1,0:T(8,128)(2,1)S(1)} %pad_maximum_fusion.2), channel_id=1, source_target_pairs={{1,2},{2,1},{5,6},{6,5},{9,10},{10,9},{13,14},{14,13},{17,18},{18,... | collective-permute-start | bytes 884744 | tf_op jit(solution)/shard_map/ppermute | solution.py:121
  23.3 7.1 %collective-permute-start.11 = (bf16[3,3,32,512]{3,2,1,0:T(8,128)(2,1)S(1)}, bf16[3,3,32,512]{3,2,1,0:T(8,128)(2,1)S(1)}, u32[]{:S(2)}, u32[]{:S(2)}) collective-permute-start(bf16[3,3,32,512]{3,2,1,0:T(8,128)(2,1)S(1)} %collective-permute-done.10.w2), channel_id=1, source_target_pairs={{0,1},{1,0},{2,3},{3,2},{4,5},{5,4},{6,7},{7,6},{8,9},{9,8},{10,11... | collective-permute-start | bytes 884744 | tf_op jit(solution)/shard_map/ppermute | solution.py:112
  30.5 0.1 collective-permute-start.12
  30.6 0.5 collective-permute-start.19
  31.1 5.2 %collective-permute-start.18 = (bf16[304,128]{1,0:T(8,128)(2,1)S(1)}, bf16[304,128]{1,0:T(8,128)(2,1)S(1)}, u32[]{:S(2)}, u32[]{:S(2)}) collective-permute-start(bf16[304,128]{1,0:T(8,128)(2,1)S(1)} %collective-permute-done.16.refs_0_), channel_id=1, source_target_pairs={{0,1},{1,0},{2,3},{3,2},{4,5},{5,4},{6,7},{7,6},{8,9},{9,8},{10,11... | collective-permute-start | bytes 233480 | tf_op jit(solution)/shard_map/ppermute | solution.py:112
  36.4 1.8 %shard_map.56.hid = bf16[2,192,1152]{2,1,0:T(8,128)(2,1)S(1)} custom-call(bf16[96,512]{1,0:T(8,128)(2,1)S(1)} %bitcast.22, bf16[96,512]{1,0:T(8,128)(2,1)S(1)} %collective-permute-done.f1, bf16[96,512]{1,0:T(8,128)(2,1)S(1)} %collective-permute-done.1.f2, bf16[96,512]{1,0:T(8,128)(2,1)S(1)} %collective-permute-done.2.f3, ...), custom_call_target="tpu_custom_call" | custom-call | flops 905969664 | bytes 2672640 | tf_op jit(solution)/shard_map/pallas_call | solution.py:253
  38.2 0.6 %shard_map.58 = (f32[2,48,256]{2,1,0:T(8,128)S(1)}, bf16[2,48,256]{2,1,0:T(8,128)(2,1)S(1)}, bf16[2,48,256]{2,1,0:T(8,128)(2,1)S(1)}, bf16[2,48,256]{2,1,0:T(8,128)(2,1)S(1)}) custom-call(bf16[2,192,1152]{2,1,0:T(8,128)(2,1)S(1)} %shard_map.56.hid, bf16[304,128]{1,0:T(8,128)(2,1)S(1)} %collective-permute-done.16.refs_0_, ...), custom_call_target="tpu_custom_call" | custom-call | flops 226492416 | bytes 1507328 | tf_op jit(solution)/shard_map/pallas_call | solution.py:253
  38.8 1.2 %collective-permute-start.20 = (bf16[2,48,256]{2,1,0:T(8,128)(2,1)S(1)}, bf16[2,48,256]{2,1,0:T(8,128)(2,1)S(1)}, u32[]{:S(2)}, u32[]{:S(2)}) collective-permute-start(bf16[2,48,256]{2,1,0:T(8,128)(2,1)S(1)} %get-tuple-element.26), channel_id=1, source_target_pairs={{0,4},{4,0},{8,12},{12,8},{1,5},{5,1},{9,13},{13,9},{2,6},{6,2},{1... | collective-permute-start | bytes 147464 | tf_op jit(solution)/shard_map/ppermute | solution.py:112
  40.0 1.9 %collective-permute-start.21 = (bf16[2,48,256]{2,1,0:T(8,128)(2,1)S(1)}, bf16[2,48,256]{2,1,0:T(8,128)(2,1)S(1)}, u32[]{:S(2)}, u32[]{:S(2)}) collective-permute-start(bf16[2,48,256]{2,1,0:T(8,128)(2,1)S(1)} %get-tuple-element.27), channel_id=1, source_target_pairs={{0,8},{4,12},{8,0},{12,4},{1,9},{5,13},{9,1},{13,5},{2,10},{6,14},... | collective-permute-start | bytes 147464 | tf_op jit(solution)/shard_map/ppermute | solution.py:112
  42.0 1.3 %collective-permute-start.22 = (bf16[2,48,256]{2,1,0:T(8,128)(2,1)S(1)}, bf16[2,48,256]{2,1,0:T(8,128)(2,1)S(1)}, u32[]{:S(2)}, u32[]{:S(2)}) collective-permute-start(bf16[2,48,256]{2,1,0:T(8,128)(2,1)S(1)} %get-tuple-element.28), channel_id=1, source_target_pairs={{0,12},{4,8},{8,4},{12,0},{1,13},{5,9},{9,5},{13,1},{2,14},{6,10},... | collective-permute-start | bytes 147464 | tf_op jit(solution)/shard_map/ppermute | solution.py:112
  43.3 0.6 %shard_map.57 = (f32[2,48,256]{2,1,0:T(8,128)S(1)}, bf16[2,48,256]{2,1,0:T(8,128)(2,1)S(1)}, bf16[2,48,256]{2,1,0:T(8,128)(2,1)S(1)}, bf16[2,48,256]{2,1,0:T(8,128)(2,1)S(1)}) custom-call(bf16[2,192,1152]{2,1,0:T(8,128)(2,1)S(1)} %shard_map.56.hid, bf16[304,128]{1,0:T(8,128)(2,1)S(1)} %get-tuple-element.17.m0.refs_0_, ...), custom_call_target="tpu_custom_call" | custom-call | flops 226492416 | bytes 1507328 | tf_op jit(solution)/shard_map/pallas_call | solution.py:253
  43.9 0.6 %collective-permute-start.13 = (bf16[2,48,256]{2,1,0:T(8,128)(2,1)S(1)}, bf16[2,48,256]{2,1,0:T(8,128)(2,1)S(1)}, u32[]{:S(2)}, u32[]{:S(2)}) collective-permute-start(bf16[2,48,256]{2,1,0:T(8,128)(2,1)S(1)} %get-tuple-element.22), channel_id=1, source_target_pairs={{0,4},{4,0},{8,12},{12,8},{1,5},{5,1},{9,13},{13,9},{2,6},{6,2},{1... | collective-permute-start | bytes 147464 | tf_op jit(solution)/shard_map/ppermute | solution.py:112
  44.4 2.6 %collective-permute-start.14 = (bf16[2,48,256]{2,1,0:T(8,128)(2,1)S(1)}, bf16[2,48,256]{2,1,0:T(8,128)(2,1)S(1)}, u32[]{:S(2)}, u32[]{:S(2)}) collective-permute-start(bf16[2,48,256]{2,1,0:T(8,128)(2,1)S(1)} %get-tuple-element.23), channel_id=1, source_target_pairs={{0,8},{4,12},{8,0},{12,4},{1,9},{5,13},{9,1},{13,5},{2,10},{6,14},... | collective-permute-start | bytes 147464 | tf_op jit(solution)/shard_map/ppermute | solution.py:112
  47.0 1.3 %collective-permute-start.15 = (bf16[2,48,256]{2,1,0:T(8,128)(2,1)S(1)}, bf16[2,48,256]{2,1,0:T(8,128)(2,1)S(1)}, u32[]{:S(2)}, u32[]{:S(2)}) collective-permute-start(bf16[2,48,256]{2,1,0:T(8,128)(2,1)S(1)} %get-tuple-element.24), channel_id=1, source_target_pairs={{0,12},{4,8},{8,4},{12,0},{1,13},{5,9},{9,5},{13,1},{2,14},{6,10},... | collective-permute-start | bytes 147464 | tf_op jit(solution)/shard_map/ppermute | solution.py:112
  48.4 0.2 collective-permute-done.13.a1
  48.6 1.3 %collective-permute-done.14.a2 = bf16[2,48,256]{2,1,0:T(8,128)(2,1)S(1)} collective-permute-done((bf16[2,48,256]{2,1,0:T(8,128)(2,1)S(1)}, bf16[2,48,256]{2,1,0:T(8,128)(2,1)S(1)}, u32[]{:S(2)}, u32[]{:S(2)}) %collective-permute-start.14) | collective-permute-done | bytes 49184 | tf_op jit(solution)/shard_map/ppermute | solution.py:112
  50.0 2.9 %collective-permute-done.15.a3 = bf16[2,48,256]{2,1,0:T(8,128)(2,1)S(1)} collective-permute-done((bf16[2,48,256]{2,1,0:T(8,128)(2,1)S(1)}, bf16[2,48,256]{2,1,0:T(8,128)(2,1)S(1)}, u32[]{:S(2)}, u32[]{:S(2)}) %collective-permute-start.15) | collective-permute-done | bytes 49184 | tf_op jit(solution)/shard_map/ppermute | solution.py:112
  52.9 0.8 %shard_map.59 = bf16[2,2,24,512]{3,2,1,0:T(8,128)(2,1)} custom-call(f32[2,48,256]{2,1,0:T(8,128)S(1)} %get-tuple-element.21.a0, bf16[2,48,256]{2,1,0:T(8,128)(2,1)S(1)} %collective-permute-done.13.a1, bf16[2,48,256]{2,1,0:T(8,128)(2,1)S(1)} %collective-permute-done.14.a2, bf16[2,48,256]{2,1,0:T(8,128)(2,1)S(1)} %collective-permute-done.15.a3, ...), custom_call_target="tpu_custom_call" | custom-call | bytes 491520 | tf_op jit(solution)/shard_map/pallas_call | solution.py:253
  (36 shorter events, 0.5 us)
Async XLA Ops:
  0.0 4.1 %copy-start.4 = (s32[2]{0:T(128)S(1)}, s32[2]{0:T(128)}, u32[]{:S(2)}) copy-start(s32[2]{0:T(128)} %param.9) | copy-start | bytes 28
  0.0 16.8 %collective-permute-start.1 = (bf16[96,512]{1,0:T(8,128)(2,1)}, bf16[96,512]{1,0:T(8,128)(2,1)S(1)}, u32[]{:S(2)}, u32[]{:S(2)}) collective-permute-start(bf16[96,512]{1,0:T(8,128)(2,1)} %bitcast.18), channel_id=1, source_target_pairs={{0,8},{4,12},{8,0},{12,4},{1,9},{5,13},{9,1},{13,5},{2,10},{6,14},... | collective-permute-start | bytes 294920 | tf_op jit(solution)/shard_map/ppermute | solution.py:112
  4.2 1.0 %copy-start.2 = (bf16[3,3,512,32]{2,3,1,0:T(8,128)(2,1)S(1)}, bf16[3,3,512,32]{2,3,1,0:T(8,128)(2,1)}, u32[]{:S(2)}) copy-start(bf16[3,3,512,32]{2,3,1,0:T(8,128)(2,1)} %param.7) | copy-start | bytes 884740
  5.1 4.5 %copy-start = (bf16[2,2,24,512]{3,2,1,0:T(8,128)(2,1)S(1)}, bf16[2,2,24,512]{3,2,1,0:T(8,128)(2,1)}, u32[]{:S(2)}) copy-start(bf16[2,2,24,512]{3,2,1,0:T(8,128)(2,1)} %param.5) | copy-start | bytes 294916
  5.2 5.3 %collective-permute-start.3 = (bf16[304,128]{1,0:T(8,128)(2,1)S(1)}, bf16[304,128]{1,0:T(8,128)(2,1)S(1)}, u32[]{:S(2)}, u32[]{:S(2)}) collective-permute-start(bf16[304,128]{1,0:T(8,128)(2,1)S(1)} %get-tuple-element.18), channel_id=1, source_target_pairs={{0,4},{4,0},{8,12},{12,8},{1,5},{5,1},{9,13},{13,9},{2,6},{6,2},{1... | collective-permute-start | bytes 233480 | tf_op jit(solution)/shard_map/ppermute | solution.py:112
  6.8 8.5 %collective-permute-start.4 = (bf16[304,128]{1,0:T(8,128)(2,1)S(1)}, bf16[304,128]{1,0:T(8,128)(2,1)S(1)}, u32[]{:S(2)}, u32[]{:S(2)}) collective-permute-start(bf16[304,128]{1,0:T(8,128)(2,1)S(1)} %get-tuple-element.19), channel_id=1, source_target_pairs={{0,8},{4,12},{8,0},{12,4},{1,9},{5,13},{9,1},{13,5},{2,10},{6,14},... | collective-permute-start | bytes 233480 | tf_op jit(solution)/shard_map/ppermute | solution.py:112
  7.5 7.8 %collective-permute-start.5 = (bf16[304,128]{1,0:T(8,128)(2,1)S(1)}, bf16[304,128]{1,0:T(8,128)(2,1)S(1)}, u32[]{:S(2)}, u32[]{:S(2)}) collective-permute-start(bf16[304,128]{1,0:T(8,128)(2,1)S(1)} %get-tuple-element.20), channel_id=1, source_target_pairs={{0,12},{4,8},{8,4},{12,0},{1,13},{5,9},{9,5},{13,1},{2,14},{6,10},... | collective-permute-start | bytes 233480 | tf_op jit(solution)/shard_map/ppermute | solution.py:112
  9.6 8.7 %collective-permute-start = (bf16[96,512]{1,0:T(8,128)(2,1)S(1)}, bf16[96,512]{1,0:T(8,128)(2,1)S(1)}, u32[]{:S(2)}, u32[]{:S(2)}) collective-permute-start(bf16[96,512]{1,0:T(8,128)(2,1)S(1)} %bitcast.19), channel_id=1, source_target_pairs={{0,4},{4,0},{8,12},{12,8},{1,5},{5,1},{9,13},{13,9},{2,6},{6,2},{1... | collective-permute-start | bytes 294920 | tf_op jit(solution)/shard_map/ppermute | solution.py:112
  10.5 12.8 %collective-permute-start.10 = (bf16[3,3,32,512]{3,2,1,0:T(8,128)(2,1)}, bf16[3,3,32,512]{3,2,1,0:T(8,128)(2,1)S(1)}, u32[]{:S(2)}, u32[]{:S(2)}) collective-permute-start(bf16[3,3,32,512]{3,2,1,0:T(8,128)(2,1)} %bitcast.29), channel_id=1, source_target_pairs={{0,2},{1,3},{2,0},{3,1},{4,6},{5,7},{6,4},{7,5},{8,10},{9,11},{10,... | collective-permute-start | bytes 884744 | tf_op jit(solution)/shard_map/ppermute | solution.py:112
  15.3 15.2 %collective-permute-start.9 = (bf16[3,3,32,512]{3,2,1,0:T(8,128)(2,1)}, bf16[3,3,32,512]{3,2,1,0:T(8,128)(2,1)S(1)}, u32[]{:S(2)}, u32[]{:S(2)}) collective-permute-start(bf16[3,3,32,512]{3,2,1,0:T(8,128)(2,1)} %bitcast.30), channel_id=1, source_target_pairs={{0,1},{1,0},{2,3},{3,2},{4,5},{5,4},{6,7},{7,6},{8,9},{9,8},{10,11... | collective-permute-start | bytes 884744 | tf_op jit(solution)/shard_map/ppermute | solution.py:112
  15.3 6.6 %collective-permute-start.16 = (bf16[304,128]{1,0:T(8,128)(2,1)S(1)}, bf16[304,128]{1,0:T(8,128)(2,1)S(1)}, u32[]{:S(2)}, u32[]{:S(2)}) collective-permute-start(bf16[304,128]{1,0:T(8,128)(2,1)S(1)} %get-tuple-element.17.m0.refs_0_), channel_id=1, source_target_pairs={{0,2},{1,3},{2,0},{3,1},{4,6},{5,7},{6,4},{7,5},{8,10},{9,11},{10,... | collective-permute-start | bytes 233480 | tf_op jit(solution)/shard_map/ppermute | solution.py:112
  16.8 4.9 %collective-permute-start.2 = (bf16[96,512]{1,0:T(8,128)(2,1)S(1)}, bf16[96,512]{1,0:T(8,128)(2,1)S(1)}, u32[]{:S(2)}, u32[]{:S(2)}) collective-permute-start(bf16[96,512]{1,0:T(8,128)(2,1)S(1)} %collective-permute-done.1.f2), channel_id=1, source_target_pairs={{0,4},{4,0},{8,12},{12,8},{1,5},{5,1},{9,13},{13,9},{2,6},{6,2},{1... | collective-permute-start | bytes 294920 | tf_op jit(solution)/shard_map/ppermute | solution.py:112
  18.3 12.3 %collective-permute-start.17 = (bf16[3,304,128]{2,1,0:T(8,128)(2,1)S(1)}, bf16[3,304,128]{2,1,0:T(8,128)(2,1)S(1)}, u32[]{:S(2)}, u32[]{:S(2)}) collective-permute-start(bf16[3,304,128]{2,1,0:T(8,128)(2,1)S(1)} %pad_maximum_fusion.3), channel_id=1, source_target_pairs={{0,2},{1,3},{2,0},{3,1},{4,6},{5,7},{6,4},{7,5},{8,10},{9,11},{10,... | collective-permute-start | bytes 700424 | tf_op jit(solution)/shard_map/ppermute | solution.py:112
  21.8 14.5 %collective-permute-start.8 = (bf16[4,96,512]{2,1,0:T(8,128)(2,1)S(1)}, bf16[4,96,512]{2,1,0:T(8,128)(2,1)S(1)}, u32[]{:S(2)}, u32[]{:S(2)}) collective-permute-start(bf16[4,96,512]{2,1,0:T(8,128)(2,1)S(1)} %pad_maximum_fusion), channel_id=1, source_target_pairs={{0,1},{1,0},{2,3},{3,2},{4,5},{5,4},{6,7},{7,6},{8,9},{9,8},{10,11... | collective-permute-start | bytes 1179656 | tf_op jit(solution)/shard_map/ppermute | solution.py:112
  21.9 0.7 %collective-permute-start.7 = (bf16[96,512]{1,0:T(8,128)(2,1)S(1)}, bf16[96,512]{1,0:T(8,128)(2,1)S(1)}, u32[]{:S(2)}, u32[]{:S(2)}) collective-permute-start(bf16[96,512]{1,0:T(8,128)(2,1)S(1)} %collective-permute-done.2.f3), channel_id=1, source_target_pairs={{1,2},{2,1},{5,6},{6,5},{9,10},{10,9},{13,14},{14,13},{17,18},{18,... | collective-permute-start | bytes 294920 | tf_op jit(solution)/shard_map/ppermute | solution.py:121
  22.6 8.5 %collective-permute-start.6 = (bf16[3,96,512]{2,1,0:T(8,128)(2,1)S(1)}, bf16[3,96,512]{2,1,0:T(8,128)(2,1)S(1)}, u32[]{:S(2)}, u32[]{:S(2)}) collective-permute-start(bf16[3,96,512]{2,1,0:T(8,128)(2,1)S(1)} %pad_maximum_fusion.2), channel_id=1, source_target_pairs={{1,2},{2,1},{5,6},{6,5},{9,10},{10,9},{13,14},{14,13},{17,18},{18,... | collective-permute-start | bytes 884744 | tf_op jit(solution)/shard_map/ppermute | solution.py:121
  23.3 13.0 %collective-permute-start.11 = (bf16[3,3,32,512]{3,2,1,0:T(8,128)(2,1)S(1)}, bf16[3,3,32,512]{3,2,1,0:T(8,128)(2,1)S(1)}, u32[]{:S(2)}, u32[]{:S(2)}) collective-permute-start(bf16[3,3,32,512]{3,2,1,0:T(8,128)(2,1)S(1)} %collective-permute-done.10.w2), channel_id=1, source_target_pairs={{0,1},{1,0},{2,3},{3,2},{4,5},{5,4},{6,7},{7,6},{8,9},{9,8},{10,11... | collective-permute-start | bytes 884744 | tf_op jit(solution)/shard_map/ppermute | solution.py:112
  30.5 5.9 %copy-start.1 = (bf16[3,3,512,32]{2,3,1,0:T(8,128)(2,1)S(1)}, bf16[3,3,512,32]{2,3,1,0:T(8,128)(2,1)}, u32[]{:S(2)}) copy-start(bf16[3,3,512,32]{2,3,1,0:T(8,128)(2,1)} %param.6) | copy-start | bytes 884740
  30.5 5.9 %copy-start.3 = (s32[512]{0:T(512)S(1)}, s32[512]{0:T(512)}, u32[]{:S(2)}) copy-start(s32[512]{0:T(512)} %param.8) | copy-start | bytes 6148
  30.5 12.8 %collective-permute-start.12 = (bf16[4,304,128]{2,1,0:T(8,128)(2,1)S(1)}, bf16[4,304,128]{2,1,0:T(8,128)(2,1)S(1)}, u32[]{:S(2)}, u32[]{:S(2)}) collective-permute-start(bf16[4,304,128]{2,1,0:T(8,128)(2,1)S(1)} %pad_maximum_fusion.1), channel_id=1, source_target_pairs={{0,1},{1,0},{2,3},{3,2},{4,5},{5,4},{6,7},{7,6},{8,9},{9,8},{10,11... | collective-permute-start | bytes 933896 | tf_op jit(solution)/shard_map/ppermute | solution.py:112
  30.6 7.6 %collective-permute-start.19 = (bf16[3,304,128]{2,1,0:T(8,128)(2,1)S(1)}, bf16[3,304,128]{2,1,0:T(8,128)(2,1)S(1)}, u32[]{:S(2)}, u32[]{:S(2)}) collective-permute-start(bf16[3,304,128]{2,1,0:T(8,128)(2,1)S(1)} %collective-permute-done.17.refs_1_), channel_id=1, source_target_pairs={{0,1},{1,0},{2,3},{3,2},{4,5},{5,4},{6,7},{7,6},{8,9},{9,8},{10,11... | collective-permute-start | bytes 700424 | tf_op jit(solution)/shard_map/ppermute | solution.py:112
  31.1 7.1 %collective-permute-start.18 = (bf16[304,128]{1,0:T(8,128)(2,1)S(1)}, bf16[304,128]{1,0:T(8,128)(2,1)S(1)}, u32[]{:S(2)}, u32[]{:S(2)}) collective-permute-start(bf16[304,128]{1,0:T(8,128)(2,1)S(1)} %collective-permute-done.16.refs_0_), channel_id=1, source_target_pairs={{0,1},{1,0},{2,3},{3,2},{4,5},{5,4},{6,7},{7,6},{8,9},{9,8},{10,11... | collective-permute-start | bytes 233480 | tf_op jit(solution)/shard_map/ppermute | solution.py:112
  38.8 8.2 %collective-permute-start.20 = (bf16[2,48,256]{2,1,0:T(8,128)(2,1)S(1)}, bf16[2,48,256]{2,1,0:T(8,128)(2,1)S(1)}, u32[]{:S(2)}, u32[]{:S(2)}) collective-permute-start(bf16[2,48,256]{2,1,0:T(8,128)(2,1)S(1)} %get-tuple-element.26), channel_id=1, source_target_pairs={{0,4},{4,0},{8,12},{12,8},{1,5},{5,1},{9,13},{13,9},{2,6},{6,2},{1... | collective-permute-start | bytes 147464 | tf_op jit(solution)/shard_map/ppermute | solution.py:112
  40.0 8.3 %collective-permute-start.21 = (bf16[2,48,256]{2,1,0:T(8,128)(2,1)S(1)}, bf16[2,48,256]{2,1,0:T(8,128)(2,1)S(1)}, u32[]{:S(2)}, u32[]{:S(2)}) collective-permute-start(bf16[2,48,256]{2,1,0:T(8,128)(2,1)S(1)} %get-tuple-element.27), channel_id=1, source_target_pairs={{0,8},{4,12},{8,0},{12,4},{1,9},{5,13},{9,1},{13,5},{2,10},{6,14},... | collective-permute-start | bytes 147464 | tf_op jit(solution)/shard_map/ppermute | solution.py:112
  42.0 6.4 %collective-permute-start.22 = (bf16[2,48,256]{2,1,0:T(8,128)(2,1)S(1)}, bf16[2,48,256]{2,1,0:T(8,128)(2,1)S(1)}, u32[]{:S(2)}, u32[]{:S(2)}) collective-permute-start(bf16[2,48,256]{2,1,0:T(8,128)(2,1)S(1)} %get-tuple-element.28), channel_id=1, source_target_pairs={{0,12},{4,8},{8,4},{12,0},{1,13},{5,9},{9,5},{13,1},{2,14},{6,10},... | collective-permute-start | bytes 147464 | tf_op jit(solution)/shard_map/ppermute | solution.py:112
  43.9 4.7 %collective-permute-start.13 = (bf16[2,48,256]{2,1,0:T(8,128)(2,1)S(1)}, bf16[2,48,256]{2,1,0:T(8,128)(2,1)S(1)}, u32[]{:S(2)}, u32[]{:S(2)}) collective-permute-start(bf16[2,48,256]{2,1,0:T(8,128)(2,1)S(1)} %get-tuple-element.22), channel_id=1, source_target_pairs={{0,4},{4,0},{8,12},{12,8},{1,5},{5,1},{9,13},{13,9},{2,6},{6,2},{1... | collective-permute-start | bytes 147464 | tf_op jit(solution)/shard_map/ppermute | solution.py:112
  44.4 5.5 %collective-permute-start.14 = (bf16[2,48,256]{2,1,0:T(8,128)(2,1)S(1)}, bf16[2,48,256]{2,1,0:T(8,128)(2,1)S(1)}, u32[]{:S(2)}, u32[]{:S(2)}) collective-permute-start(bf16[2,48,256]{2,1,0:T(8,128)(2,1)S(1)} %get-tuple-element.23), channel_id=1, source_target_pairs={{0,8},{4,12},{8,0},{12,4},{1,9},{5,13},{9,1},{13,5},{2,10},{6,14},... | collective-permute-start | bytes 147464 | tf_op jit(solution)/shard_map/ppermute | solution.py:112
  47.0 5.9 %collective-permute-start.15 = (bf16[2,48,256]{2,1,0:T(8,128)(2,1)S(1)}, bf16[2,48,256]{2,1,0:T(8,128)(2,1)S(1)}, u32[]{:S(2)}, u32[]{:S(2)}) collective-permute-start(bf16[2,48,256]{2,1,0:T(8,128)(2,1)S(1)} %get-tuple-element.24), channel_id=1, source_target_pairs={{0,12},{4,8},{8,4},{12,0},{1,13},{5,9},{9,5},{13,1},{2,14},{6,10},... | collective-permute-start | bytes 147464 | tf_op jit(solution)/shard_map/ppermute | solution.py:112

commit v4 on v3

--- a/solution.py
+++ b/solution.py
@@ -232,8 +232,12 @@
             out[row] = part[row, here, :].astype(out.dtype)
 
 
-def sum_kernel(width, a0, a1, a2, a3, b0, b1, b2, b3, out):
-    near = a0[...] + a1[...].astype(F32) + a2[...].astype(F32) + a3[...].astype(F32)
+def near_kernel(a0, a1, a2, a3, near):
+    near[...] = a0[...] + a1[...].astype(F32) + a2[...].astype(F32) + a3[...].astype(F32)
+
+
+def sum_kernel(width, near_ref, b0, b1, b2, b3, out):
+    near = near_ref[...]
     far = b0[...] + b1[...].astype(F32) + b2[...].astype(F32) + b3[...].astype(F32)
     first = lax.axis_index("row") < 2
     low, high = jnp.where(first, near, far), jnp.where(first, far, near)
@@ -342,8 +346,9 @@
 
     own_sums = mixed(q0, g1, g2, g3, c0)
     far_sums = mixed(x0, x123, cx0, cx123)
+    near = call(near_kernel, shape(own_sums[0].shape, F32), [], *own_sums)
     return call(
-        functools.partial(sum_kernel, width), shape(frames.shape, BF16), [], *own_sums, *far_sums
+        functools.partial(sum_kernel, width), shape(frames.shape, BF16), [], near, *far_sums
     )
 
 

time: 53.8 us -> 55 us (1.022)
  waiting for transfers between devices: 10.9 us -> 13.3 us
  starting transfers between devices: 37.6 us -> 36.3 us
    ppermute x21, waiting for transfers between devices: 10.9 us -> 13.3 us  [swapped(): return lax.ppermute(array, axis, [(i, i ^ distance) for i in range(size)])]
    ppermute x21, starting transfers between devices: 36.2 us -> 34.9 us  [swapped(): return lax.ppermute(array, axis, [(i, i ^ distance) for i in range(size)])]
    pallas_call x5 -> x6, Pallas kernels: 3.86 us -> 3.85 us  [call(): pl.pallas_call(kernel, out_shape=outs, in_specs=specs or [VMEM] * len(arg...]
  transfers between devices with their start and end apart: 23 -> 23, of which waited for: 7 -> 6; matrix products, arithmetic and copies ran while one was open for 0% -> 0% of each run, Pallas kernels for 6% -> 6%
where the time goes in v4:
time: 55 us; the launch traced here: 54.8 us
  starting transfers between devices  36.3 us (66%)
  waiting for transfers between devices  13.3 us (24%)
  Pallas kernels  3.85 us (7%)
  local copies, waits for them, and re-layouts  1.06 us (2%)
    ppermute x21, starting transfers between devices, swapped(): return lax.ppermute(array, axis, [(i, i ^ distance) for i in range(size)])  34.9 us
    ppermute x21, waiting for transfers between devices, swapped(): return lax.ppermute(array, axis, [(i, i ^ distance) for i in range(size)])  13.3 us
    pallas_call x6, Pallas kernels, call(): pl.pallas_call(kernel, out_shape=outs, in_specs=specs or [VMEM] * len(arg...  3.85 us
    ppermute x2, starting transfers between devices, across(): return lax.ppermute(array, 'row', pairs + [(j, i) for i, j in pairs])  1.34 us
  transfers between devices with their start and end apart: 23, of which 6 were waited for; matrix products, arithmetic and copies ran while one was open for 0% of the time, Pallas kernels for 6%

profile of v4, /device:TPU:0, one launch (start us, length us, event | category | flops | bytes accessed | tf_op | source)
XLA Modules:
  0.0 54.8 jit_solution(1768498574702413892)
XLA Ops:
  0.0 4.1 %collective-permute-start.1 = (bf16[96,512]{1,0:T(8,128)(2,1)}, bf16[96,512]{1,0:T(8,128)(2,1)S(1)}, u32[]{:S(2)}, u32[]{:S(2)}) collective-permute-start(bf16[96,512]{1,0:T(8,128)(2,1)} %bitcast.18), channel_id=1, source_target_pairs={{0,8},{4,12},{8,0},{12,4},{1,9},{5,13},{9,1},{13,5},{2,10},{6,14},... | collective-permute-start | bytes 294920 | tf_op jit(solution)/shard_map/ppermute | solution.py:112
  4.1 0.1 broadcast_in_dim.2.marks
  4.2 1.0 %copy-done.2 = bf16[3,3,512,32]{2,3,1,0:T(8,128)(2,1)S(1)} copy-done((bf16[3,3,512,32]{2,3,1,0:T(8,128)(2,1)S(1)}, bf16[3,3,512,32]{2,3,1,0:T(8,128)(2,1)}, u32[]{:S(2)}) %copy-start.2) | copy-done | bytes 294936
  5.2 1.6 %collective-permute-start.3 = (bf16[304,128]{1,0:T(8,128)(2,1)S(1)}, bf16[304,128]{1,0:T(8,128)(2,1)S(1)}, u32[]{:S(2)}, u32[]{:S(2)}) collective-permute-start(bf16[304,128]{1,0:T(8,128)(2,1)S(1)} %get-tuple-element.18), channel_id=1, source_target_pairs={{0,4},{4,0},{8,12},{12,8},{1,5},{5,1},{9,13},{13,9},{2,6},{6,2},{1... | collective-permute-start | bytes 233480 | tf_op jit(solution)/shard_map/ppermute | solution.py:112
  6.8 0.7 %collective-permute-start.4 = (bf16[304,128]{1,0:T(8,128)(2,1)S(1)}, bf16[304,128]{1,0:T(8,128)(2,1)S(1)}, u32[]{:S(2)}, u32[]{:S(2)}) collective-permute-start(bf16[304,128]{1,0:T(8,128)(2,1)S(1)} %get-tuple-element.19), channel_id=1, source_target_pairs={{0,8},{4,12},{8,0},{12,4},{1,9},{5,13},{9,1},{13,5},{2,10},{6,14},... | collective-permute-start | bytes 233480 | tf_op jit(solution)/shard_map/ppermute | solution.py:112
  7.5 2.2 %collective-permute-start.5 = (bf16[304,128]{1,0:T(8,128)(2,1)S(1)}, bf16[304,128]{1,0:T(8,128)(2,1)S(1)}, u32[]{:S(2)}, u32[]{:S(2)}) collective-permute-start(bf16[304,128]{1,0:T(8,128)(2,1)S(1)} %get-tuple-element.20), channel_id=1, source_target_pairs={{0,12},{4,8},{8,4},{12,0},{1,13},{5,9},{9,5},{13,1},{2,14},{6,10},... | collective-permute-start | bytes 233480 | tf_op jit(solution)/shard_map/ppermute | solution.py:112
  9.6 0.7 %collective-permute-start = (bf16[96,512]{1,0:T(8,128)(2,1)S(1)}, bf16[96,512]{1,0:T(8,128)(2,1)S(1)}, u32[]{:S(2)}, u32[]{:S(2)}) collective-permute-start(bf16[96,512]{1,0:T(8,128)(2,1)S(1)} %bitcast.19), channel_id=1, source_target_pairs={{0,4},{4,0},{8,12},{12,8},{1,5},{5,1},{9,13},{13,9},{2,6},{6,2},{1... | collective-permute-start | bytes 294920 | tf_op jit(solution)/shard_map/ppermute | solution.py:112
  10.3 0.1 collective-permute-done.3.m1.refs_1_
  10.5 1.5 %collective-permute-start.10 = (bf16[3,3,32,512]{3,2,1,0:T(8,128)(2,1)}, bf16[3,3,32,512]{3,2,1,0:T(8,128)(2,1)S(1)}, u32[]{:S(2)}, u32[]{:S(2)}) collective-permute-start(bf16[3,3,32,512]{3,2,1,0:T(8,128)(2,1)} %bitcast.29), channel_id=1, source_target_pairs={{0,2},{1,3},{2,0},{3,1},{4,6},{5,7},{6,4},{7,5},{8,10},{9,11},{10,... | collective-permute-start | bytes 884744 | tf_op jit(solution)/shard_map/ppermute | solution.py:112
  12.0 3.3 %collective-permute-done.4.m2.refs_2_ = bf16[304,128]{1,0:T(8,128)(2,1)S(1)} collective-permute-done((bf16[304,128]{1,0:T(8,128)(2,1)S(1)}, bf16[304,128]{1,0:T(8,128)(2,1)S(1)}, u32[]{:S(2)}, u32[]{:S(2)}) %collective-permute-start.4) | collective-permute-done | bytes 77856 | tf_op jit(solution)/shard_map/ppermute | solution.py:112
  15.3 1.5 %collective-permute-start.16 = (bf16[304,128]{1,0:T(8,128)(2,1)S(1)}, bf16[304,128]{1,0:T(8,128)(2,1)S(1)}, u32[]{:S(2)}, u32[]{:S(2)}) collective-permute-start(bf16[304,128]{1,0:T(8,128)(2,1)S(1)} %get-tuple-element.17.m0.refs_0_), channel_id=1, source_target_pairs={{0,2},{1,3},{2,0},{3,1},{4,6},{5,7},{6,4},{7,5},{8,10},{9,11},{10,... | collective-permute-start | bytes 233480 | tf_op jit(solution)/shard_map/ppermute | solution.py:112
  16.8 1.5 %collective-permute-start.2 = (bf16[96,512]{1,0:T(8,128)(2,1)S(1)}, bf16[96,512]{1,0:T(8,128)(2,1)S(1)}, u32[]{:S(2)}, u32[]{:S(2)}) collective-permute-start(bf16[96,512]{1,0:T(8,128)(2,1)S(1)} %collective-permute-done.1.f2), channel_id=1, source_target_pairs={{0,4},{4,0},{8,12},{12,8},{1,5},{5,1},{9,13},{13,9},{2,6},{6,2},{1... | collective-permute-start | bytes 294920 | tf_op jit(solution)/shard_map/ppermute | solution.py:112
  18.3 3.4 %collective-permute-done.2.f3 = bf16[96,512]{1,0:T(8,128)(2,1)S(1)} collective-permute-done((bf16[96,512]{1,0:T(8,128)(2,1)S(1)}, bf16[96,512]{1,0:T(8,128)(2,1)S(1)}, u32[]{:S(2)}, u32[]{:S(2)}) %collective-permute-start.2) | collective-permute-done | bytes 98336 | tf_op jit(solution)/shard_map/ppermute | solution.py:112
  21.9 0.7 %collective-permute-start.7 = (bf16[96,512]{1,0:T(8,128)(2,1)S(1)}, bf16[96,512]{1,0:T(8,128)(2,1)S(1)}, u32[]{:S(2)}, u32[]{:S(2)}) collective-permute-start(bf16[96,512]{1,0:T(8,128)(2,1)S(1)} %collective-permute-done.2.f3), channel_id=1, source_target_pairs={{1,2},{2,1},{5,6},{6,5},{9,10},{10,9},{13,14},{14,13},{17,18},{18,... | collective-permute-start | bytes 294920 | tf_op jit(solution)/shard_map/ppermute | solution.py:121
  22.6 3.4 %collective-permute-start.17 = (bf16[3,304,128]{2,1,0:T(8,128)(2,1)S(1)}, bf16[3,304,128]{2,1,0:T(8,128)(2,1)S(1)}, u32[]{:S(2)}, u32[]{:S(2)}) collective-permute-start(bf16[3,304,128]{2,1,0:T(8,128)(2,1)S(1)} %pad_maximum_fusion.3), channel_id=1, source_target_pairs={{0,2},{1,3},{2,0},{3,1},{4,6},{5,7},{6,4},{7,5},{8,10},{9,11},{10,... | collective-permute-start | bytes 700424 | tf_op jit(solution)/shard_map/ppermute | solution.py:112
  26.0 0.7 %collective-permute-start.6 = (bf16[3,96,512]{2,1,0:T(8,128)(2,1)S(1)}, bf16[3,96,512]{2,1,0:T(8,128)(2,1)S(1)}, u32[]{:S(2)}, u32[]{:S(2)}) collective-permute-start(bf16[3,96,512]{2,1,0:T(8,128)(2,1)S(1)} %pad_maximum_fusion.2), channel_id=1, source_target_pairs={{1,2},{2,1},{5,6},{6,5},{9,10},{10,9},{13,14},{14,13},{17,18},{18,... | collective-permute-start | bytes 884744 | tf_op jit(solution)/shard_map/ppermute | solution.py:121
  26.7 4.6 %collective-permute-start.11 = (bf16[3,3,32,512]{3,2,1,0:T(8,128)(2,1)S(1)}, bf16[3,3,32,512]{3,2,1,0:T(8,128)(2,1)S(1)}, u32[]{:S(2)}, u32[]{:S(2)}) collective-permute-start(bf16[3,3,32,512]{3,2,1,0:T(8,128)(2,1)S(1)} %collective-permute-done.10.w2), channel_id=1, source_target_pairs={{0,1},{1,0},{2,3},{3,2},{4,5},{5,4},{6,7},{7,6},{8,9},{9,8},{10,11... | collective-permute-start | bytes 884744 | tf_op jit(solution)/shard_map/ppermute | solution.py:112
  31.4 0.1 collective-permute-start.12
  31.5 1.7 %collective-permute-done.17.refs_1_ = bf16[3,304,128]{2,1,0:T(8,128)(2,1)S(1)} collective-permute-done((bf16[3,304,128]{2,1,0:T(8,128)(2,1)S(1)}, bf16[3,304,128]{2,1,0:T(8,128)(2,1)S(1)}, u32[]{:S(2)}, u32[]{:S(2)}) %collective-permute-start.17) | collective-permute-done | bytes 233504 | tf_op jit(solution)/shard_map/ppermute | solution.py:112
  33.2 4.2 %collective-permute-start.18 = (bf16[304,128]{1,0:T(8,128)(2,1)S(1)}, bf16[304,128]{1,0:T(8,128)(2,1)S(1)}, u32[]{:S(2)}, u32[]{:S(2)}) collective-permute-start(bf16[304,128]{1,0:T(8,128)(2,1)S(1)} %collective-permute-done.16.refs_0_), channel_id=1, source_target_pairs={{0,1},{1,0},{2,3},{3,2},{4,5},{5,4},{6,7},{7,6},{8,9},{9,8},{10,11... | collective-permute-start | bytes 233480 | tf_op jit(solution)/shard_map/ppermute | solution.py:112
  37.4 1.8 %shard_map.56.hid = bf16[2,192,1152]{2,1,0:T(8,128)(2,1)S(1)} custom-call(bf16[96,512]{1,0:T(8,128)(2,1)S(1)} %bitcast.22, bf16[96,512]{1,0:T(8,128)(2,1)S(1)} %collective-permute-done.f1, bf16[96,512]{1,0:T(8,128)(2,1)S(1)} %collective-permute-done.1.f2, bf16[96,512]{1,0:T(8,128)(2,1)S(1)} %collective-permute-done.2.f3, ...), custom_call_target="tpu_custom_call" | custom-call | flops 905969664 | bytes 2672640 | tf_op jit(solution)/shard_map/pallas_call | solution.py:257
  39.3 0.6 %shard_map.57 = (f32[2,48,256]{2,1,0:T(8,128)S(1)}, bf16[2,48,256]{2,1,0:T(8,128)(2,1)S(1)}, bf16[2,48,256]{2,1,0:T(8,128)(2,1)S(1)}, bf16[2,48,256]{2,1,0:T(8,128)(2,1)S(1)}) custom-call(bf16[2,192,1152]{2,1,0:T(8,128)(2,1)S(1)} %shard_map.56.hid, bf16[304,128]{1,0:T(8,128)(2,1)S(1)} %get-tuple-element.17.m0.refs_0_, ...), custom_call_target="tpu_custom_call" | custom-call | flops 226492416 | bytes 1507328 | tf_op jit(solution)/shard_map/pallas_call | solution.py:257
  39.9 1.2 %collective-permute-start.13 = (bf16[2,48,256]{2,1,0:T(8,128)(2,1)S(1)}, bf16[2,48,256]{2,1,0:T(8,128)(2,1)S(1)}, u32[]{:S(2)}, u32[]{:S(2)}) collective-permute-start(bf16[2,48,256]{2,1,0:T(8,128)(2,1)S(1)} %get-tuple-element.22), channel_id=1, source_target_pairs={{0,4},{4,0},{8,12},{12,8},{1,5},{5,1},{9,13},{13,9},{2,6},{6,2},{1... | collective-permute-start | bytes 147464 | tf_op jit(solution)/shard_map/ppermute | solution.py:112
  41.1 0.6 %shard_map.59 = (f32[2,48,256]{2,1,0:T(8,128)S(1)}, bf16[2,48,256]{2,1,0:T(8,128)(2,1)S(1)}, bf16[2,48,256]{2,1,0:T(8,128)(2,1)S(1)}, bf16[2,48,256]{2,1,0:T(8,128)(2,1)S(1)}) custom-call(bf16[2,192,1152]{2,1,0:T(8,128)(2,1)S(1)} %shard_map.56.hid, bf16[304,128]{1,0:T(8,128)(2,1)S(1)} %collective-permute-done.16.refs_0_, ...), custom_call_target="tpu_custom_call" | custom-call | flops 226492416 | bytes 1507328 | tf_op jit(solution)/shard_map/pallas_call | solution.py:257
  41.7 0.9 %collective-permute-start.20 = (bf16[2,48,256]{2,1,0:T(8,128)(2,1)S(1)}, bf16[2,48,256]{2,1,0:T(8,128)(2,1)S(1)}, u32[]{:S(2)}, u32[]{:S(2)}) collective-permute-start(bf16[2,48,256]{2,1,0:T(8,128)(2,1)S(1)} %get-tuple-element.26), channel_id=1, source_target_pairs={{0,4},{4,0},{8,12},{12,8},{1,5},{5,1},{9,13},{13,9},{2,6},{6,2},{1... | collective-permute-start | bytes 147464 | tf_op jit(solution)/shard_map/ppermute | solution.py:112
  42.6 2.9 %collective-permute-start.14 = (bf16[2,48,256]{2,1,0:T(8,128)(2,1)S(1)}, bf16[2,48,256]{2,1,0:T(8,128)(2,1)S(1)}, u32[]{:S(2)}, u32[]{:S(2)}) collective-permute-start(bf16[2,48,256]{2,1,0:T(8,128)(2,1)S(1)} %get-tuple-element.23), channel_id=1, source_target_pairs={{0,8},{4,12},{8,0},{12,4},{1,9},{5,13},{9,1},{13,5},{2,10},{6,14},... | collective-permute-start | bytes 147464 | tf_op jit(solution)/shard_map/ppermute | solution.py:112
  45.5 0.6 %collective-permute-start.15 = (bf16[2,48,256]{2,1,0:T(8,128)(2,1)S(1)}, bf16[2,48,256]{2,1,0:T(8,128)(2,1)S(1)}, u32[]{:S(2)}, u32[]{:S(2)}) collective-permute-start(bf16[2,48,256]{2,1,0:T(8,128)(2,1)S(1)} %get-tuple-element.24), channel_id=1, source_target_pairs={{0,12},{4,8},{8,4},{12,0},{1,13},{5,9},{9,5},{13,1},{2,14},{6,10},... | collective-permute-start | bytes 147464 | tf_op jit(solution)/shard_map/ppermute | solution.py:112
  46.1 1.0 %collective-permute-start.21 = (bf16[2,48,256]{2,1,0:T(8,128)(2,1)S(1)}, bf16[2,48,256]{2,1,0:T(8,128)(2,1)S(1)}, u32[]{:S(2)}, u32[]{:S(2)}) collective-permute-start(bf16[2,48,256]{2,1,0:T(8,128)(2,1)S(1)} %get-tuple-element.27), channel_id=1, source_target_pairs={{0,8},{4,12},{8,0},{12,4},{1,9},{5,13},{9,1},{13,5},{2,10},{6,14},... | collective-permute-start | bytes 147464 | tf_op jit(solution)/shard_map/ppermute | solution.py:112
  47.2 2.2 %collective-permute-start.22 = (bf16[2,48,256]{2,1,0:T(8,128)(2,1)S(1)}, bf16[2,48,256]{2,1,0:T(8,128)(2,1)S(1)}, u32[]{:S(2)}, u32[]{:S(2)}) collective-permute-start(bf16[2,48,256]{2,1,0:T(8,128)(2,1)S(1)} %get-tuple-element.28), channel_id=1, source_target_pairs={{0,12},{4,8},{8,4},{12,0},{1,13},{5,9},{9,5},{13,1},{2,14},{6,10},... | collective-permute-start | bytes 147464 | tf_op jit(solution)/shard_map/ppermute | solution.py:112
  49.3 2.1 %collective-permute-done.15.a3 = bf16[2,48,256]{2,1,0:T(8,128)(2,1)S(1)} collective-permute-done((bf16[2,48,256]{2,1,0:T(8,128)(2,1)S(1)}, bf16[2,48,256]{2,1,0:T(8,128)(2,1)S(1)}, u32[]{:S(2)}, u32[]{:S(2)}) %collective-permute-start.15) | collective-permute-done | bytes 49184 | tf_op jit(solution)/shard_map/ppermute | solution.py:112
  51.4 2.6 %collective-permute-done.21.b2 = bf16[2,48,256]{2,1,0:T(8,128)(2,1)S(1)} collective-permute-done((bf16[2,48,256]{2,1,0:T(8,128)(2,1)S(1)}, bf16[2,48,256]{2,1,0:T(8,128)(2,1)S(1)}, u32[]{:S(2)}, u32[]{:S(2)}) %collective-permute-start.21) | collective-permute-done | bytes 49184 | tf_op jit(solution)/shard_map/ppermute | solution.py:112
  54.0 0.8 %shard_map.60 = bf16[2,2,24,512]{3,2,1,0:T(8,128)(2,1)} custom-call(f32[2,48,256]{2,1,0:T(8,128)S(1)} %shard_map.58.near_ref, f32[2,48,256]{2,1,0:T(8,128)S(1)} %get-tuple-element.25.b0, bf16[2,48,256]{2,1,0:T(8,128)(2,1)S(1)} %collective-permute-done.20.b1, bf16[2,48,256]{2,1,0:T(8,128)(2,1)S(1)} %collective-permute-done.21.b2, ...), custom_call_target="tpu_custom_call" | custom-call | bytes 344064 | tf_op jit(solution)/shard_map/pallas_call | solution.py:257
  (37 shorter events, 0.4 us)
Async XLA Ops:
  0.0 4.1 %copy-start.4 = (s32[2]{0:T(128)S(1)}, s32[2]{0:T(128)}, u32[]{:S(2)}) copy-start(s32[2]{0:T(128)} %param.9) | copy-start | bytes 28
  0.0 16.8 %collective-permute-start.1 = (bf16[96,512]{1,0:T(8,128)(2,1)}, bf16[96,512]{1,0:T(8,128)(2,1)S(1)}, u32[]{:S(2)}, u32[]{:S(2)}) collective-permute-start(bf16[96,512]{1,0:T(8,128)(2,1)} %bitcast.18), channel_id=1, source_target_pairs={{0,8},{4,12},{8,0},{12,4},{1,9},{5,13},{9,1},{13,5},{2,10},{6,14},... | collective-permute-start | bytes 294920 | tf_op jit(solution)/shard_map/ppermute | solution.py:112
  4.2 1.0 %copy-start.2 = (bf16[3,3,512,32]{2,3,1,0:T(8,128)(2,1)S(1)}, bf16[3,3,512,32]{2,3,1,0:T(8,128)(2,1)}, u32[]{:S(2)}) copy-start(bf16[3,3,512,32]{2,3,1,0:T(8,128)(2,1)} %param.7) | copy-start | bytes 884740
  5.1 4.5 %copy-start = (bf16[2,2,24,512]{3,2,1,0:T(8,128)(2,1)S(1)}, bf16[2,2,24,512]{3,2,1,0:T(8,128)(2,1)}, u32[]{:S(2)}) copy-start(bf16[2,2,24,512]{3,2,1,0:T(8,128)(2,1)} %param.5) | copy-start | bytes 294916
  5.2 5.3 %collective-permute-start.3 = (bf16[304,128]{1,0:T(8,128)(2,1)S(1)}, bf16[304,128]{1,0:T(8,128)(2,1)S(1)}, u32[]{:S(2)}, u32[]{:S(2)}) collective-permute-start(bf16[304,128]{1,0:T(8,128)(2,1)S(1)} %get-tuple-element.18), channel_id=1, source_target_pairs={{0,4},{4,0},{8,12},{12,8},{1,5},{5,1},{9,13},{13,9},{2,6},{6,2},{1... | collective-permute-start | bytes 233480 | tf_op jit(solution)/shard_map/ppermute | solution.py:112
  6.8 8.5 %collective-permute-start.4 = (bf16[304,128]{1,0:T(8,128)(2,1)S(1)}, bf16[304,128]{1,0:T(8,128)(2,1)S(1)}, u32[]{:S(2)}, u32[]{:S(2)}) collective-permute-start(bf16[304,128]{1,0:T(8,128)(2,1)S(1)} %get-tuple-element.19), channel_id=1, source_target_pairs={{0,8},{4,12},{8,0},{12,4},{1,9},{5,13},{9,1},{13,5},{2,10},{6,14},... | collective-permute-start | bytes 233480 | tf_op jit(solution)/shard_map/ppermute | solution.py:112
  7.5 7.8 %collective-permute-start.5 = (bf16[304,128]{1,0:T(8,128)(2,1)S(1)}, bf16[304,128]{1,0:T(8,128)(2,1)S(1)}, u32[]{:S(2)}, u32[]{:S(2)}) collective-permute-start(bf16[304,128]{1,0:T(8,128)(2,1)S(1)} %get-tuple-element.20), channel_id=1, source_target_pairs={{0,12},{4,8},{8,4},{12,0},{1,13},{5,9},{9,5},{13,1},{2,14},{6,10},... | collective-permute-start | bytes 233480 | tf_op jit(solution)/shard_map/ppermute | solution.py:112
  9.6 8.7 %collective-permute-start = (bf16[96,512]{1,0:T(8,128)(2,1)S(1)}, bf16[96,512]{1,0:T(8,128)(2,1)S(1)}, u32[]{:S(2)}, u32[]{:S(2)}) collective-permute-start(bf16[96,512]{1,0:T(8,128)(2,1)S(1)} %bitcast.19), channel_id=1, source_target_pairs={{0,4},{4,0},{8,12},{12,8},{1,5},{5,1},{9,13},{13,9},{2,6},{6,2},{1... | collective-permute-start | bytes 294920 | tf_op jit(solution)/shard_map/ppermute | solution.py:112
  10.5 16.2 %collective-permute-start.10 = (bf16[3,3,32,512]{3,2,1,0:T(8,128)(2,1)}, bf16[3,3,32,512]{3,2,1,0:T(8,128)(2,1)S(1)}, u32[]{:S(2)}, u32[]{:S(2)}) collective-permute-start(bf16[3,3,32,512]{3,2,1,0:T(8,128)(2,1)} %bitcast.29), channel_id=1, source_target_pairs={{0,2},{1,3},{2,0},{3,1},{4,6},{5,7},{6,4},{7,5},{8,10},{9,11},{10,... | collective-permute-start | bytes 884744 | tf_op jit(solution)/shard_map/ppermute | solution.py:112
  15.3 16.1 %collective-permute-start.9 = (bf16[3,3,32,512]{3,2,1,0:T(8,128)(2,1)}, bf16[3,3,32,512]{3,2,1,0:T(8,128)(2,1)S(1)}, u32[]{:S(2)}, u32[]{:S(2)}) collective-permute-start(bf16[3,3,32,512]{3,2,1,0:T(8,128)(2,1)} %bitcast.30), channel_id=1, source_target_pairs={{0,1},{1,0},{2,3},{3,2},{4,5},{5,4},{6,7},{7,6},{8,9},{9,8},{10,11... | collective-permute-start | bytes 884744 | tf_op jit(solution)/shard_map/ppermute | solution.py:112
  15.3 7.3 %collective-permute-start.16 = (bf16[304,128]{1,0:T(8,128)(2,1)S(1)}, bf16[304,128]{1,0:T(8,128)(2,1)S(1)}, u32[]{:S(2)}, u32[]{:S(2)}) collective-permute-start(bf16[304,128]{1,0:T(8,128)(2,1)S(1)} %get-tuple-element.17.m0.refs_0_), channel_id=1, source_target_pairs={{0,2},{1,3},{2,0},{3,1},{4,6},{5,7},{6,4},{7,5},{8,10},{9,11},{10,... | collective-permute-start | bytes 233480 | tf_op jit(solution)/shard_map/ppermute | solution.py:112
  16.8 4.9 %collective-permute-start.2 = (bf16[96,512]{1,0:T(8,128)(2,1)S(1)}, bf16[96,512]{1,0:T(8,128)(2,1)S(1)}, u32[]{:S(2)}, u32[]{:S(2)}) collective-permute-start(bf16[96,512]{1,0:T(8,128)(2,1)S(1)} %collective-permute-done.1.f2), channel_id=1, source_target_pairs={{0,4},{4,0},{8,12},{12,8},{1,5},{5,1},{9,13},{13,9},{2,6},{6,2},{1... | collective-permute-start | bytes 294920 | tf_op jit(solution)/shard_map/ppermute | solution.py:112
  21.8 15.6 %collective-permute-start.8 = (bf16[4,96,512]{2,1,0:T(8,128)(2,1)S(1)}, bf16[4,96,512]{2,1,0:T(8,128)(2,1)S(1)}, u32[]{:S(2)}, u32[]{:S(2)}) collective-permute-start(bf16[4,96,512]{2,1,0:T(8,128)(2,1)S(1)} %pad_maximum_fusion), channel_id=1, source_target_pairs={{0,1},{1,0},{2,3},{3,2},{4,5},{5,4},{6,7},{7,6},{8,9},{9,8},{10,11... | collective-permute-start | bytes 1179656 | tf_op jit(solution)/shard_map/ppermute | solution.py:112
  21.9 4.2 %collective-permute-start.7 = (bf16[96,512]{1,0:T(8,128)(2,1)S(1)}, bf16[96,512]{1,0:T(8,128)(2,1)S(1)}, u32[]{:S(2)}, u32[]{:S(2)}) collective-permute-start(bf16[96,512]{1,0:T(8,128)(2,1)S(1)} %collective-permute-done.2.f3), channel_id=1, source_target_pairs={{1,2},{2,1},{5,6},{6,5},{9,10},{10,9},{13,14},{14,13},{17,18},{18,... | collective-permute-start | bytes 294920 | tf_op jit(solution)/shard_map/ppermute | solution.py:121
  22.6 10.6 %collective-permute-start.17 = (bf16[3,304,128]{2,1,0:T(8,128)(2,1)S(1)}, bf16[3,304,128]{2,1,0:T(8,128)(2,1)S(1)}, u32[]{:S(2)}, u32[]{:S(2)}) collective-permute-start(bf16[3,304,128]{2,1,0:T(8,128)(2,1)S(1)} %pad_maximum_fusion.3), channel_id=1, source_target_pairs={{0,2},{1,3},{2,0},{3,1},{4,6},{5,7},{6,4},{7,5},{8,10},{9,11},{10,... | collective-permute-start | bytes 700424 | tf_op jit(solution)/shard_map/ppermute | solution.py:112
  26.0 7.2 %collective-permute-start.6 = (bf16[3,96,512]{2,1,0:T(8,128)(2,1)S(1)}, bf16[3,96,512]{2,1,0:T(8,128)(2,1)S(1)}, u32[]{:S(2)}, u32[]{:S(2)}) collective-permute-start(bf16[3,96,512]{2,1,0:T(8,128)(2,1)S(1)} %pad_maximum_fusion.2), channel_id=1, source_target_pairs={{1,2},{2,1},{5,6},{6,5},{9,10},{10,9},{13,14},{14,13},{17,18},{18,... | collective-permute-start | bytes 884744 | tf_op jit(solution)/shard_map/ppermute | solution.py:121
  26.7 10.7 %collective-permute-start.11 = (bf16[3,3,32,512]{3,2,1,0:T(8,128)(2,1)S(1)}, bf16[3,3,32,512]{3,2,1,0:T(8,128)(2,1)S(1)}, u32[]{:S(2)}, u32[]{:S(2)}) collective-permute-start(bf16[3,3,32,512]{3,2,1,0:T(8,128)(2,1)S(1)} %collective-permute-done.10.w2), channel_id=1, source_target_pairs={{0,1},{1,0},{2,3},{3,2},{4,5},{5,4},{6,7},{7,6},{8,9},{9,8},{10,11... | collective-permute-start | bytes 884744 | tf_op jit(solution)/shard_map/ppermute | solution.py:112
  31.3 6.0 %copy-start.1 = (bf16[3,3,512,32]{2,3,1,0:T(8,128)(2,1)S(1)}, bf16[3,3,512,32]{2,3,1,0:T(8,128)(2,1)}, u32[]{:S(2)}) copy-start(bf16[3,3,512,32]{2,3,1,0:T(8,128)(2,1)} %param.6) | copy-start | bytes 884740
  31.3 6.0 %copy-start.3 = (s32[512]{0:T(512)S(1)}, s32[512]{0:T(512)}, u32[]{:S(2)}) copy-start(s32[512]{0:T(512)} %param.8) | copy-start | bytes 6148
  31.4 7.9 %collective-permute-start.12 = (bf16[4,304,128]{2,1,0:T(8,128)(2,1)S(1)}, bf16[4,304,128]{2,1,0:T(8,128)(2,1)S(1)}, u32[]{:S(2)}, u32[]{:S(2)}) collective-permute-start(bf16[4,304,128]{2,1,0:T(8,128)(2,1)S(1)} %pad_maximum_fusion.1), channel_id=1, source_target_pairs={{0,1},{1,0},{2,3},{3,2},{4,5},{5,4},{6,7},{7,6},{8,9},{9,8},{10,11... | collective-permute-start | bytes 933896 | tf_op jit(solution)/shard_map/ppermute | solution.py:112
  33.2 7.9 %collective-permute-start.19 = (bf16[3,304,128]{2,1,0:T(8,128)(2,1)S(1)}, bf16[3,304,128]{2,1,0:T(8,128)(2,1)S(1)}, u32[]{:S(2)}, u32[]{:S(2)}) collective-permute-start(bf16[3,304,128]{2,1,0:T(8,128)(2,1)S(1)} %collective-permute-done.17.refs_1_), channel_id=1, source_target_pairs={{0,1},{1,0},{2,3},{3,2},{4,5},{5,4},{6,7},{7,6},{8,9},{9,8},{10,11... | collective-permute-start | bytes 700424 | tf_op jit(solution)/shard_map/ppermute | solution.py:112
  33.2 7.8 %collective-permute-start.18 = (bf16[304,128]{1,0:T(8,128)(2,1)S(1)}, bf16[304,128]{1,0:T(8,128)(2,1)S(1)}, u32[]{:S(2)}, u32[]{:S(2)}) collective-permute-start(bf16[304,128]{1,0:T(8,128)(2,1)S(1)} %collective-permute-done.16.refs_0_), channel_id=1, source_target_pairs={{0,1},{1,0},{2,3},{3,2},{4,5},{5,4},{6,7},{7,6},{8,9},{9,8},{10,11... | collective-permute-start | bytes 233480 | tf_op jit(solution)/shard_map/ppermute | solution.py:112
  39.9 7.3 %collective-permute-start.13 = (bf16[2,48,256]{2,1,0:T(8,128)(2,1)S(1)}, bf16[2,48,256]{2,1,0:T(8,128)(2,1)S(1)}, u32[]{:S(2)}, u32[]{:S(2)}) collective-permute-start(bf16[2,48,256]{2,1,0:T(8,128)(2,1)S(1)} %get-tuple-element.22), channel_id=1, source_target_pairs={{0,4},{4,0},{8,12},{12,8},{1,5},{5,1},{9,13},{13,9},{2,6},{6,2},{1... | collective-permute-start | bytes 147464 | tf_op jit(solution)/shard_map/ppermute | solution.py:112
  41.7 9.7 %collective-permute-start.20 = (bf16[2,48,256]{2,1,0:T(8,128)(2,1)S(1)}, bf16[2,48,256]{2,1,0:T(8,128)(2,1)S(1)}, u32[]{:S(2)}, u32[]{:S(2)}) collective-permute-start(bf16[2,48,256]{2,1,0:T(8,128)(2,1)S(1)} %get-tuple-element.26), channel_id=1, source_target_pairs={{0,4},{4,0},{8,12},{12,8},{1,5},{5,1},{9,13},{13,9},{2,6},{6,2},{1... | collective-permute-start | bytes 147464 | tf_op jit(solution)/shard_map/ppermute | solution.py:112
  42.6 6.7 %collective-permute-start.14 = (bf16[2,48,256]{2,1,0:T(8,128)(2,1)S(1)}, bf16[2,48,256]{2,1,0:T(8,128)(2,1)S(1)}, u32[]{:S(2)}, u32[]{:S(2)}) collective-permute-start(bf16[2,48,256]{2,1,0:T(8,128)(2,1)S(1)} %get-tuple-element.23), channel_id=1, source_target_pairs={{0,8},{4,12},{8,0},{12,4},{1,9},{5,13},{9,1},{13,5},{2,10},{6,14},... | collective-permute-start | bytes 147464 | tf_op jit(solution)/shard_map/ppermute | solution.py:112
  45.5 5.9 %collective-permute-start.15 = (bf16[2,48,256]{2,1,0:T(8,128)(2,1)S(1)}, bf16[2,48,256]{2,1,0:T(8,128)(2,1)S(1)}, u32[]{:S(2)}, u32[]{:S(2)}) collective-permute-start(bf16[2,48,256]{2,1,0:T(8,128)(2,1)S(1)} %get-tuple-element.24), channel_id=1, source_target_pairs={{0,12},{4,8},{8,4},{12,0},{1,13},{5,9},{9,5},{13,1},{2,14},{6,10},... | collective-permute-start | bytes 147464 | tf_op jit(solution)/shard_map/ppermute | solution.py:112
  46.1 7.9 %collective-permute-start.21 = (bf16[2,48,256]{2,1,0:T(8,128)(2,1)S(1)}, bf16[2,48,256]{2,1,0:T(8,128)(2,1)S(1)}, u32[]{:S(2)}, u32[]{:S(2)}) collective-permute-start(bf16[2,48,256]{2,1,0:T(8,128)(2,1)S(1)} %get-tuple-element.27), channel_id=1, source_target_pairs={{0,8},{4,12},{8,0},{12,4},{1,9},{5,13},{9,1},{13,5},{2,10},{6,14},... | collective-permute-start | bytes 147464 | tf_op jit(solution)/shard_map/ppermute | solution.py:112
  47.2 6.9 %collective-permute-start.22 = (bf16[2,48,256]{2,1,0:T(8,128)(2,1)S(1)}, bf16[2,48,256]{2,1,0:T(8,128)(2,1)S(1)}, u32[]{:S(2)}, u32[]{:S(2)}) collective-permute-start(bf16[2,48,256]{2,1,0:T(8,128)(2,1)S(1)} %get-tuple-element.28), channel_id=1, source_target_pairs={{0,12},{4,8},{8,4},{12,0},{1,13},{5,9},{9,5},{13,1},{2,14},{6,10},... | collective-permute-start | bytes 147464 | tf_op jit(solution)/shard_map/ppermute | solution.py:112
